TPU v7x, 32 devices: a whole 2x2x4 slice. The times are simulated.
32 devices in a mesh: batch: 8 (over y, x, core), mem: 4 (over z).
Axes of the slice: x: 2, y: 2, z: 4, core: 2. Of those that a mesh axis runs over, the one named last changes fastest.
Arguments:
- content_in: bfloat16 [32, 512, 768], P(('batch', 'mem')), may hold values from -6 to 6
- query_in: bfloat16 [32, 512, 768], P(('batch', 'mem')), may hold values from -6 to 6
- memory: bfloat16 [32, 384, 768], P('batch', 'mem'), may hold values from -6 to 6
- sequence_lengths: int32 [32], P(('batch', 'mem')), may hold values from 1 to 512, 12288 in all
- order_rank: int32 [32, 512], P(('batch', 'mem')), may hold values from 0 to 511, each once within a row
- segment_ids: int32 [32, 512], P(('batch', 'mem')), may hold values from 0 to 1
- w_query: bfloat16 [768, 768], replicated, may hold values from -0.21875 to 0.21875
- w_key: bfloat16 [768, 768], replicated, may hold values from -0.21875 to 0.21875
- w_value: bfloat16 [768, 768], replicated, may hold values from -0.21875 to 0.21875
- w_out: bfloat16 [768, 768], replicated, may hold values from -1.75 to 1.75
- w_rel: bfloat16 [768, 768], replicated, may hold values from -0.21875 to 0.21875
- bias_content: bfloat16 [768], replicated, may hold values from -3 to 3
- bias_position: bfloat16 [768], replicated, may hold values from -3 to 3
- bias_segment: bfloat16 [768], replicated, may hold values from -3 to 3
- segment_embed: bfloat16 [2, 768], replicated, may hold values from -5 to 5
- gain_one: bfloat16 [768], replicated, may hold values from 0.5 to 1.5
- shift_one: bfloat16 [768], replicated, may hold values from -2 to 2
- w_inner: bfloat16 [768, 3072], replicated, may hold values from -0.21875 to 0.21875
- bias_inner: bfloat16 [3072], replicated, may hold values from -2 to 2
- w_outer: bfloat16 [3072, 768], replicated, may hold values from -0.109375 to 0.109375
- bias_outer: bfloat16 [768], replicated, may hold values from -2 to 2
- gain_two: bfloat16 [768], replicated, may hold values from 0.5 to 1.5
- shift_two: bfloat16 [768], replicated, may hold values from -2 to 2
- content_cotangent: bfloat16 [32, 512, 768], P(('batch', 'mem')), may hold values from -6 to 6
- query_cotangent: bfloat16 [32, 512, 768], P(('batch', 'mem')), may hold values from -6 to 6
Outputs:
- content_out: bfloat16 [32, 512, 768], P(('batch', 'mem'))
- query_out: bfloat16 [32, 512, 768], P(('batch', 'mem'))
- grad_content_in: bfloat16 [32, 512, 768], P(('batch', 'mem'))
- grad_query_in: bfloat16 [32, 512, 768], P(('batch', 'mem'))
- grad_w_query: float32 [768, 768], replicated
- grad_w_key: float32 [768, 768], replicated
- grad_w_value: float32 [768, 768], replicated
- grad_w_out: float32 [768, 768], replicated
- grad_w_rel: float32 [768, 768], replicated
- grad_bias_content: float32 [768], replicated
- grad_bias_position: float32 [768], replicated
- grad_bias_segment: float32 [768], replicated
- grad_segment_embed: float32 [2, 768], replicated
- grad_gain_one: float32 [768], replicated
- grad_shift_one: float32 [768], replicated
- grad_w_inner: float32 [768, 3072], replicated
- grad_bias_inner: float32 [3072], replicated
- grad_w_outer: float32 [3072, 768], replicated
- grad_bias_outer: float32 [768], replicated
- grad_gain_two: float32 [768], replicated
- grad_shift_two: float32 [768], replicated
Inputs may be any that keep to these rules, and one draw needn't show every extreme that they name: `sequence_lengths`: the number of live current tokens of each sequence; over all sequences they sum to 12288, and one sequence has all 512. `order_rank`: each row is a permutation of 0 to 511.
All inputs are finite; a program needn't handle non-finite values. No bound on the sum of `sequence_lengths` on one device may be relied on, other than what follows from the above.
Results may differ from a plain program's by a relative error of at most 0.03.
Values may be sent and summed in bfloat16 or wider, within the bound.
No kernel may reach another device: no remote copies, remote signals or barrier semaphores. Data moves between devices by JAX's collectives and lax.ppermute only.
A program may use at most 448 MiB of HBM per device.

v0:
```python
import jax
import jax.numpy as jnp
from jax import lax
from jax.sharding import PartitionSpec as P

D = 768
HEADS = 12
HEAD = 64
SEG = 512
MEM = 384


norm_epsilon = 1e-06
highest = lax.Precision.HIGHEST


def layer_norm(tensor, norm_gain, norm_shift):
    centred = tensor - jnp.mean(tensor, axis=-1, keepdims=True)
    variance = jnp.mean(centred * centred, axis=-1, keepdims=True)
    return centred * lax.rsqrt(variance + norm_epsilon) * norm_gain + norm_shift


def sinusoid(memory_count, segment_count, feature_count):
    distance = (
        memory_count
        + segment_count
        - 1
        - jnp.arange(memory_count + 2 * segment_count - 1, dtype=jnp.int32)
    ).astype(jnp.float32)
    frequency = 1.0 / 10000.0 ** (
        jnp.arange(0, feature_count, 2, dtype=jnp.int32).astype(jnp.float32) / feature_count
    )
    phases = distance[:, None] * frequency[None, :]
    return jnp.concatenate([jnp.sin(phases), jnp.cos(phases)], axis=1)


def skew_grid(score_grid):
    head_count, row_count, column_count = score_grid.shape
    kept_columns = MEM + SEG
    flattened = score_grid.reshape(head_count, row_count * column_count)[
        :, row_count - 1 : row_count - 1 + row_count * (column_count - 1)
    ]
    return flattened.reshape(head_count, row_count, column_count - 1)[:, :, :kept_columns]


def gelu_exact(tensor):
    return jax.nn.gelu(tensor, approximate=False)


def matmul(left, right):
    return jnp.dot(left, right, preferred_element_type=jnp.float32)


def heads_first(tensor):
    return tensor.reshape(tensor.shape[0], HEADS, HEAD).transpose(1, 0, 2)


def heads_joined(tensor):
    return tensor.transpose(1, 0, 2).reshape(tensor.shape[1], D)


def shards(
    content_in,
    query_in,
    memory,
    sequence_lengths,
    order_rank,
    segment_ids,
    w_query,
    w_key,
    w_value,
    w_out,
    w_rel,
    bias_content,
    bias_position,
    bias_segment,
    segment_embed,
    gain_one,
    shift_one,
    w_inner,
    bias_inner,
    w_outer,
    bias_outer,
    gain_two,
    shift_two,
    content_cotangent,
    query_cotangent,
):
    key_count = MEM + SEG
    relative_count = MEM + 2 * SEG - 1
    padded_count = relative_count + 2
    scale_factor = HEAD ** (-0.5)
    position_low = sinusoid(MEM, SEG, D).astype(jnp.bfloat16)
    relative_rows = matmul(position_low, w_rel).astype(jnp.bfloat16)
    relative_padded = jnp.concatenate([relative_rows, jnp.zeros((2, D), jnp.bfloat16)], axis=0)
    relative_heads = heads_first(relative_padded)
    segment_table = segment_embed.astype(jnp.float32).reshape(2, HEADS, HEAD)
    content_offset = bias_content.astype(jnp.float32)
    position_offset = bias_position.astype(jnp.float32)
    segment_offset = bias_segment.astype(jnp.float32)
    inner_offset = bias_inner.astype(jnp.float32)
    outer_offset = bias_outer.astype(jnp.float32)
    gain_first = gain_one.astype(jnp.float32)
    shift_first = shift_one.astype(jnp.float32)
    gain_second = gain_two.astype(jnp.float32)
    shift_second = shift_two.astype(jnp.float32)
    shift_zero, shift_back = jax.vjp(skew_grid, jnp.zeros((HEADS, SEG, padded_count), jnp.float32))
    memory_flat = memory.reshape(-1, D)
    memory_key_part = matmul(memory_flat, w_key).astype(jnp.bfloat16).reshape(memory.shape)
    memory_value_part = matmul(memory_flat, w_value).astype(jnp.bfloat16).reshape(memory.shape)
    memory_side = (
        lax.all_to_all(memory_key_part, "mem", split_axis=0, concat_axis=1, tiled=True),
        lax.all_to_all(memory_value_part, "mem", split_axis=0, concat_axis=1, tiled=True),
    )

    def one_sequence(totals, packed):
        (
            content,
            query_rows,
            memory_part,
            length,
            order_row,
            segment,
            content_grad_out,
            query_grad_out,
        ) = packed
        keys_flat = jnp.concatenate(
            [memory_part[0], matmul(content, w_key).astype(jnp.bfloat16)], axis=0
        )
        values_flat = jnp.concatenate(
            [memory_part[1], matmul(content, w_value).astype(jnp.bfloat16)], axis=0
        )
        key_heads = heads_first(keys_flat)
        value_heads = heads_first(values_flat)
        key_place = jnp.arange(key_count, dtype=jnp.int32) - MEM
        key_rank = jnp.concatenate([jnp.full((MEM,), -1, jnp.int32), order_row])
        key_segment = jnp.concatenate([jnp.zeros((MEM,), jnp.int32), segment])
        key_live = key_place < length
        differ = segment[:, None] != key_segment[None, :]
        content_allowed = key_live[None, :] & (key_rank[None, :] <= order_row[:, None])
        query_allowed = key_live[None, :] & (key_rank[None, :] < order_row[:, None])

        def scores(query_content, query_position, query_segment, allowed):
            content_score = jnp.einsum(
                "hid,hjd->hij", query_content, key_heads, preferred_element_type=jnp.float32
            )
            position_grid = jnp.einsum(
                "hid,hud->hiu", query_position, relative_heads, preferred_element_type=jnp.float32
            )
            segment_terms = jnp.einsum(
                "hid,chd->hic", query_segment.astype(jnp.float32), segment_table, precision=highest
            )
            segment_score = jnp.where(
                differ[None], segment_terms[:, :, 1:2], segment_terms[:, :, 0:1]
            )
            score_sum = content_score + skew_grid(position_grid) + segment_score
            return jnp.where(allowed[None], score_sum * scale_factor, -1e30)

        def stream(inputs, allowed, cotangent):
            projected = matmul(inputs, w_query)
            query_content = heads_first((projected + content_offset).astype(jnp.bfloat16))
            query_position = heads_first((projected + position_offset).astype(jnp.bfloat16))
            query_segment = heads_first((projected + segment_offset).astype(jnp.bfloat16))
            logits = scores(query_content, query_position, query_segment, allowed)
            row_top = jnp.max(logits, axis=-1, keepdims=True)
            log_norm = row_top + jnp.log(jnp.sum(jnp.exp(logits - row_top), axis=-1, keepdims=True))
            softmax_out = jnp.exp(logits - log_norm)
            mixture_heads = jnp.einsum(
                "hij,hjd->hid",
                softmax_out.astype(jnp.bfloat16),
                value_heads,
                preferred_element_type=jnp.float32,
            )
            mixture = heads_joined(mixture_heads).astype(jnp.bfloat16)
            attended = matmul(mixture, w_out)
            normed_one, norm_back_one = jax.vjp(
                layer_norm, inputs.astype(jnp.float32) + attended, gain_first, shift_first
            )
            normed_low = normed_one.astype(jnp.bfloat16)
            inner_pre = matmul(normed_low, w_inner) + inner_offset
            activated, gelu_back = jax.vjp(gelu_exact, inner_pre)
            active_low = activated.astype(jnp.bfloat16)
            outer_sum = matmul(active_low, w_outer) + outer_offset
            final_out, norm_back_two = jax.vjp(
                layer_norm, normed_one + outer_sum, gain_second, shift_second
            )
            grad_final_sum, grad_second_gain, grad_second_shift = norm_back_two(
                cotangent.astype(jnp.float32)
            )
            grad_outer_low = grad_final_sum.astype(jnp.bfloat16)
            grad_outer_bias = jnp.sum(grad_outer_low.astype(jnp.float32), axis=0)
            grad_outer_w = matmul(active_low.T, grad_outer_low)
            (grad_inner_pre,) = gelu_back(matmul(grad_outer_low, w_outer.T))
            grad_inner_low = grad_inner_pre.astype(jnp.bfloat16)
            grad_inner_bias = jnp.sum(grad_inner_low.astype(jnp.float32), axis=0)
            grad_inner_w = matmul(normed_low.T, grad_inner_low)
            grad_residual, grad_first_gain, grad_first_shift = norm_back_one(
                grad_final_sum + matmul(grad_inner_low, w_inner.T)
            )
            grad_attended = grad_residual.astype(jnp.bfloat16)
            grad_out_w = matmul(mixture.T, grad_attended)
            grad_mixture = heads_first(matmul(grad_attended, w_out.T).astype(jnp.bfloat16))
            logits_again = scores(query_content, query_position, query_segment, allowed)
            soft_again = jnp.exp(logits_again - log_norm)
            grad_values = jnp.einsum(
                "hij,hid->hjd",
                soft_again.astype(jnp.bfloat16),
                grad_mixture,
                preferred_element_type=jnp.float32,
            )
            grad_soft = jnp.einsum(
                "hid,hjd->hij", grad_mixture, value_heads, preferred_element_type=jnp.float32
            )
            grad_logits = soft_again * (
                grad_soft - jnp.sum(soft_again * grad_soft, axis=-1, keepdims=True)
            )
            grad_total = (grad_logits * scale_factor).astype(jnp.bfloat16)
            grad_query_content = heads_joined(
                jnp.einsum(
                    "hij,hjd->hid", grad_total, key_heads, preferred_element_type=jnp.float32
                )
            ).astype(jnp.bfloat16)
            grad_keys = jnp.einsum(
                "hij,hid->hjd", grad_total, query_content, preferred_element_type=jnp.float32
            )
            total_wide = grad_total.astype(jnp.float32)
            (grad_grid,) = shift_back(total_wide)
            grad_grid_low = grad_grid.astype(jnp.bfloat16)
            grad_query_position = heads_joined(
                jnp.einsum(
                    "hiu,hud->hid",
                    grad_grid_low,
                    relative_heads,
                    preferred_element_type=jnp.float32,
                )
            ).astype(jnp.bfloat16)
            grad_relative = jnp.einsum(
                "hiu,hid->hud", grad_grid_low, query_position, preferred_element_type=jnp.float32
            )
            same_part = jnp.sum(jnp.where(differ[None], 0.0, total_wide), axis=-1)
            differ_part = jnp.sum(jnp.where(differ[None], total_wide, 0.0), axis=-1)
            grad_terms = jnp.stack([same_part, differ_part], axis=-1)
            grad_query_segment = heads_joined(
                jnp.einsum("hic,chd->hid", grad_terms, segment_table, precision=highest)
            ).astype(jnp.bfloat16)
            grad_segment_table = jnp.einsum(
                "hic,hid->chd", grad_terms, query_segment.astype(jnp.float32), precision=highest
            ).reshape(2, D)
            content_wide = grad_query_content.astype(jnp.float32)
            position_wide = grad_query_position.astype(jnp.float32)
            segment_wide = grad_query_segment.astype(jnp.float32)
            grad_projected = (content_wide + position_wide + segment_wide).astype(jnp.bfloat16)
            grad_query_w = matmul(inputs.T, grad_projected)
            grad_inputs = grad_residual + matmul(grad_projected, w_query.T)
            stream_grads = (
                grad_query_w,
                grad_out_w,
                jnp.sum(content_wide, axis=0),
                jnp.sum(position_wide, axis=0),
                jnp.sum(segment_wide, axis=0),
                grad_segment_table,
                grad_first_gain,
                grad_first_shift,
                grad_inner_w,
                grad_inner_bias,
                grad_outer_w,
                grad_outer_bias,
                grad_second_gain,
                grad_second_shift,
            )
            return (
                final_out.astype(jnp.bfloat16),
                grad_inputs,
                stream_grads,
                grad_keys,
                grad_values,
                grad_relative,
            )

        (
            content_out,
            content_grad,
            content_grads,
            content_keys_grad,
            content_values_grad,
            content_relative,
        ) = stream(content, content_allowed, content_grad_out)
        query_out, query_grad, query_grads, query_keys_grad, query_values_grad, query_relative = (
            stream(query_rows, query_allowed, query_grad_out)
        )
        joined = jax.tree.map(jnp.add, content_grads, query_grads)
        keys_low = heads_joined(content_keys_grad + query_keys_grad).astype(jnp.bfloat16)
        values_low = heads_joined(content_values_grad + query_values_grad).astype(jnp.bfloat16)
        relative_low = heads_joined(content_relative + query_relative)[:relative_count].astype(
            jnp.bfloat16
        )
        grad_rel_w = matmul(position_low.T, relative_low)
        grad_key_w = matmul(content.T, keys_low[MEM:])
        grad_value_w = matmul(content.T, values_low[MEM:])
        passed_back = (keys_low[:MEM], values_low[:MEM])
        grad_content_total = (
            content_grad + matmul(keys_low[MEM:], w_key.T) + matmul(values_low[MEM:], w_value.T)
        )
        contributions = (
            joined[0],
            grad_key_w,
            grad_value_w,
            joined[1],
            grad_rel_w,
            joined[2],
            joined[3],
            joined[4],
            joined[5],
            joined[6],
            joined[7],
            joined[8],
            joined[9],
            joined[10],
            joined[11],
            joined[12],
            joined[13],
        )
        new_totals = jax.tree.map(jnp.add, totals, contributions)
        produced = (
            content_out,
            query_out,
            grad_content_total.astype(jnp.bfloat16),
            query_grad.astype(jnp.bfloat16),
        ) + passed_back
        return (new_totals, produced)

    weight_list = (
        w_query,
        w_key,
        w_value,
        w_out,
        w_rel,
        bias_content,
        bias_position,
        bias_segment,
        segment_embed,
        gain_one,
        shift_one,
        w_inner,
        bias_inner,
        w_outer,
        bias_outer,
        gain_two,
        shift_two,
    )
    zero_totals = jax.tree.map(lambda tensor: jnp.zeros(tensor.shape, jnp.float32), weight_list)
    totals, stacked = lax.scan(
        one_sequence,
        zero_totals,
        (
            content_in,
            query_in,
            memory_side,
            sequence_lengths,
            order_rank,
            segment_ids,
            content_cotangent,
            query_cotangent,
        ),
    )
    (
        grad_query,
        grad_key,
        grad_value,
        grad_out,
        grad_rel,
        grad_content_bias,
        grad_position_bias,
        grad_segment_bias,
        grad_seg_table,
        grad_gain_one,
        grad_shift_one,
        grad_inner,
        grad_inner_bias,
        grad_outer,
        grad_outer_bias,
        grad_gain_two,
        grad_shift_two,
    ) = totals
    back_keys, back_values = (
        lax.all_to_all(stacked[4], "mem", split_axis=1, concat_axis=0, tiled=True),
        lax.all_to_all(stacked[5], "mem", split_axis=1, concat_axis=0, tiled=True),
    )
    memory_rows_flat = memory.reshape(-1, D)
    grad_key = grad_key + matmul(memory_rows_flat.T, back_keys.reshape(-1, D))
    grad_value = grad_value + matmul(memory_rows_flat.T, back_values.reshape(-1, D))
    summed = lax.psum(
        (
            grad_query,
            grad_key,
            grad_value,
            grad_out,
            grad_rel,
            grad_content_bias,
            grad_position_bias,
            grad_segment_bias,
            grad_seg_table,
            grad_gain_one,
            grad_shift_one,
            grad_inner,
            grad_inner_bias,
            grad_outer,
            grad_outer_bias,
            grad_gain_two,
            grad_shift_two,
        ),
        ("batch", "mem"),
    )
    return (
        stacked[0],
        stacked[1],
        stacked[2],
        stacked[3],
        summed[0],
        summed[1],
        summed[2],
        summed[3],
        summed[4],
        summed[5],
        summed[6],
        summed[7],
        summed[8],
        summed[9],
        summed[10],
        summed[11],
        summed[12],
        summed[13],
        summed[14],
        summed[15],
        summed[16],
    )


def solution(mesh):
    return jax.shard_map(
        shards,
        mesh=mesh,
        in_specs=(
            P(("batch", "mem"), None, None),
            P(("batch", "mem"), None, None),
            P("batch", "mem", None),
            P(("batch", "mem")),
            P(("batch", "mem"), None),
            P(("batch", "mem"), None),
            P(),
            P(),
            P(),
            P(),
            P(),
            P(),
            P(),
            P(),
            P(),
            P(),
            P(),
            P(),
            P(),
            P(),
            P(),
            P(),
            P(),
            P(("batch", "mem"), None, None),
            P(("batch", "mem"), None, None),
        ),
        out_specs=(
            P(("batch", "mem"), None, None),
            P(("batch", "mem"), None, None),
            P(("batch", "mem"), None, None),
            P(("batch", "mem"), None, None),
            P(),
            P(),
            P(),
            P(),
            P(),
            P(),
            P(),
            P(),
            P(),
            P(),
            P(),
            P(),
            P(),
            P(),
            P(),
            P(),
            P(),
        ),
        check_vma=False,
    )
```

profile of v0, /device:TPU:0, one launch (start us, length us, event | category | flops | bytes accessed | tf_op | source)
XLA Modules:
  0.0 1586.7 jit_solution(15338260703119654508)
XLA Ops:
  48.7 14.8 fusion.154
  63.5 15.1 fusion.153
  103.0 54.9 %reshape.539 = f32[12,721408]{1,0:T(8,128)} reshape(f32[12,512,1409]{2,1,0:T(8,128)} %fusion.154) | data formatting | bytes 69255168 | tf_op jit(solution)/shard_map/while/body/eval_jaxpr/reshape | solution.py:40
  157.8 36.5 %slice.91 = f32[12,720896]{1,0:T(8,128)} slice(f32[12,721408]{1,0:T(8,128)} %reshape.539), slice={[0:12], [511:721407]} | slice | bytes 69206016 | tf_op jit(solution)/shard_map/while/body/eval_jaxpr/slice | solution.py:40
  194.4 39.6 %copy.165 = f32[2,8,512,1408]{3,2,1,0:T(8,128)} copy(f32[2,8,512,1408]{3,1,2,0:T(8,128)} %bitcast.331) | data formatting | bytes 92274688
  234.0 23.0 %slice.101 = f32[12,512,1408]{2,1,0:T(8,128)} slice(f32[16,512,1408]{2,1,0:T(8,128)} %bitcast.333), slice={[0:12], [0:512], [0:1408]} | slice | bytes 69206016 | tf_op jit(solution)/shard_map/while/body/eval_jaxpr/reshape | solution.py:43
  257.0 55.1 %reshape.532 = f32[12,721408]{1,0:T(8,128)} reshape(f32[12,512,1409]{2,1,0:T(8,128)} %fusion.153) | data formatting | bytes 69255168 | tf_op jit(solution)/shard_map/while/body/eval_jaxpr/reshape | solution.py:40
  312.1 36.5 %slice.87 = f32[12,720896]{1,0:T(8,128)} slice(f32[12,721408]{1,0:T(8,128)} %reshape.532), slice={[0:12], [511:721407]} | slice | bytes 69206016 | tf_op jit(solution)/shard_map/while/body/eval_jaxpr/slice | solution.py:40
  348.6 39.6 %copy.164 = f32[2,8,512,1408]{3,2,1,0:T(8,128)} copy(f32[2,8,512,1408]{3,1,2,0:T(8,128)} %bitcast.332) | data formatting | bytes 92274688
  388.3 23.1 %slice.100 = f32[12,512,1408]{2,1,0:T(8,128)} slice(f32[16,512,1408]{2,1,0:T(8,128)} %bitcast.334), slice={[0:12], [0:512], [0:1408]} | slice | bytes 69206016 | tf_op jit(solution)/shard_map/while/body/eval_jaxpr/reshape | solution.py:43
  419.3 18.2 %fusion.150 = (f32[12,512]{1,0:T(8,128)S(1)}, f32[12,512,896]{2,1,0:T(8,128)}) fusion(f32[12,512]{1,0:T(8,128)S(1)} %get-tuple-element.364, f32[12,512]{1,0:T(8,128)S(1)} %get-tuple-element.365, pred[512,896]{1,0:T(8,128)(4,1)} %broadcast_compare_fusion, f32[12,512,1408]{2,1,0:T(8,128)} %slice.101, bf16[12,512,64]{1,2,0:T(8,128)(2,1)S(1)} %bitcast.362, ...), kind=kOutput, calls=%fused_computation.270 | convolution fusion | flops 740419584 | bytes 47194112 | tf_op jit(solution)/shard_map/while/body/eval_jaxpr/hid,hjd->hij/dot_general | solution.py:144
  458.5 18.1 %fusion.147 = (f32[12,512]{1,0:T(8,128)}, f32[12,512,896]{2,1,0:T(8,128)}) fusion(f32[12,512]{1,0:T(8,128)} %get-tuple-element.362, f32[12,512]{1,0:T(8,128)} %get-tuple-element.363, pred[512,896]{1,0:T(8,128)(4,1)} %broadcast_compare_fusion, f32[12,512,1408]{2,1,0:T(8,128)} %slice.100, bf16[12,512,64]{1,2,0:T(8,128)(2,1)} %bitcast.366, ...), kind=kOutput, calls=%fused_computation.267 | convolution fusion | flops 740419584 | bytes 47194112 | tf_op jit(solution)/shard_map/while/body/eval_jaxpr/hid,hjd->hij/dot_general | solution.py:144
  503.0 18.0 %multiply_convert_fusion.3 = (bf16[512,3072]{1,0:T(8,128)(2,1)S(1)}, f32[512,3072]{1,0:T(8,128)S(1)}, f32[512,3072]{1,0:T(8,128)}) fusion(f32[3072]{0:T(1024)S(1)} %copy-done.93, bf16[768,3072]{1,0:T(8,128)(2,1)S(1)} %bitcast.404, f32[512,768]{1,0:T(8,128)S(1)} %get-tuple-element.350, f32[768]{0:T(1024)S(1)} %copy-done.73, f32[768]{0:T(1024)S(1)} %copy-done.69, ...), kind=kOutput, calls=%fused_computation.53 | convolution fusion | flops 2521694208 | bytes 22042624 | tf_op jit(solution)/shard_map/while/body/eval_jaxpr/dot_general | solution.py:51
  527.9 22.6 %convert_reduce_fusion.1 = (f32[3072]{0:T(1024)}, bf16[512,3072]{1,0:T(8,128)(2,1)}, bf16[512,3072]{1,0:T(8,128)(2,1)S(1)}, f32[512,3072]{1,0:T(8,128)}) fusion(f32[512,3072]{1,0:T(8,128)S(1)} %get-tuple-element.310, f32[512,3072]{1,0:T(8,128)} %get-tuple-element.351, f32[3072]{0:T(1024)S(1)} %copy-done.93, f32[512,3072]{1,0:T(8,128)S(1)} %fusion.133, ...), kind=kOutput, calls=%fused_computation.37 | convolution fusion | flops 2546463744 | bytes 36986880 | tf_op jit(solution)/shard_map/while/body/eval_jaxpr/dot_general | solution.py:51
  598.5 26.8 %multiply_convert_fusion.1 = bf16[12,512,896]{2,1,0:T(8,128)(2,1)} fusion(f32[12,512,896]{2,1,0:T(8,128)} %get-tuple-element.348, f32[12,512]{1,0:T(8,128)S(1)} %copy-done.68, bf16[12,512,64]{1,2,0:T(8,128)(2,1)} %bitcast.370, bf16[512,12,64]{0,2,1:T(8,128)(2,1)S(1)} %bitcast.358, bf16[384,12,64]{0,2,1:T(8,128)(2,1)S(1)} %copy-done.36), kind=kOutput, calls=%fused_computation.21 | convolution fusion | flops 1453333376 | bytes 35217408 | tf_op jit(solution)/shard_map/while/body/eval_jaxpr/sub | solution.py:215
  637.7 32.9 %fusion.4 = (f32[12,512]{1,0:T(8,128)S(1)}, f32[12,512]{1,0:T(8,128)S(1)}, f32[12,512]{1,0:T(8,128)S(1)}, f32[12,512]{1,0:T(8,128)S(1)}, bf16[12,512,896]{2,1,0:T(8,128)(2,1)}) fusion(pred[512,896]{1,0:T(8,128)(4,1)} %broadcast_compare_fusion, bf16[12,512,896]{2,1,0:T(8,128)(2,1)} %multiply_convert_fusion.1, f32[12,512,896]{2,1,0:T(8,128)} %get-tuple-element.355, ...), kind=kOutput, calls=%fused_computation.8 | convolution fusion | flops 1508359040 | bytes 46784512 | tf_op jit(solution)/shard_map/while/body/eval_jaxpr/sub | solution.py:215
  779.8 19.6 %copy.167 = bf16[2,8,512,1408]{3,1,2,0:T(8,128)(2,1)S(1)} copy(bf16[2,8,512,1408]{3,2,1,0:T(8,128)(2,1)} %bitcast.337) | data formatting | bytes 46137344
  811.6 69.5 %convert_element_type.485 = bf16[12,512,1409]{2,1,0:T(8,128)(2,1)} reshape(bf16[12,721408]{1,0:T(8,128)(2,1)} %pad.26) | data formatting | bytes 34627584 | tf_op jit(solution)/shard_map/while/body/eval_jaxpr/convert_element_type | solution.py:228
  881.1 14.8 pad.37
  895.9 19.6 %copy.166 = bf16[2,8,512,1408]{3,1,2,0:T(8,128)(2,1)S(1)} copy(bf16[2,8,512,1408]{3,2,1,0:T(8,128)(2,1)} %bitcast.338) | data formatting | bytes 46137344
  927.7 69.1 %convert_element_type.464 = bf16[12,512,1409]{2,1,0:T(8,128)(2,1)} reshape(bf16[12,721408]{1,0:T(8,128)(2,1)} %pad.24) | data formatting | bytes 34627584 | tf_op jit(solution)/shard_map/while/body/eval_jaxpr/convert_element_type | solution.py:228
  1032.4 12.2 fusion.71
  1091.9 44.5 %all-reduce.7 = (f32[768]{0:T(1024)}, f32[768]{0:T(1024)}, f32[768]{0:T(1024)}, f32[2,768]{1,0:T(2,128)}, f32[768]{0:T(1024)}, /*index=5*/f32[768]{0:T(1024)}, f...) all-reduce(f32[768]{0:T(1024)S(1)} %add.557, ...), channel_id=1, replica_groups=mesh['batch'=8,'mem'=4] {'batch','mem'}, use_global_device_ids=true, to_apply=%region_33.34 | all-reduce | flops 10752 | bytes 86016 | tf_op jit(solution)/shard_map/psum | solution.py:392
  1144.3 410.0 %all-reduce.11.cloned.1.call-done = (f32[768,768]{0,1:T(8,128)}, f32[768,768]{0,1:T(8,128)}, f32[768,768]{0,1:T(8,128)}, f32[768,768]{1,0:T(8,128)}, f32[768,768...) async-done(((f32[768,768]{0,1:T(8,128)}, f32[768,768]{0,1:T(8,128)}, f32[768,768]{0,1:T(8,128)}, f32[768,768]{1,0:T(8,128)}, f32[768,768]{1,0:T(8,128)}, ...) | async-done | bytes 30670864 | tf_op jit(solution)/shard_map/psum | solution.py:392
  (456 shorter events, 436.0 us)
Async XLA Ops:
  7.2 25.4 %copy-start = (bf16[768,768]{1,0:T(8,128)(2,1)S(1)}, bf16[768,768]{1,0:T(8,128)(2,1)}, u32[]{:S(2)}) copy-start(bf16[768,768]{1,0:T(8,128)(2,1)} %param.31) | copy-start | bytes 3538948
  10.2 73.9 %all-to-all-start.1 = ((bf16[4,96,768]{2,1,0:T(8,128)(2,1)}), bf16[4,96,768]{2,1,0:T(8,128)(2,1)}, u32[]{:S(2)}, u32[]{:S(2)}) async-start(bf16[4,96,768]{2,1,0:T(8,128)(2,1)} %bitcast.16), calls=%async_computation.1 | async-start | bytes 1179648 | tf_op jit(solution)/shard_map/all_to_all | solution.py:113
  17.3 27.6 %copy-start.70 = (bf16[2,12,64]{2,1,0:T(8,128)(2,1)}, bf16[2,12,64]{2,1,0:T(8,128)(2,1)S(1)}, u32[]{:S(2)}) copy-start(bf16[2,12,64]{2,1,0:T(8,128)(2,1)S(1)} %reshape.535) | copy-start | bytes 9220
  40.6 22.9 %copy-start.9 = (bf16[512,768]{0,1:T(8,128)(2,1)}, bf16[512,768]{0,1:T(8,128)(2,1)S(1)}, u32[]{:S(2)}) copy-start(bf16[512,768]{0,1:T(8,128)(2,1)S(1)} %copy.125) | copy-start | bytes 2359300
  84.1 332.1 %all-to-all-start = ((bf16[4,96,768]{2,1,0:T(8,128)(2,1)}), bf16[4,96,768]{2,1,0:T(8,128)(2,1)}, u32[]{:S(2)}, u32[]{:S(2)}) async-start(bf16[4,96,768]{2,1,0:T(8,128)(2,1)} %bitcast.396), calls=%async_computation | async-start | bytes 1179648 | tf_op jit(solution)/shard_map/all_to_all | solution.py:112
  388.2 23.2 %copy-start.95 = (s32[1,512]{1,0:T(1,128)S(1)}, s32[1,512]{1,0:T(1,128)}, u32[]{:S(2)}) copy-start(s32[1,512]{1,0:T(1,128)} %param.29) | copy-start | bytes 6148
  388.2 23.2 %copy-start.94 = (s32[1,512]{1,0:T(1,128)S(1)}, s32[1,512]{1,0:T(1,128)}, u32[]{:S(2)}) copy-start(s32[1,512]{1,0:T(1,128)} %param.30) | copy-start | bytes 6148
  388.2 23.2 %copy-start.79 = (f32[12,512,1]{1,2,0:T(1,128)S(1)}, f32[12,512,1]{1,2,0:T(1,128)}, u32[]{:S(2)}) copy-start(f32[12,512,1]{1,2,0:T(1,128)} %get-tuple-element.329) | copy-start | bytes 73732
  388.3 23.2 %copy-start.80 = (f32[12,512,1]{1,2,0:T(1,128)S(1)}, f32[12,512,1]{1,2,0:T(1,128)}, u32[]{:S(2)}) copy-start(f32[12,512,1]{1,2,0:T(1,128)} %get-tuple-element.330) | copy-start | bytes 73732
  416.2 31.5 %copy-start.34 = (bf16[384,12,64]{0,2,1:T(8,128)(2,1)}, bf16[384,12,64]{0,2,1:T(8,128)(2,1)S(1)}, u32[]{:S(2)}) copy-start(bf16[384,12,64]{0,2,1:T(8,128)(2,1)S(1)} %concatenate.40) | copy-start | bytes 1769476
  458.1 120.5 %copy-start.3 = (f32[512,768]{1,0:T(8,128)}, f32[512,768]{1,0:T(8,128)S(1)}, u32[]{:S(2)}) copy-start(f32[512,768]{1,0:T(8,128)S(1)} %get-tuple-element.357) | copy-start | bytes 4718596
  458.5 18.1 %copy-start.84 = (f32[512]{0:T(512)}, f32[512]{0:T(512)S(1)}, u32[]{:S(2)}) copy-start(f32[512]{0:T(512)S(1)} %multiply_reduce_fusion.7) | copy-start | bytes 6148
  497.3 81.4 %copy-start.29 = (f32[512,768]{1,0:T(8,128)}, f32[512,768]{1,0:T(8,128)S(1)}, u32[]{:S(2)}) copy-start(f32[512,768]{1,0:T(8,128)S(1)} %get-tuple-element.350) | copy-start | bytes 4718596
  497.6 81.0 %copy-start.96 = (f32[512]{0:T(512)}, f32[512]{0:T(512)S(1)}, u32[]{:S(2)}) copy-start(f32[512]{0:T(512)S(1)} %fusion.115) | copy-start | bytes 6148
  497.6 23.4 %slice-start.15 = ((s8[4718592]{0:T(1024)(128)(4,1)}), s8[4194304]{0:T(1024)(128)(4,1)S(1)}, s32[]{:S(2)}) async-start(s8[4718592]{0:T(1024)(128)(4,1)} %bitcast.401), calls=%async_computation.20 | async-start | bytes 8388608
  503.0 24.9 %copy-start.116 = (f32[512,3072]{1,0:T(8,128)}, f32[512,3072]{1,0:T(8,128)S(1)}, u32[]{:S(2)}) copy-start(f32[512,3072]{1,0:T(8,128)S(1)} %fusion.133) | copy-start | bytes 18874372
  503.0 18.0 %copy-start.101 = (f32[768]{0:T(1024)S(1)}, f32[768]{0:T(1024)}, u32[]{:S(2)}) copy-start(f32[768]{0:T(1024)} %convert_element_type.440) | copy-start | bytes 9220
  527.9 22.6 %copy-start.63 = (bf16[512,768]{1,0:T(8,128)(2,1)}, bf16[512,768]{1,0:T(8,128)(2,1)S(1)}, u32[]{:S(2)}) copy-start(bf16[512,768]{1,0:T(8,128)(2,1)S(1)} %get-tuple-element.294) | copy-start | bytes 2359300
  583.4 146.2 %copy-start.98 = (f32[512]{0:T(512)}, f32[512]{0:T(512)S(1)}, u32[]{:S(2)}) copy-start(f32[512]{0:T(512)S(1)} %negate_multiply_fusion.2) | copy-start | bytes 6148
  752.0 303.1 %all-to-all-start.2 = ((bf16[4,2,36864]{2,1,0:T(2,128)(2,1)}), bf16[4,2,36864]{2,1,0:T(2,128)(2,1)}, u32[]{:S(2)}, u32[]{:S(2)}) async-start(bf16[4,2,36864]{2,1,0:T(2,128)(2,1)} %reshape.548), calls=%async_computation.2 | async-start | bytes 1179648 | tf_op jit(solution)/shard_map/all_to_all | solution.py:386
  927.7 69.1 %copy-start.10 = (bf16[512,768]{0,1:T(8,128)(2,1)S(1)}, bf16[512,768]{0,1:T(8,128)(2,1)}, u32[]{:S(2)}) copy-start(bf16[512,768]{0,1:T(8,128)(2,1)} %copy-done.9) | copy-start | bytes 2359300
  1055.2 20.6 %all-to-all-start.3 = ((bf16[4,2,36864]{2,1,0:T(2,128)(2,1)}), bf16[4,2,36864]{2,1,0:T(2,128)(2,1)}, u32[]{:S(2)}, u32[]{:S(2)}) async-start(bf16[4,2,36864]{2,1,0:T(2,128)(2,1)} %reshape.550), calls=%async_computation.3 | async-start | bytes 1179648 | tf_op jit(solution)/shard_map/all_to_all | solution.py:387
  1060.3 494.0 %all-reduce.11.cloned.1.call-start = ((), (), s32[]{:S(2)}) async-start(), calls=%async_computation.4 | async-start | bytes 61341696 | tf_op jit(solution)/shard_map/psum | solution.py:392
  1083.7 55.2 %copy-start.112 = (bf16[512,12,64]{0,2,1:T(8,128)(2,1)S(1)}, bf16[512,12,64]{0,2,1:T(8,128)(2,1)}, u32[]{:S(2)}) copy-start(bf16[512,12,64]{0,2,1:T(8,128)(2,1)} %get-tuple-element.314) | copy-start | bytes 2359300
  (119 other events, 865.4 us)
Sparse Core Ops, SparseCore 0:
  1082.2 472.0 all-reduce.10
where the time goes:
time: 1600 us; the launch traced here: 1590 us
  local copies, waits for them, and re-layouts  629 us (39%)
  waiting for transfers between devices  410 us (26%)
  matrix products  402 us (25%)
  other arithmetic  61.8 us (4%)
  blocking collectives  44.5 us (3%)
  starting transfers between devices  22.3 us (1%)
  between operations  16.5 us (1%)
    psum x1, waiting for transfers between devices, shards(): lax.psum((grad_query, grad_key, grad_value, grad_out, grad_rel, grad_cont...  410 us
    unnamed x295, local copies, waits for them, and re-layouts  186 us
    dot_general x36, matrix products, matmul(): return jnp.dot(left, right, preferred_element_type=jnp.float32)  155 us
    convert_element_type x2, local copies, waits for them, and re-layouts, stream(): grad_grid_low = grad_grid.astype(jnp.bfloat16)  139 us
    reshape x2, local copies, waits for them, and re-layouts, skew_grid(): score_grid.reshape(head_count, row_count * column_count)  110 us
    slice x2, local copies, waits for them, and re-layouts, skew_grid(): score_grid.reshape(head_count, row_count * column_count)  73.1 us
    sub x2, matrix products, stream(): grad_soft - jnp.sum(soft_again * grad_soft, axis=-1, keepdims=True)  59.7 us
    reshape x2, local copies, waits for them, and re-layouts, skew_grid(): flattened.reshape(head_count, row_count, column_count - 1)  46.1 us
  transfers between devices with their start and end apart: 5, of which 1 were waited for; matrix products, arithmetic and copies ran while one was open for 45% of the time, Pallas kernels for 0%

commit v1 on v0

v1 whole, which is shorter than its diff:
```python
import jax
import jax.numpy as jnp
from jax import lax
from jax.experimental import pallas as pl
from jax.experimental.pallas import tpu as pltpu
from jax.sharding import PartitionSpec as P

D = 768
HEADS = 12
HEAD = 64
SEG = 512
MEM = 384
KEYS = MEM + SEG
REL = MEM + 2 * SEG
PAIR = 2 * HEAD
PAIRS = HEADS // 2
ROWS = 256
SUB = 128
WIN = KEYS + SUB
FAR = -1e30
LOG2E = 1.4426950408889634
SCALE = HEAD**-0.5
VMEM_BYTES = 60 * 1024 * 1024
nt = (((1,), (1,)), ((), ()))
nn = (((1,), (0,)), ((), ()))
tn = (((0,), (0,)), ((), ()))


def mm(left, right, dims):
    return lax.dot_general(left, right, dims, preferred_element_type=jnp.float32)


def lane_low(rows):
    return lax.broadcasted_iota(jnp.int32, (rows, PAIR), 1) < HEAD


def forward_kernel(
    qc_ref, qp_ref, qs_ref, k_ref, v_ref, rel_ref, emb_ref, qseg_ref, kseg_ref, qrank_ref, krank_ref,
    mix_ref, inv_ref, prob_ref, kcat, vcat,
):
    half = pl.program_id(2)

    @pl.when((pl.program_id(1) == 0) & (half == 0))
    def _():
        low = lane_low(KEYS)
        same = kseg_ref[...] == 0
        kcat[0, :, :PAIR] = k_ref[...]
        kcat[1, :, :PAIR] = k_ref[...]
        zero_row = emb_ref[0:1, :].astype(jnp.float32)
        one_row = emb_ref[1:2, :].astype(jnp.float32)
        zero_roll = pltpu.roll(zero_row, HEAD, 1)
        one_roll = pltpu.roll(one_row, HEAD, 1)
        low_row = lane_low(1)
        for head in range(2):
            if head == 0:
                near = jnp.where(low_row, zero_row, one_roll)
                away = jnp.where(low_row, one_row, zero_roll)
            else:
                near = jnp.where(low_row, zero_roll, one_row)
                away = jnp.where(low_row, one_roll, zero_row)
            kcat[head, :, PAIR:] = jnp.where(same, near, away).astype(jnp.bfloat16)
        vcat[:, :PAIR] = v_ref[...]
        vcat[:, PAIR:] = jnp.ones((KEYS, PAIR), jnp.bfloat16)

    low = lane_low(ROWS)
    zero = jnp.zeros((ROWS, PAIR), jnp.bfloat16)
    qc = qc_ref[...]
    qp = qp_ref[...]
    qs = qs_ref[...]
    qs_roll = pltpu.roll(qs.astype(jnp.float32), HEAD, 1).astype(jnp.bfloat16)
    first = qseg_ref[...] == 0
    seg_keep = first == low
    krank = krank_ref[...]
    mixed = []
    inverse = []
    for head in range(2):
        mine = low if head == 0 else ~low
        twice = jnp.where(mine, qs, qs_roll)
        qcat = jnp.concatenate(
            [jnp.where(mine, qc, zero), jnp.where(seg_keep, twice, zero)], axis=1
        )
        score = mm(qcat, kcat[head], nt)
        qp_mine = jnp.where(mine, qp, zero)
        parts = []
        for sub in range(ROWS // SUB):
            tile = half * (ROWS // SUB) + sub
            window = rel_ref[pl.ds(3 - tile, WIN // SUB)].reshape(WIN, PAIR)
            grid = mm(qp_mine[sub * SUB : (sub + 1) * SUB], window, nt)
            shifted = pltpu.roll(grid, WIN - SUB + 1, 1, stride=1, stride_axis=0)[:, :KEYS]
            logit = score[sub * SUB : (sub + 1) * SUB] + shifted
            current = jnp.where(
                krank <= qrank_ref[sub * SUB : (sub + 1) * SUB, :], logit[:, MEM:], FAR
            )
            past = logit[:, :MEM]
            top = jnp.maximum(
                jnp.max(past, axis=-1, keepdims=True), jnp.max(current, axis=-1, keepdims=True)
            )
            factor = SCALE * LOG2E
            soft = jnp.concatenate(
                [jnp.exp2((past - top) * factor), jnp.exp2((current - top) * factor)], axis=1
            ).astype(jnp.bfloat16)
            prob_ref[head, sub * SUB : (sub + 1) * SUB, :] = soft
            parts.append(soft)
        summed = mm(jnp.concatenate(parts, axis=0), vcat[...], nn)
        scale = 1.0 / summed[:, PAIR:]
        mixed.append(summed[:, :PAIR] * scale)
        inverse.append(scale)
    mix_ref[...] = jnp.where(low, mixed[0], mixed[1]).astype(jnp.bfloat16)
    inv_ref[...] = jnp.where(low, inverse[0], inverse[1])


def attention_forward(qc, qp, qs, keys, values, rel, emb, qseg, kseg, qrank, krank):
    halves = SEG // ROWS
    row = pl.BlockSpec((ROWS, PAIR), lambda p, s, h: (s * halves + h, p))
    col = pl.BlockSpec((ROWS, 1), lambda p, s, h: (s * halves + h, 0))
    pair = lambda rows: pl.BlockSpec((rows, PAIR), lambda p, s, h: (0, p))
    return pl.pallas_call(
        forward_kernel,
        grid=(PAIRS, 2, halves),
        in_specs=[
            row, row, row, pair(KEYS), pair(KEYS),
            pl.BlockSpec((REL // SUB, SUB, PAIR), lambda p, s, h: (0, 0, p)),
            pair(2), col,
            pl.BlockSpec((KEYS, 1), lambda p, s, h: (0, 0)),
            col,
            pl.BlockSpec((1, SEG), lambda p, s, h: (0, 0)),
        ],
        out_specs=[
            row, row,
            pl.BlockSpec((None, 2, ROWS, KEYS), lambda p, s, h: (p, 0, s * halves + h, 0)),
        ],
        out_shape=[
            jax.ShapeDtypeStruct((2 * SEG, D), jnp.bfloat16),
            jax.ShapeDtypeStruct((2 * SEG, D), jnp.float32),
            jax.ShapeDtypeStruct((PAIRS, 2, 2 * SEG, KEYS), jnp.bfloat16),
        ],
        scratch_shapes=[
            pltpu.VMEM((2, KEYS, 2 * PAIR), jnp.bfloat16),
            pltpu.VMEM((KEYS, 2 * PAIR), jnp.bfloat16),
        ],
        compiler_params=pltpu.CompilerParams(
            dimension_semantics=("arbitrary",) * 3, vmem_limit_bytes=VMEM_BYTES
        ),
        name="attention_forward",
    )(qc, qp, qs, keys, values, rel.reshape(REL // SUB, SUB, D), emb, qseg, kseg, qrank, krank)


def backward_kernel(
    prob_ref, dmix_ref, mix_ref, inv_ref, qc_ref, qp_ref, qs_ref, k_ref, v_ref, rel_ref, emb_ref,
    qseg_ref, kseg_ref,
    dproj_ref, dk_ref, dv_ref, drel_ref, small_ref,
    kcat, dk_acc, dv_acc, drel_acc,
):
    stream = pl.program_id(1)
    half = pl.program_id(2)
    halves = SEG // ROWS

    @pl.when((stream == 0) & (half == 0))
    def _():
        kcat[:, :PAIR] = k_ref[...]
        kcat[:, PAIR:] = jnp.where((kseg_ref[...] == 0) == lane_low(KEYS), 1.0, 0.0).astype(
            jnp.bfloat16
        )
        dk_acc[...] = jnp.zeros_like(dk_acc)
        dv_acc[...] = jnp.zeros_like(dv_acc)
        drel_acc[...] = jnp.zeros_like(drel_acc)
        small_ref[...] = jnp.zeros_like(small_ref)

    low = lane_low(ROWS)
    low_sub = lane_low(SUB)
    zero = jnp.zeros((ROWS, PAIR), jnp.bfloat16)
    flip = jnp.where(
        lax.broadcasted_iota(jnp.int32, (SUB, SUB), 0) + lax.broadcasted_iota(jnp.int32, (SUB, SUB), 1)
        == SUB - 1,
        1.0, 0.0,
    ).astype(jnp.bfloat16)
    dmix = (dmix_ref[...].astype(jnp.float32) * (inv_ref[...] * SCALE)).astype(jnp.bfloat16)
    weighted = dmix.astype(jnp.float32) * mix_ref[...].astype(jnp.float32)
    qc = qc_ref[...]
    qp = qp_ref[...]
    qs = qs_ref[...].astype(jnp.float32)
    flipped = [
        mm(flip, qp[s * SUB : (s + 1) * SUB], nn).astype(jnp.bfloat16) for s in range(ROWS // SUB)
    ]
    first = qseg_ref[...] == 0
    emb = emb_ref[...].astype(jnp.float32)
    dqc = []
    dqs = []
    seg_sum = []
    dqp = [[] for _ in range(ROWS // SUB)]
    grids = [[] for _ in range(ROWS // SUB)]
    totals = []
    dm_heads = []
    qc_heads = []
    for head in range(2):
        mine = low if head == 0 else ~low
        dm = jnp.where(mine, dmix, zero)
        dm_heads.append(dm)
        qc_heads.append(jnp.where(mine, qc, zero))
        row_sum = jnp.sum(jnp.where(mine, weighted, 0.0), axis=-1, keepdims=True)
        dprob = mm(dm, v_ref[...], nt)
        total = (prob_ref[head].astype(jnp.float32) * (dprob - row_sum)).astype(jnp.bfloat16)
        totals.append(total)
        back = mm(total, kcat[...], nn)
        dqc.append(back[:, :PAIR])
        sums = back[:, PAIR:]
        sums_roll = pltpu.roll(sums, HEAD, 1)
        key_zero = jnp.where(low, sums, sums_roll)
        key_one = jnp.where(low, sums_roll, sums)
        same = jnp.where(first, key_zero, key_one)
        other = jnp.where(first, key_one, key_zero)
        dqs.append(same * emb[0:1] + other * emb[1:2])
        seg_sum.append((same, other))
        for s in range(ROWS // SUB):
            tile = half * (ROWS // SUB) + s
            turned = mm(flip, total[s * SUB : (s + 1) * SUB], nn)
            padded = jnp.concatenate([turned, jnp.zeros((SUB, SUB), jnp.float32)], axis=1)
            grid = pltpu.roll(padded, 0, 1, stride=1, stride_axis=0).astype(jnp.bfloat16)
            grids[s].append(grid)
            window = rel_ref[pl.ds(3 - tile, WIN // SUB)].reshape(WIN, PAIR)
            dqp[s].append(mm(grid, window, nn))
    prob_all = prob_ref[...].reshape(2 * ROWS, KEYS)
    dv_acc[...] += mm(jnp.concatenate(dm_heads, axis=0), prob_all, tn)
    dk_acc[...] += mm(jnp.concatenate(qc_heads, axis=0), jnp.concatenate(totals, axis=0), tn)
    position_parts = []
    for s in range(ROWS // SUB):
        tile = half * (ROWS // SUB) + s
        zero_sub = jnp.zeros((SUB, PAIR), jnp.bfloat16)
        left = jnp.concatenate(
            [jnp.where(low_sub, flipped[s], zero_sub), jnp.where(low_sub, zero_sub, flipped[s])],
            axis=0,
        )
        drel = mm(left, jnp.concatenate(grids[s], axis=0), tn)
        for block in range(WIN // SUB):
            drel_acc[3 - tile + block] += drel[:, block * SUB : (block + 1) * SUB]
        turned = jnp.where(low_sub, dqp[s][0], dqp[s][1]).astype(jnp.bfloat16)
        position_parts.append(mm(flip, turned, nn))
    dqp_wide = jnp.concatenate(position_parts, axis=0)
    dqc_wide = jnp.where(low, dqc[0], dqc[1]).astype(jnp.bfloat16).astype(jnp.float32)
    dqs_wide = jnp.where(low, dqs[0], dqs[1]).astype(jnp.bfloat16).astype(jnp.float32)
    dproj_ref[...] = (dqc_wide + dqp_wide + dqs_wide).astype(jnp.bfloat16)
    same = jnp.where(low, seg_sum[0][0], seg_sum[1][0])
    other = jnp.where(low, seg_sum[0][1], seg_sum[1][1])
    rows = [
        dqc_wide, dqp_wide, dqs_wide, same * qs, other * qs,
    ]
    for index, value in enumerate(rows):
        small_ref[index : index + 1, :] += jnp.sum(value, axis=0, keepdims=True)

    @pl.when((stream == 1) & (half == halves - 1))
    def _():
        dk_ref[...] = dk_acc[...].T.astype(jnp.bfloat16)
        dv_ref[...] = (dv_acc[...].T * (1.0 / SCALE)).astype(jnp.bfloat16)
        for block in range(REL // SUB):
            drel_ref[block] = drel_acc[block].T.astype(jnp.bfloat16)


def attention_backward(
    prob, dmix, mix, inv, qc, qp, qs, keys, values, rel, emb, qseg, kseg
):
    halves = SEG // ROWS
    row = pl.BlockSpec((ROWS, PAIR), lambda p, s, h: (s * halves + h, p))
    col = pl.BlockSpec((ROWS, 1), lambda p, s, h: (s * halves + h, 0))
    pair = lambda rows: pl.BlockSpec((rows, PAIR), lambda p, s, h: (0, p))
    rel_block = pl.BlockSpec((REL // SUB, SUB, PAIR), lambda p, s, h: (0, 0, p))
    outs = pl.pallas_call(
        backward_kernel,
        grid=(PAIRS, 2, halves),
        in_specs=[
            pl.BlockSpec((None, 2, ROWS, KEYS), lambda p, s, h: (p, 0, s * halves + h, 0)),
            row, row, row, row, row, row, pair(KEYS), pair(KEYS), rel_block, pair(2), col,
            pl.BlockSpec((KEYS, 1), lambda p, s, h: (0, 0)),
        ],
        out_specs=[row, pair(KEYS), pair(KEYS), rel_block, pair(8)],
        out_shape=[
            jax.ShapeDtypeStruct((2 * SEG, D), jnp.bfloat16),
            jax.ShapeDtypeStruct((KEYS, D), jnp.bfloat16),
            jax.ShapeDtypeStruct((KEYS, D), jnp.bfloat16),
            jax.ShapeDtypeStruct((REL // SUB, SUB, D), jnp.bfloat16),
            jax.ShapeDtypeStruct((8, D), jnp.float32),
        ],
        scratch_shapes=[
            pltpu.VMEM((KEYS, 2 * PAIR), jnp.bfloat16),
            pltpu.VMEM((PAIR, KEYS), jnp.float32),
            pltpu.VMEM((PAIR, KEYS), jnp.float32),
            pltpu.VMEM((REL // SUB, PAIR, SUB), jnp.float32),
        ],
        compiler_params=pltpu.CompilerParams(
            dimension_semantics=("arbitrary",) * 3, vmem_limit_bytes=VMEM_BYTES
        ),
        name="attention_backward",
    )(prob, dmix, mix, inv, qc, qp, qs, keys, values, rel.reshape(REL // SUB, SUB, D), emb, qseg, kseg)
    return outs[0], outs[1], outs[2], outs[3].reshape(REL, D), outs[4]


norm_epsilon = 1e-06


def layer_norm(tensor, norm_gain, norm_shift):
    centred = tensor - jnp.mean(tensor, axis=-1, keepdims=True)
    variance = jnp.mean(centred * centred, axis=-1, keepdims=True)
    return centred * lax.rsqrt(variance + norm_epsilon) * norm_gain + norm_shift


def gelu_exact(tensor):
    return jax.nn.gelu(tensor, approximate=False)


def sinusoid():
    fine_count = 32
    frequency = 1.0 / 10000.0 ** (
        jnp.arange(0, D, 2, dtype=jnp.int32).astype(jnp.float32) / D
    )
    coarse = (KEYS - 1 - fine_count * jnp.arange(REL // fine_count, dtype=jnp.int32)).astype(
        jnp.float32
    )[:, None] * frequency[None]
    fine = jnp.arange(fine_count, dtype=jnp.int32).astype(jnp.float32)[:, None] * frequency[None]
    sin_coarse, cos_coarse = jnp.sin(coarse)[:, None], jnp.cos(coarse)[:, None]
    sin_fine, cos_fine = jnp.sin(fine)[None], jnp.cos(fine)[None]
    sine = sin_coarse * cos_fine - cos_coarse * sin_fine
    cosine = cos_coarse * cos_fine + sin_coarse * sin_fine
    return jnp.concatenate([sine, cosine], axis=-1).reshape(REL, D).astype(jnp.bfloat16)


def shards(
    content_in, query_in, memory, sequence_lengths, order_rank, segment_ids,
    w_query, w_key, w_value, w_out, w_rel,
    bias_content, bias_position, bias_segment, segment_embed,
    gain_one, shift_one, w_inner, bias_inner, w_outer, bias_outer, gain_two, shift_two,
    content_cotangent, query_cotangent,
):
    wide = lambda tensor: tensor.astype(jnp.float32)
    low = lambda tensor: tensor.astype(jnp.bfloat16)
    past = lax.all_to_all(memory, "mem", split_axis=0, concat_axis=1, tiled=True)[0]
    content = content_in[0]
    inputs = jnp.concatenate([content, query_in[0]], axis=0)
    cotangent = jnp.concatenate([content_cotangent[0], query_cotangent[0]], axis=0)
    segment = segment_ids[0]
    rank = order_rank[0]
    length = sequence_lengths[0]
    query_seg = jnp.concatenate([segment, segment])[:, None]
    key_seg = jnp.concatenate([jnp.zeros((MEM,), jnp.int32), segment])[:, None]
    query_rank = jnp.concatenate([rank, rank - 1])[:, None]
    key_rank = jnp.where(jnp.arange(SEG, dtype=jnp.int32) < length, rank, 2 * SEG)[None, :]

    positions = sinusoid()
    relative = low(mm(positions, w_rel, nn))
    frame = jnp.concatenate([past, content], axis=0)
    keys = low(mm(frame, w_key, nn))
    values = low(mm(frame, w_value, nn))
    projected = mm(inputs, w_query, nn)
    query_content = low(projected + wide(bias_content))
    query_position = low(projected + wide(bias_position))
    query_segment = low(projected + wide(bias_segment))
    mixture, inverse, probs = attention_forward(
        query_content, query_position, query_segment, keys, values, relative, segment_embed,
        query_seg, key_seg, query_rank, key_rank,
    )
    gain_first, shift_first = wide(gain_one), wide(shift_one)
    gain_second, shift_second = wide(gain_two), wide(shift_two)
    normed_one, norm_back_one = jax.vjp(
        layer_norm, wide(inputs) + mm(mixture, w_out, nn), gain_first, shift_first
    )
    normed_low = low(normed_one)
    activated, gelu_back = jax.vjp(gelu_exact, mm(normed_low, w_inner, nn) + wide(bias_inner))
    active_low = low(activated)
    final_out, norm_back_two = jax.vjp(
        layer_norm,
        normed_one + mm(active_low, w_outer, nn) + wide(bias_outer),
        gain_second,
        shift_second,
    )
    grad_final, grad_second_gain, grad_second_shift = norm_back_two(wide(cotangent))
    grad_outer_low = low(grad_final)
    grad_outer_bias = jnp.sum(wide(grad_outer_low), axis=0)
    grad_outer_w = low(mm(active_low, grad_outer_low, tn))
    (grad_inner_pre,) = gelu_back(mm(grad_outer_low, w_outer, nt))
    grad_inner_low = low(grad_inner_pre)
    grad_inner_bias = jnp.sum(wide(grad_inner_low), axis=0)
    grad_inner_w = low(mm(normed_low, grad_inner_low, tn))
    grad_residual, grad_first_gain, grad_first_shift = norm_back_one(
        grad_final + mm(grad_inner_low, w_inner, nt)
    )
    grad_attended = low(grad_residual)
    grad_out_w = low(mm(mixture, grad_attended, tn))
    grad_mixture = low(mm(grad_attended, w_out, nt))
    grad_projected, grad_keys, grad_values, grad_relative, small = attention_backward(
        probs, grad_mixture, mixture, inverse, query_content, query_position, query_segment,
        keys, values, relative, segment_embed, query_seg, key_seg,
    )
    grad_query_w = low(mm(inputs, grad_projected, tn))
    grad_key_w = low(mm(frame, grad_keys, tn))
    grad_value_w = low(mm(frame, grad_values, tn))
    grad_rel_w = low(mm(positions, grad_relative, tn))
    grad_inputs = grad_residual + mm(grad_projected, w_query, nt)
    grad_content = (
        grad_inputs[:SEG] + mm(grad_keys[MEM:], w_key, nt) + mm(grad_values[MEM:], w_value, nt)
    )
    both = ("batch", "mem")
    big = lax.psum(
        (grad_query_w, grad_key_w, grad_value_w, grad_out_w, grad_rel_w, grad_inner_w, grad_outer_w),
        both,
    )
    query_sum, key_sum, value_sum, out_sum, rel_sum, inner_sum, outer_sum = [wide(t) for t in big]
    vectors = jnp.concatenate(
        [
            small[:5].reshape(-1), grad_first_gain, grad_first_shift, grad_inner_bias,
            grad_outer_bias, grad_second_gain, grad_second_shift,
        ]
    )
    vectors = lax.psum(vectors, both)
    pieces = {}
    start = 0
    for name, count in (
        ("content", D), ("position", D), ("segment", D), ("embed", 2 * D), ("gain1", D),
        ("shift1", D), ("inner", bias_inner.shape[0]), ("outer", D), ("gain2", D), ("shift2", D),
    ):
        pieces[name] = vectors[start : start + count]
        start += count
    return (
        low(final_out[None, :SEG]), low(final_out[None, SEG:]),
        low(grad_content[None]), low(grad_inputs[None, SEG:]),
        query_sum, key_sum, value_sum, out_sum, rel_sum,
        pieces["content"], pieces["position"], pieces["segment"], pieces["embed"].reshape(2, D),
        pieces["gain1"], pieces["shift1"], inner_sum, pieces["inner"], outer_sum, pieces["outer"],
        pieces["gain2"], pieces["shift2"],
    )


def solution(mesh):
    both = ("batch", "mem")
    rows = P(both, None, None)
    return jax.shard_map(
        shards,
        mesh=mesh,
        in_specs=(rows, rows, P("batch", "mem", None), P(both), P(both, None), P(both, None))
        + (P(),) * 17
        + (rows, rows),
        out_specs=(rows,) * 4 + (P(),) * 17,
        check_vma=False,
    )
```

time: 1600 us -> 619 us (0.39)
  local copies, waits for them, and re-layouts: 629 us -> 23 us
  matrix products: 402 us -> 138 us
  waiting for transfers between devices: 410 us -> 209 us
  Pallas kernels: 0 us -> 140 us
  other arithmetic: 61.8 us -> 33.1 us
    dot_general x58 -> x20, matrix products: 342 us -> 138 us  [mm(): lax.dot_general(left, right, dims, preferred_element_type=jnp.float32)]
    psum x1, waiting for transfers between devices: 410 us -> 209 us  [shards(): lax.psum((grad_query_w, grad_key_w, grad_value_w, grad_out_w, grad_rel_w,...]
    unnamed x295 -> x122, local copies, waits for them, and re-layouts: 186 us -> 14.5 us
    reshape x5 -> x1, local copies, waits for them, and re-layouts: 156 us -> 0.01 us  [shards(): small[:5].reshape(-1)]
    convert_element_type x12 -> x2, local copies, waits for them, and re-layouts: 153 us -> 2.53 us  [shards(): low = lambda tensor: tensor.astype(jnp.bfloat16)]
    pallas_call x0 -> x2, Pallas kernels: none -> 140 us  [the longest x1 78 us: attention_forward(): pl.pallas_call(forward_kernel, grid=(PAIRS, 2, halves), in_specs=[row, ro...]
    slice x10 -> x4, local copies, waits for them, and re-layouts: 80.6 us -> 1.83 us  [shards(): pieces[name] = vectors[start:start + count]]
    sub x2 -> x0, matrix products: 59.7 us -> none  [stream(): grad_soft - jnp.sum(soft_again * grad_soft, axis=-1, keepdims=True)]
  transfers between devices with their start and end apart: 5 -> 2, of which waited for: 1 -> 1; matrix products, arithmetic and copies ran while one was open for 45% -> 7% of each run, Pallas kernels for 0% -> 0%
where the time goes in v1:
time: 619 us; the launch traced here: 609 us
  waiting for transfers between devices  209 us (34%)
  Pallas kernels  140 us (23%)
  matrix products  138 us (22%)
  blocking collectives  43.4 us (7%)
  other arithmetic  33.1 us (5%)
  local copies, waits for them, and re-layouts  23 us (4%)
  between operations  15.6 us (3%)
  starting transfers between devices  6.63 us (1%)
    psum x1, waiting for transfers between devices, shards(): lax.psum((grad_query_w, grad_key_w, grad_value_w, grad_out_w, grad_rel_w,...  209 us
    dot_general x20, matrix products, mm(): lax.dot_general(left, right, dims, preferred_element_type=jnp.float32)  138 us
    pallas_call x1, Pallas kernels, attention_forward(): pl.pallas_call(forward_kernel, grid=(PAIRS, 2, halves), in_specs=[row, ro...  78 us
    pallas_call x1, Pallas kernels, attention_backward(): pl.pallas_call(backward_kernel, grid=(PAIRS, 2, halves), in_specs=[pl.Blo...  62.1 us
    psum x1, blocking collectives, shards(): vectors = lax.psum(vectors, both)  43.4 us
    convert_element_type x16, other arithmetic, shards(): wide = lambda tensor: tensor.astype(jnp.float32)  21.1 us
    unnamed x122, local copies, waits for them, and re-layouts  14.5 us
  transfers between devices with their start and end apart: 2, of which 1 were waited for; matrix products, arithmetic and copies ran while one was open for 7% of the time, Pallas kernels for 0%

profile of v1, /device:TPU:0, one launch (start us, length us, event | category | flops | bytes accessed | tf_op | source)
XLA Modules:
  0.0 608.5 jit_solution(6817214205960742291)
XLA Ops:
  7.2 6.6 %all-to-all-start = ((bf16[4,96,768]{2,1,0:T(8,128)(2,1)}), bf16[4,96,768]{2,1,0:T(8,128)(2,1)S(1)}, u32[]{:S(2)}, u32[]{:S(2)}) async-start(bf16[4,96,768]{2,1,0:T(8,128)(2,1)} %param.27), calls=%async_computation | async-start | bytes 1179648 | tf_op jit(solution)/shard_map/all_to_all | solution.py:334
  29.4 5.2 convolution_convert_fusion.2
  34.7 3.8 add_convert_fusion.2
  39.5 4.2 convolution_convert_fusion.4.v_ref
  46.1 78.0 %attention_forward.1 = (bf16[1024,768]{1,0:T(8,128)(2,1)}, f32[1024,768]{1,0:T(8,128)}, bf16[6,2,1024,896]{3,2,1,0:T(8,128)(2,1)}) custom-call(bf16[1024,768]{1,0:T(8,128)(2,1)} %get-tuple-element.103.qc_ref, bf16[1024,768]{1,0:T(8,128)(2,1)} %get-tuple-element.102.qp_ref, bf16[1024,768]{1,0:T(8,128)(2,1)} %get-tuple-element.101.qs_ref, ...), custom_call_target="tpu_custom_call" | custom-call | tf_op jit(solution)/shard_map/attention_forward/pallas_call | solution.py:117
  124.1 3.7 fusion.32
  128.5 44.9 %multiply_convert_fusion = (bf16[1024,3072]{1,0:T(8,128)(2,1)S(1)}, f32[1024,3072]{1,0:T(8,128)}, f32[1024,3072]{1,0:T(8,128)}) fusion(f32[3072]{0:T(1024)S(1)} %copy-done.33, bf16[768,3072]{1,0:T(8,128)(2,1)S(1)} %bitcast.85, f32[1024,768]{0,1:T(8,128)S(1)} %get-tuple-element.123, f32[768]{0:T(1024)S(1)} %convert_element_type.177, ...), kind=kOutput, calls=%fused_computation.4 | convolution fusion | flops 5043388416 | bytes 39348224 | tf_op jit(solution)/shard_map/dot_general | solution.py:30
  173.5 6.0 fusion.33
  182.3 2.8 convert_reduce_fusion.2
  185.1 6.9 %convolution_convert_fusion = bf16[3072,768]{1,0:T(8,128)(2,1)} fusion(bf16[1024,3072]{1,0:T(8,128)(2,1)S(1)} %get-tuple-element.98, bf16[1024,768]{0,1:T(8,128)(2,1)S(1)} %get-tuple-element.95), kind=kOutput, calls=%fused_computation.18 | convolution fusion | flops 4834197504 | bytes 12582912 | tf_op jit(solution)/shard_map/dot_general | solution.py:30
  191.9 18.6 %convert_reduce_fusion = (f32[3072]{0:T(1024)S(1)}, bf16[1024,3072]{1,0:T(8,128)(2,1)}) fusion(f32[1024,3072]{1,0:T(8,128)} %get-tuple-element.99, bf16[1024,768]{0,1:T(8,128)(2,1)} %copy-done.9, bf16[3072,768]{1,0:T(8,128)(2,1)} %param.44, f32[1024,3072]{1,0:T(8,128)} %get-tuple-element.124, f32[3072]{0:T(1024)S(1)} %copy-done.33), kind=kOutput, calls=%fused_computation.2 | convolution fusion | flops 4885312512 | bytes 37773312 | tf_op jit(solution)/shard_map/dot_general | solution.py:30
  210.5 11.1 %multiply_reduce_fusion = (f32[768]{0:T(1024)S(1)}, f32[1024]{0:T(1024)S(1)}, f32[768]{0:T(1024)S(1)}, f32[1024,768]{0,1:T(8,128)S(1)}) fusion(f32[1024,768]{0,1:T(8,128)} %copy-done.1, f32[1024]{0:T(1024)S(1)} %fusion.19, f32[1024]{0:T(1024)S(1)} %broadcast_multiply_fusion.1, f32[768]{0:T(1024)S(1)} %convert_element_type.176, ...), kind=kOutput, calls=%fused_computation.31 | convolution fusion | flops 4847563776 | bytes 22061056 | tf_op jit(solution)/shard_map/dot_general | solution.py:30
  221.6 7.5 %convolution_convert_fusion.1 = bf16[768,3072]{1,0:T(8,128)(2,1)} fusion(bf16[1024,3072]{1,0:T(8,128)(2,1)S(1)} %copy-done.49, f32[1024,768]{0,1:T(8,128)S(1)} %copy-done.2, f32[768]{0:T(1024)S(1)} %convert_element_type.177, f32[768]{0:T(1024)S(1)} %convert_element_type.176, f32[1024]{0:T(1024)S(1)} %fusion.19, f32[1024]{0:T(1024)S(1)} %broadcast_multiply_fusion.1), kind=kOutput, calls=%fused_computation.19 | convolution fusion | flops 4838129664 | bytes 14170112 | tf_op jit(solution)/shard_map/dot_general | solution.py:30
  230.4 2.6 convolution_convert_fusion.3.dmix_ref
  233.1 2.5 convolution_convert_fusion.7
  235.6 62.1 %attention_backward.1 = (bf16[1024,768]{1,0:T(8,128)(2,1)}, bf16[896,768]{1,0:T(8,128)(2,1)}, bf16[896,768]{1,0:T(8,128)(2,1)}, bf16[11,128,768]{2,1,0:T(8,128)(2,1)}, f32[8,768]{1,0:T(8,128)}) custom-call(bf16[6,2,1024,896]{3,2,1,0:T(8,128)(2,1)} %get-tuple-element.30.prob_ref, bf16[1024,768]{1,0:T(8,128)(2,1)} %convolution_convert_fusion.3.dmix_ref, ...), custom_call_target="tpu_custom_call" | custom-call | tf_op jit(solution)/shard_map/attention_backward/pallas_call | solution.py:266
  297.8 4.8 convolution_convert_fusion.6
  305.0 2.4 convolution_convert_fusion.8
  310.7 43.4 %psum.61 = f32[10752]{0:T(1024)S(1)} all-reduce(f32[10752]{0:T(1024)S(1)} %constant_dynamic-update-slice_fusion), channel_id=1, replica_groups=mesh['batch'=8,'mem'=4] {'batch','mem'}, use_global_device_ids=true, to_apply=%region_19.20 | all-reduce | flops 10752 | bytes 86016 | tf_op jit(solution)/shard_map/psum | solution.py:411
  355.3 2.7 fusion.16
  358.2 3.2 add_add_fusion.3
  372.9 208.6 %all-reduce.4.cloned.1.call-done = (bf16[768,768]{1,0:T(8,128)(2,1)}, bf16[768,768]{1,0:T(8,128)(2,1)}, bf16[768,768]{1,0:T(8,128)(2,1)}, bf16[768,768]{1,0:T(8,...) async-done(((bf16[768,768]{1,0:T(8,128)(2,1)}, bf16[768,768]{1,0:T(8,128)(2,1)}, bf16[768,768]{1,0:T(8,128)(2,1)}, ...) | async-done | bytes 15335440 | tf_op jit(solution)/shard_map/psum | solution.py:400
  581.5 7.5 %convert_element_type.207 = f32[768,3072]{1,0:T(8,128)} convert(bf16[768,3072]{1,0:T(8,128)(2,1)} %get-tuple-element.92) | non-fusion elementwise | flops 2359296 | bytes 14155776 | tf_op jit(solution)/shard_map/convert_element_type | solution.py:332
  589.0 4.5 convert_element_type.209
  (180 shorter events, 49.3 us)
Async XLA Ops:
  7.2 27.5 %copy-start = (bf16[768,768]{1,0:T(8,128)(2,1)S(1)}, bf16[768,768]{1,0:T(8,128)(2,1)}, u32[]{:S(2)}) copy-start(bf16[768,768]{1,0:T(8,128)(2,1)} %param.31) | copy-start | bytes 3538948
  7.2 12.7 %copy-start.34 = (s32[1,512]{1,0:T(1,128)S(1)}, s32[1,512]{1,0:T(1,128)}, u32[]{:S(2)}) copy-start(s32[1,512]{1,0:T(1,128)} %param.30) | copy-start | bytes 6148
  7.2 12.7 %copy-start.18 = (bf16[1,512,768]{2,1,0:T(8,128)(2,1)S(1)}, bf16[1,512,768]{2,1,0:T(8,128)(2,1)}, u32[]{:S(2)}) copy-start(bf16[1,512,768]{2,1,0:T(8,128)(2,1)} %param.25) | copy-start | bytes 2359300
  7.2 13.8 %copy-start.19 = (bf16[1,512,768]{2,1,0:T(8,128)(2,1)S(1)}, bf16[1,512,768]{2,1,0:T(8,128)(2,1)}, u32[]{:S(2)}) copy-start(bf16[1,512,768]{2,1,0:T(8,128)(2,1)} %param.26) | copy-start | bytes 2359300
  7.2 31.2 %all-to-all-start = ((bf16[4,96,768]{2,1,0:T(8,128)(2,1)}), bf16[4,96,768]{2,1,0:T(8,128)(2,1)S(1)}, u32[]{:S(2)}, u32[]{:S(2)}) async-start(bf16[4,96,768]{2,1,0:T(8,128)(2,1)} %param.27), calls=%async_computation | async-start | bytes 1179648 | tf_op jit(solution)/shard_map/all_to_all | solution.py:334
  13.8 8.4 %copy-start.37 = (bf16[768]{0:T(1024)(128)(2,1)S(1)}, bf16[768]{0:T(1024)(128)(2,1)}, u32[]{:S(2)}) copy-start(bf16[768]{0:T(1024)(128)(2,1)} %param.36) | copy-start | bytes 4612
  13.8 8.4 %copy-start.38 = (bf16[768]{0:T(1024)(128)(2,1)S(1)}, bf16[768]{0:T(1024)(128)(2,1)}, u32[]{:S(2)}) copy-start(bf16[768]{0:T(1024)(128)(2,1)} %param.37) | copy-start | bytes 4612
  13.8 8.4 %copy-start.39 = (bf16[768]{0:T(1024)(128)(2,1)S(1)}, bf16[768]{0:T(1024)(128)(2,1)}, u32[]{:S(2)}) copy-start(bf16[768]{0:T(1024)(128)(2,1)} %param.38) | copy-start | bytes 4612
  13.8 567.7 %all-reduce.4.cloned.1.call-start = ((), (), s32[]{:S(2)}) async-start(), calls=%async_computation.1 | async-start | bytes 30670848 | tf_op jit(solution)/shard_map/psum | solution.py:400
  17.8 7.5 %copy-start.35 = (bf16[3072]{0:T(1024)(128)(2,1)S(1)}, bf16[3072]{0:T(1024)(128)(2,1)}, u32[]{:S(2)}) copy-start(bf16[3072]{0:T(1024)(128)(2,1)} %param.43) | copy-start | bytes 18436
  17.8 8.1 %copy-start.42 = (bf16[768]{0:T(1024)(128)(2,1)S(1)}, bf16[768]{0:T(1024)(128)(2,1)}, u32[]{:S(2)}) copy-start(bf16[768]{0:T(1024)(128)(2,1)} %param.45) | copy-start | bytes 4612
  21.1 8.3 %copy-start.43 = (bf16[768]{0:T(1024)(128)(2,1)S(1)}, bf16[768]{0:T(1024)(128)(2,1)}, u32[]{:S(2)}) copy-start(bf16[768]{0:T(1024)(128)(2,1)} %param.46) | copy-start | bytes 4612
  21.1 8.3 %copy-start.44 = (bf16[768]{0:T(1024)(128)(2,1)S(1)}, bf16[768]{0:T(1024)(128)(2,1)}, u32[]{:S(2)}) copy-start(bf16[768]{0:T(1024)(128)(2,1)} %param.47) | copy-start | bytes 4612
  124.1 49.4 %slice-start = ((s8[4718592]{0:T(1024)(128)(4,1)}), s8[4194304]{0:T(1024)(128)(4,1)S(1)}, s32[]{:S(2)}) async-start(s8[4718592]{0:T(1024)(128)(4,1)} %bitcast.82), calls=%async_computation.2 | async-start | bytes 8388608
  127.8 45.7 %copy-start.1 = (f32[1024,768]{0,1:T(8,128)}, f32[1024,768]{0,1:T(8,128)S(1)}, u32[]{:S(2)}) copy-start(f32[1024,768]{0,1:T(8,128)S(1)} %get-tuple-element.123) | copy-start | bytes 9437188
  128.2 45.3 %copy-start.30 = (f32[1024]{0:T(1024)}, f32[1024]{0:T(1024)S(1)}, u32[]{:S(2)}) copy-start(f32[1024]{0:T(1024)S(1)} %multiply_reduce_fusion.3) | copy-start | bytes 12292
  128.5 45.0 %copy-start.36 = (f32[768]{0:T(1024)S(1)}, f32[768]{0:T(1024)}, u32[]{:S(2)}) copy-start(f32[768]{0:T(1024)} %convert_element_type.181) | copy-start | bytes 9220
  128.5 45.0 %slice-start.1 = ((s8[4718592]{0:T(1024)(128)(4,1)}), s8[524288]{0:T(1024)(128)(4,1)S(1)}, s32[]{:S(2)}) async-start(s8[4718592]{0:T(1024)(128)(4,1)} %bitcast.82), calls=%async_computation.3 | async-start | bytes 1048576
  210.5 11.1 %copy-start.2 = (f32[1024,768]{0,1:T(8,128)S(1)}, f32[1024,768]{0,1:T(8,128)}, u32[]{:S(2)}) copy-start(f32[1024,768]{0,1:T(8,128)} %copy-done.1) | copy-start | bytes 9437188
  210.5 11.1 %copy-start.49 = (bf16[1024,3072]{1,0:T(8,128)(2,1)S(1)}, bf16[1024,3072]{1,0:T(8,128)(2,1)}, u32[]{:S(2)}) copy-start(bf16[1024,3072]{1,0:T(8,128)(2,1)} %get-tuple-element.129) | copy-start | bytes 18874372
  221.6 7.5 %copy-start.31 = (f32[1024]{0:T(1024)S(1)}, f32[1024]{0:T(1024)}, u32[]{:S(2)}) copy-start(f32[1024]{0:T(1024)} %copy-done.30) | copy-start | bytes 12292
  235.6 62.1 %copy-start.16 = (bf16[44,32,384]{2,1,0:T(8,128)(2,1)S(1)}, bf16[44,32,384]{2,1,0:T(8,128)(2,1)}, u32[]{:S(2)}) copy-start(bf16[44,32,384]{2,1,0:T(8,128)(2,1)} %get-tuple-element.106) | copy-start | bytes 3244036
  235.6 62.1 %copy-start.17 = (bf16[44,32,384]{2,1,0:T(8,128)(2,1)S(1)}, bf16[44,32,384]{2,1,0:T(8,128)(2,1)}, u32[]{:S(2)}) copy-start(bf16[44,32,384]{2,1,0:T(8,128)(2,1)} %get-tuple-element.107) | copy-start | bytes 3244036
  581.5 7.5 %copy-start.4 = (bf16[3072,768]{1,0:T(8,128)(2,1)S(1)}, bf16[3072,768]{1,0:T(8,128)(2,1)}, u32[]{:S(2)}) copy-start(bf16[3072,768]{1,0:T(8,128)(2,1)} %get-tuple-element.93) | copy-start | bytes 14155780
  (32 other events, 123.5 us)
Sparse Core Ops, SparseCore 0:
  310.0 271.4 all-reduce.3

commit v2 on v1

v2 whole, which is shorter than its diff:
```python
import jax
import jax.numpy as jnp
from jax import lax
from jax.experimental import pallas as pl
from jax.experimental.pallas import tpu as pltpu
from jax.sharding import PartitionSpec as P

D = 768
HEADS = 12
HEAD = 64
SEG = 512
MEM = 384
KEYS = MEM + SEG
REL = MEM + 2 * SEG
PAIR = 2 * HEAD
PAIRS = HEADS // 2
ROWS = 256
SUB = 128
CHUNK = 32
WIN = KEYS + SUB
FAR = -1e30
LOG2E = 1.4426950408889634
SCALE = HEAD**-0.5
VMEM_BYTES = 60 * 1024 * 1024
nt = (((1,), (1,)), ((), ()))
nn = (((1,), (0,)), ((), ()))
tn = (((0,), (0,)), ((), ()))


def mm(left, right, dims):
    return lax.dot_general(left, right, dims, preferred_element_type=jnp.float32)


def lane_low(rows):
    return lax.broadcasted_iota(jnp.int32, (rows, PAIR), 1) < HEAD


def tile_spans(tile):
    start = pl.multiple_of(tile * SUB, SUB)
    return [start, start + SEG]


def both_rows(ref, spans):
    return jnp.concatenate([ref[pl.ds(start, SUB), :] for start in spans], axis=0)


def forward_kernel(
    qc_ref, qp_ref, qs_ref, k_ref, v_ref, rel_ref, emb_ref, side_ref, key_side_ref, krank_ref,
    mix_ref, inv_ref, prob_ref, kcat, vcat,
):
    low_keys = lane_low(KEYS)
    same = key_side_ref[:, 0:1] == 0
    zero_row = emb_ref[0:1, :].astype(jnp.float32)
    one_row = emb_ref[1:2, :].astype(jnp.float32)
    zero_roll = pltpu.roll(zero_row, HEAD, 1)
    one_roll = pltpu.roll(one_row, HEAD, 1)
    low_row = lane_low(1)
    for head in range(2):
        if head == 0:
            near = jnp.where(low_row, zero_row, one_roll)
            away = jnp.where(low_row, one_row, zero_roll)
        else:
            near = jnp.where(low_row, zero_roll, one_row)
            away = jnp.where(low_row, one_roll, zero_row)
        kcat[head, :, :PAIR] = k_ref[...]
        kcat[head, :, PAIR:] = jnp.where(same, near, away).astype(jnp.bfloat16)
    vcat[:, :PAIR] = v_ref[...]
    vcat[:, PAIR:] = jnp.ones((KEYS, PAIR), jnp.bfloat16)

    def block(tile, carry):
        spans = tile_spans(tile)
        low = lane_low(ROWS)
        zero = jnp.zeros((ROWS, PAIR), jnp.bfloat16)
        qc = both_rows(qc_ref, spans)
        qp = both_rows(qp_ref, spans)
        qs = both_rows(qs_ref, spans)
        qs_roll = pltpu.roll(qs.astype(jnp.float32), HEAD, 1).astype(jnp.bfloat16)
        side = both_rows(side_ref, spans)
        seg_keep = (side[:, 0:1] == 0) == low
        krank = krank_ref[...]
        factor = SCALE * LOG2E
        window = rel_ref[pl.ds(3 - tile, WIN // SUB)].reshape(WIN, PAIR)
        grid = mm(
            jnp.concatenate([jnp.where(low, qp, zero), jnp.where(low, zero, qp)], axis=0), window, nt
        )
        parts = []
        for head in range(2):
            mine = low if head == 0 else ~low
            twice = jnp.where(mine, qs, qs_roll)
            qcat = jnp.concatenate(
                [jnp.where(mine, qc, zero), jnp.where(seg_keep, twice, zero)], axis=1
            )
            score = mm(qcat, kcat[head], nt)
            for row in range(0, ROWS, CHUNK):
                at = row % SUB
                shifted = pltpu.roll(
                    grid[head * ROWS + row : head * ROWS + row + CHUNK],
                    WIN - SUB + 1 + at, 1, stride=1, stride_axis=0,
                )[:, :KEYS]
                logit = score[row : row + CHUNK] + shifted
                current = jnp.where(krank <= side[row : row + CHUNK, 1:2], logit[:, MEM:], FAR)
                logit = jnp.concatenate([logit[:, :MEM], current], axis=1)
                top = jnp.max(logit, axis=-1, keepdims=True)
                soft = jnp.exp2((logit - top) * factor).astype(jnp.bfloat16)
                prob_ref[head, pl.ds(spans[row // SUB] + at, CHUNK), :] = soft
                parts.append(soft)
        summed = mm(jnp.concatenate(parts, axis=0), vcat[...], nn)
        scale = 1.0 / summed[:, PAIR:]
        mixed = summed[:, :PAIR] * scale
        mixed = jnp.where(low, mixed[:ROWS], mixed[ROWS:]).astype(jnp.bfloat16)
        scale = jnp.where(low, scale[:ROWS], scale[ROWS:])
        for index, start in enumerate(spans):
            mix_ref[pl.ds(start, SUB), :] = mixed[index * SUB : (index + 1) * SUB]
            inv_ref[pl.ds(start, SUB), :] = scale[index * SUB : (index + 1) * SUB]
        return carry

    lax.fori_loop(0, SEG // SUB, block, 0)


def whole(rows, lanes):
    return pl.BlockSpec((rows, lanes), lambda p: (0, 0))


def attention_forward(qc, qp, qs, keys, values, rel, emb, side, key_side, krank):
    pair = lambda rows: pl.BlockSpec((rows, PAIR), lambda p: (0, p))
    return pl.pallas_call(
        forward_kernel,
        grid=(PAIRS,),
        in_specs=[
            pair(2 * SEG), pair(2 * SEG), pair(2 * SEG), pair(KEYS), pair(KEYS),
            pl.BlockSpec((REL // SUB, SUB, PAIR), lambda p: (0, 0, p)),
            pair(2), whole(*side.shape), whole(*key_side.shape), whole(1, SEG),
        ],
        out_specs=[
            pair(2 * SEG), pair(2 * SEG),
            pl.BlockSpec((None, 2, 2 * SEG, KEYS), lambda p: (p, 0, 0, 0)),
        ],
        out_shape=[
            jax.ShapeDtypeStruct((2 * SEG, D), jnp.bfloat16),
            jax.ShapeDtypeStruct((2 * SEG, D), jnp.float32),
            jax.ShapeDtypeStruct((PAIRS, 2, 2 * SEG, KEYS), jnp.bfloat16),
        ],
        scratch_shapes=[
            pltpu.VMEM((2, KEYS, 2 * PAIR), jnp.bfloat16),
            pltpu.VMEM((KEYS, 2 * PAIR), jnp.bfloat16),
        ],
        compiler_params=pltpu.CompilerParams(
            dimension_semantics=("arbitrary",), vmem_limit_bytes=VMEM_BYTES
        ),
        cost_estimate=pl.CostEstimate(
            flops=30000000000, transcendentals=11000000, bytes_accessed=30000000
        ),
        name="attention_forward",
    )(qc, qp, qs, keys, values, rel.reshape(REL // SUB, SUB, D), emb, side, key_side, krank)


def backward_kernel(
    prob_ref, dmix_ref, mix_ref, inv_ref, qc_ref, qp_ref, qs_ref, k_ref, v_ref, rel_ref, emb_ref,
    side_ref, key_side_ref,
    dproj_ref, dk_ref, dv_ref, drel_ref, small_ref,
    kcat, dk_acc, dv_acc, drel_acc,
):
    kcat[:, :PAIR] = k_ref[...]
    kcat[:, PAIR:] = jnp.where((key_side_ref[:, 0:1] == 0) == lane_low(KEYS), 1.0, 0.0).astype(
        jnp.bfloat16
    )
    dk_acc[...] = jnp.zeros_like(dk_acc)
    dv_acc[...] = jnp.zeros_like(dv_acc)
    drel_acc[...] = jnp.zeros_like(drel_acc)
    small_ref[...] = jnp.zeros_like(small_ref)

    def block(tile, carry):
        spans = tile_spans(tile)
        low = lane_low(ROWS)
        zero = jnp.zeros((ROWS, PAIR), jnp.bfloat16)
        row_index = lax.broadcasted_iota(jnp.int32, (ROWS, ROWS), 0)
        column_index = lax.broadcasted_iota(jnp.int32, (ROWS, ROWS), 1)
        flip = jnp.where(
            (row_index // SUB == column_index // SUB)
            & (row_index % SUB + column_index % SUB == SUB - 1),
            1.0, 0.0,
        ).astype(jnp.bfloat16)
        dmix = (
            both_rows(dmix_ref, spans).astype(jnp.float32) * (both_rows(inv_ref, spans) * SCALE)
        ).astype(jnp.bfloat16)
        weighted = dmix.astype(jnp.float32) * both_rows(mix_ref, spans).astype(jnp.float32)
        qc = both_rows(qc_ref, spans)
        qp = both_rows(qp_ref, spans)
        qs = both_rows(qs_ref, spans).astype(jnp.float32)
        qp_turned = mm(flip, qp, nn).astype(jnp.bfloat16)
        first = both_rows(side_ref, spans)[:, 0:1] == 0
        emb = emb_ref[...].astype(jnp.float32)
        dm = jnp.concatenate([jnp.where(low, dmix, zero), jnp.where(low, zero, dmix)], axis=0)
        qc_both = jnp.concatenate([jnp.where(low, qc, zero), jnp.where(low, zero, qc)], axis=0)
        qp_both = jnp.concatenate(
            [jnp.where(low, qp_turned, zero), jnp.where(low, zero, qp_turned)], axis=0
        )
        row_sum = jnp.concatenate(
            [
                jnp.sum(jnp.where(low, weighted, 0.0), axis=-1, keepdims=True),
                jnp.sum(jnp.where(low, 0.0, weighted), axis=-1, keepdims=True),
            ],
            axis=0,
        )
        prob = jnp.concatenate([both_rows(prob_ref.at[head], spans) for head in range(2)], axis=0)
        dprob = mm(dm, v_ref[...], nt)
        total = jnp.concatenate(
            [
                (
                    prob[at : at + CHUNK].astype(jnp.float32)
                    * (dprob[at : at + CHUNK] - row_sum[at : at + CHUNK])
                ).astype(jnp.bfloat16)
                for at in range(0, 2 * ROWS, CHUNK)
            ],
            axis=0,
        )
        back = mm(total, kcat[...], nn)
        turned = [mm(flip, total[head * ROWS : (head + 1) * ROWS], nn) for head in range(2)]
        grid = jnp.concatenate(
            [
                pltpu.roll(
                    jnp.concatenate(
                        [turned[head][row : row + CHUNK], jnp.zeros((CHUNK, SUB), jnp.float32)],
                        axis=1,
                    ),
                    row % SUB, 1, stride=1, stride_axis=0,
                ).astype(jnp.bfloat16)
                for head in range(2)
                for row in range(0, ROWS, CHUNK)
            ],
            axis=0,
        )
        window = rel_ref[pl.ds(3 - tile, WIN // SUB)].reshape(WIN, PAIR)
        dqp = mm(grid, window, nn)
        dqp = jnp.where(low, dqp[:ROWS], dqp[ROWS:]).astype(jnp.bfloat16)
        dqp_wide = mm(flip, dqp, nn)
        dv_acc[...] += mm(dm, prob, tn)
        dk_acc[...] += mm(qc_both, total, tn)
        drel = mm(qp_both, grid, tn)
        for part in range(WIN // SUB):
            drel_acc[3 - tile + part] += drel[:, part * SUB : (part + 1) * SUB]
        dqc_wide = (
            jnp.where(low, back[:ROWS, :PAIR], back[ROWS:, :PAIR])
            .astype(jnp.bfloat16)
            .astype(jnp.float32)
        )
        sums = [back[head * ROWS : (head + 1) * ROWS, PAIR:] for head in range(2)]
        rolled = [pltpu.roll(part, HEAD, 1) for part in sums]
        key_zero = jnp.where(low, sums[0], rolled[1])
        key_one = jnp.where(low, rolled[0], sums[1])
        near = jnp.where(first, key_zero, key_one)
        other = jnp.where(first, key_one, key_zero)
        dqs_wide = (near * emb[0:1] + other * emb[1:2]).astype(jnp.bfloat16).astype(jnp.float32)
        dproj = (dqc_wide + dqp_wide + dqs_wide).astype(jnp.bfloat16)
        for index, start in enumerate(spans):
            dproj_ref[pl.ds(start, SUB), :] = dproj[index * SUB : (index + 1) * SUB]
        rows = [dqc_wide, dqp_wide, dqs_wide, near * qs, other * qs]
        for row, value in enumerate(rows):
            small_ref[row : row + 1, :] += jnp.sum(value, axis=0, keepdims=True)
        return carry

    lax.fori_loop(0, SEG // SUB, block, 0)
    dk_ref[...] = dk_acc[...].T.astype(jnp.bfloat16)
    dv_ref[...] = (dv_acc[...].T * (1.0 / SCALE)).astype(jnp.bfloat16)
    for part in range(REL // SUB):
        drel_ref[part] = drel_acc[part].T.astype(jnp.bfloat16)


def attention_backward(
    base, pairs, prob, dmix, mix, inv, qc, qp, qs, keys, values, rel, emb, side, key_side
):
    pair = lambda rows: pl.BlockSpec((rows, PAIR), lambda p: (0, base + p))
    pair_out = lambda rows: pl.BlockSpec((rows, PAIR), lambda p: (0, p))
    rel_block = pl.BlockSpec((REL // SUB, SUB, PAIR), lambda p: (0, 0, base + p))
    lanes = pairs * PAIR
    outs = pl.pallas_call(
        backward_kernel,
        grid=(pairs,),
        in_specs=[
            pl.BlockSpec((None, 2, 2 * SEG, KEYS), lambda p: (base + p, 0, 0, 0)),
            pair(2 * SEG), pair(2 * SEG), pair(2 * SEG), pair(2 * SEG), pair(2 * SEG), pair(2 * SEG),
            pair(KEYS), pair(KEYS), rel_block, pair(2), whole(*side.shape), whole(*key_side.shape),
        ],
        out_specs=[
            pair_out(2 * SEG), pair_out(KEYS), pair_out(KEYS),
            pl.BlockSpec((REL // SUB, SUB, PAIR), lambda p: (0, 0, p)), pair_out(8),
        ],
        out_shape=[
            jax.ShapeDtypeStruct((2 * SEG, lanes), jnp.bfloat16),
            jax.ShapeDtypeStruct((KEYS, lanes), jnp.bfloat16),
            jax.ShapeDtypeStruct((KEYS, lanes), jnp.bfloat16),
            jax.ShapeDtypeStruct((REL // SUB, SUB, lanes), jnp.bfloat16),
            jax.ShapeDtypeStruct((8, lanes), jnp.float32),
        ],
        scratch_shapes=[
            pltpu.VMEM((KEYS, 2 * PAIR), jnp.bfloat16),
            pltpu.VMEM((PAIR, KEYS), jnp.float32),
            pltpu.VMEM((PAIR, KEYS), jnp.float32),
            pltpu.VMEM((REL // SUB, PAIR, SUB), jnp.float32),
        ],
        compiler_params=pltpu.CompilerParams(
            dimension_semantics=("arbitrary",), vmem_limit_bytes=VMEM_BYTES
        ),
        cost_estimate=pl.CostEstimate(
            flops=pairs * 7000000000, transcendentals=0, bytes_accessed=pairs * 6000000
        ),
        name="attention_backward",
    )(
        prob, dmix, mix, inv, qc, qp, qs, keys, values, rel.reshape(REL // SUB, SUB, D), emb, side,
        key_side,
    )
    return outs[0], outs[1], outs[2], outs[3].reshape(REL, lanes), outs[4]


norm_epsilon = 1e-06
TOKENS = 256
FF_CHUNK = 768
half_erfc = (0.5 * 0.254829592, 0.5 * -0.284496736, 0.5 * 1.421413741, 0.5 * -1.453152027, 0.5 * 1.061405429)


def gelu_pair(x):
    gauss = jnp.exp2(x * x * (-0.5 * LOG2E))
    t = 1.0 / (1.0 + (0.3275911 * 0.7071067811865476) * jnp.abs(x))
    a1, a2, a3, a4, a5 = half_erfc
    tail = t * (a1 + t * (a2 + t * (a3 + t * (a4 + t * a5)))) * gauss
    cdf = jnp.where(x >= 0.0, 1.0 - tail, tail)
    return x * cdf, cdf + x * gauss * 0.3989422804014327


def normalise(tensor):
    centred = tensor - jnp.mean(tensor, axis=-1, keepdims=True)
    inverse = lax.rsqrt(jnp.mean(centred * centred, axis=-1, keepdims=True) + norm_epsilon)
    return centred * inverse, inverse


def norm_back(grad, hat, inverse):
    return inverse * (
        grad
        - jnp.mean(grad, axis=-1, keepdims=True)
        - hat * jnp.mean(grad * hat, axis=-1, keepdims=True)
    )


def token_kernel(
    x_ref, mix_ref, cot_ref, wo_ref, wi_ref, wf_ref, bias_inner_ref, rows_ref,
    final_ref, active_ref, outer_ref, inner_ref, attended_ref, dmix_ref, low_ref, residual_ref,
    sums_ref, inner_sum_ref,
    slope,
):
    @pl.when(pl.program_id(0) == 0)
    def _():
        sums_ref[...] = jnp.zeros_like(sums_ref)
        inner_sum_ref[...] = jnp.zeros_like(inner_sum_ref)

    gain_one, shift_one = rows_ref[0:1, :], rows_ref[1:2, :]
    gain_two, shift_two = rows_ref[2:3, :], rows_ref[3:4, :]
    bias_outer = rows_ref[4:5, :]
    hat_one, inverse_one = normalise(
        x_ref[...].astype(jnp.float32) + mm(mix_ref[...], wo_ref[...], nn)
    )
    normed = hat_one * gain_one + shift_one
    normed_low = normed.astype(jnp.bfloat16)
    low_ref[...] = normed_low
    chunks = [slice(at, at + FF_CHUNK) for at in range(0, wi_ref.shape[1], FF_CHUNK)]
    pre = mm(normed_low, wi_ref[:, chunks[0]], nn)
    total = normed + bias_outer
    for index, chunk in enumerate(chunks):
        here = pre + bias_inner_ref[:, chunk]
        if index + 1 < len(chunks):
            pre = mm(normed_low, wi_ref[:, chunks[index + 1]], nn)
        value, derivative = gelu_pair(here)
        value = value.astype(jnp.bfloat16)
        active_ref[:, chunk] = value
        slope[:, chunk] = derivative
        total = total + mm(value, wf_ref[chunk, :], nn)
    hat_two, inverse_two = normalise(total)
    final_ref[...] = (hat_two * gain_two + shift_two).astype(jnp.bfloat16)
    cot = cot_ref[...].astype(jnp.float32)
    grad_total = norm_back(cot * gain_two, hat_two, inverse_two)
    grad_outer = grad_total.astype(jnp.bfloat16)
    outer_ref[...] = grad_outer
    sums_ref[2:3, :] += jnp.sum(cot * hat_two, axis=0, keepdims=True)
    sums_ref[3:4, :] += jnp.sum(cot, axis=0, keepdims=True)
    sums_ref[4:5, :] += jnp.sum(grad_outer.astype(jnp.float32), axis=0, keepdims=True)
    back = mm(grad_outer, wf_ref[chunks[0], :], nt)
    for index, chunk in enumerate(chunks):
        here = back
        if index + 1 < len(chunks):
            back = mm(grad_outer, wf_ref[chunks[index + 1], :], nt)
        grad_inner = (here * slope[:, chunk]).astype(jnp.bfloat16)
        inner_ref[:, chunk] = grad_inner
        inner_sum_ref[:, chunk] += jnp.sum(grad_inner.astype(jnp.float32), axis=0, keepdims=True)
        grad_total = grad_total + mm(grad_inner, wi_ref[:, chunk], nt)
    sums_ref[0:1, :] += jnp.sum(grad_total * hat_one, axis=0, keepdims=True)
    sums_ref[1:2, :] += jnp.sum(grad_total, axis=0, keepdims=True)
    residual = norm_back(grad_total * gain_one, hat_one, inverse_one)
    residual_ref[...] = residual
    attended = residual.astype(jnp.bfloat16)
    attended_ref[...] = attended
    dmix_ref[...] = mm(attended, wo_ref[...], nt).astype(jnp.bfloat16)


def token_layer(x, mix, cot, w_out, w_inner, w_outer, bias_inner, rows):
    count = x.shape[0]
    hidden = w_inner.shape[1]
    tile = lambda lanes: pl.BlockSpec((TOKENS, lanes), lambda i: (i, 0))
    once = lambda a, b: pl.BlockSpec((a, b), lambda i: (0, 0), pipeline_mode=pl.Buffered(1))
    sums = lambda a, b: pl.BlockSpec((a, b), lambda i: (0, 0))
    low = lambda lanes: jax.ShapeDtypeStruct((count, lanes), jnp.bfloat16)
    return pl.pallas_call(
        token_kernel,
        grid=(count // TOKENS,),
        in_specs=[
            tile(D), tile(D), tile(D), once(D, D), once(D, hidden), once(hidden, D),
            once(1, hidden), once(8, D),
        ],
        out_specs=[
            tile(D), tile(hidden), tile(D), tile(hidden), tile(D), tile(D), tile(D), tile(D),
            sums(8, D), sums(1, hidden),
        ],
        out_shape=[
            low(D), low(hidden), low(D), low(hidden), low(D), low(D), low(D),
            jax.ShapeDtypeStruct((count, D), jnp.float32),
            jax.ShapeDtypeStruct((8, D), jnp.float32),
            jax.ShapeDtypeStruct((1, hidden), jnp.float32),
        ],
        scratch_shapes=[pltpu.VMEM((TOKENS, hidden), jnp.float32)],
        compiler_params=pltpu.CompilerParams(
            dimension_semantics=("arbitrary",), vmem_limit_bytes=VMEM_BYTES
        ),
        cost_estimate=pl.CostEstimate(
            flops=22000000000, transcendentals=6000000, bytes_accessed=40000000
        ),
        name="token_layer",
    )(x, mix, cot, w_out, w_inner, w_outer, bias_inner, rows)


def chip_bits():
    bits = []
    bit = 2
    while bit < lax.axis_size("batch"):
        bits.append(bit)
        bit *= 2
    return bits


def digit(bit):
    return lax.axis_index("batch") // bit % 2


def across(tensor, bit):
    count = lax.axis_size("batch")
    return lax.ppermute(tensor, "batch", [(i, i ^ bit) for i in range(count)])


def along(tensor, shift):
    ring = lax.axis_size("mem")
    return lax.ppermute(tensor, "mem", [(i, (i + shift) % ring) for i in range(ring)])


def rows_of(tensor, start, count):
    return lax.dynamic_slice(tensor, (start, 0), (count, tensor.shape[1]))


class Sum:
    def __init__(self, tensor, order):
        bits = chip_bits()
        self.bits = [1] + (bits if order == 0 else bits[::-1])
        self.state = tensor
        self.at = 0
        self.stages = 2 * len(self.bits) + 2

    def step(self):
        count, tensor = len(self.bits), self.state
        ring, me = lax.axis_size("mem"), lax.axis_index("mem")
        if self.at < count:
            bit = self.bits[self.at]
            half = tensor.shape[0] // 2
            mine = digit(bit)
            got = across(rows_of(tensor, (1 - mine) * half, half), bit)
            kept = rows_of(tensor, mine * half, half)
            self.state = (kept.astype(jnp.float32) + got.astype(jnp.float32)).astype(jnp.bfloat16)
        elif self.at == count:
            block = tensor.shape[0] // ring
            total = rows_of(tensor, me * block, block).astype(jnp.float32)
            for shift in range(1, ring):
                sent = rows_of(tensor, (me + shift) % ring * block, block)
                total = total + along(sent, shift).astype(jnp.float32)
            self.state = total.astype(jnp.bfloat16)
        elif self.at == count + 1:
            parts = [tensor] + [along(tensor, shift) for shift in range(1, ring)]
            self.state = jnp.concatenate(parts, axis=0)
        else:
            bit = self.bits[2 * count + 1 - self.at]
            self.state = jnp.concatenate([tensor, across(tensor, bit)], axis=0)
        self.at += 1

    def places(self):
        ring = lax.axis_size("mem")
        weight = ring * lax.axis_size("batch") // 2
        index = jnp.arange(2 * weight, dtype=jnp.int32)
        place = (lax.axis_index("mem") - index % ring) % ring
        for bit in self.bits:
            place = place + (index // weight % 2 + digit(bit)) % 2 * weight
            weight //= 2
        return place


class Small:
    def __init__(self, tensor):
        self.state = tensor
        self.at = 0
        self.bits = [1] + chip_bits()
        self.mem_bits = []
        bit = 1
        while bit < lax.axis_size("mem"):
            self.mem_bits.append(bit)
            bit *= 2
        self.stages = len(self.bits) + len(self.mem_bits)

    def step(self):
        ring = lax.axis_size("mem")
        if self.at < len(self.bits):
            got = across(self.state, self.bits[self.at])
        else:
            bit = self.mem_bits[self.at - len(self.bits)]
            got = lax.ppermute(self.state, "mem", [(i, i ^ bit) for i in range(ring)])
        self.state = self.state + got
        self.at += 1


def together(active, tree):
    states, tree = lax.optimization_barrier(([item.state for item in active], tree))
    for item, state in zip(active, states):
        item.state = state
    return tree


def step_all(active):
    for item in active:
        if item.at < item.stages:
            item.step()


def settle_kernel(place_ref, in_ref, out_ref):
    rows = in_ref.shape[0] // place_ref.shape[0]
    per_step = out_ref.shape[0] // rows
    for item in range(per_step):
        start = pl.multiple_of(place_ref[pl.program_id(0) * per_step + item] * rows, 8)
        out_ref[item * rows : (item + 1) * rows, :] = in_ref[pl.ds(start, rows), :].astype(jnp.float32)


def settle(item):
    tensor, place = item.state, item.places()
    blocks = place.shape[0]
    rows, lanes = tensor.shape
    if rows // blocks % 8:
        return tensor.reshape(blocks, -1, lanes)[place].reshape(rows, lanes).astype(jnp.float32)
    steps = 4
    return pl.pallas_call(
        settle_kernel,
        grid_spec=pltpu.PrefetchScalarGridSpec(
            num_scalar_prefetch=1,
            grid=(steps,),
            in_specs=[pl.BlockSpec((rows, lanes), lambda i, p: (0, 0))],
            out_specs=pl.BlockSpec((rows // steps, lanes), lambda i, p: (i, 0)),
        ),
        out_shape=jax.ShapeDtypeStruct((rows, lanes), jnp.float32),
        compiler_params=pltpu.CompilerParams(vmem_limit_bytes=48 * 1024 * 1024),
        name="settle",
    )(place, tensor)


def sinusoid():
    fine_count = 32
    frequency = 1.0 / 10000.0 ** (
        jnp.arange(0, D, 2, dtype=jnp.int32).astype(jnp.float32) / D
    )
    coarse = (KEYS - 1 - fine_count * jnp.arange(REL // fine_count, dtype=jnp.int32)).astype(
        jnp.float32
    )[:, None] * frequency[None]
    fine = jnp.arange(fine_count, dtype=jnp.int32).astype(jnp.float32)[:, None] * frequency[None]
    sin_coarse, cos_coarse = jnp.sin(coarse)[:, None], jnp.cos(coarse)[:, None]
    sin_fine, cos_fine = jnp.sin(fine)[None], jnp.cos(fine)[None]
    sine = sin_coarse * cos_fine - cos_coarse * sin_fine
    cosine = cos_coarse * cos_fine + sin_coarse * sin_fine
    return jnp.concatenate([sine, cosine], axis=-1).reshape(REL, D).astype(jnp.bfloat16)


def shards(
    content_in, query_in, memory, sequence_lengths, order_rank, segment_ids,
    w_query, w_key, w_value, w_out, w_rel,
    bias_content, bias_position, bias_segment, segment_embed,
    gain_one, shift_one, w_inner, bias_inner, w_outer, bias_outer, gain_two, shift_two,
    content_cotangent, query_cotangent,
):
    wide = lambda tensor: tensor.astype(jnp.float32)
    low = lambda tensor: tensor.astype(jnp.bfloat16)
    both = ("batch", "mem")
    past = lax.all_to_all(memory, "mem", split_axis=0, concat_axis=1, tiled=True)[0]
    content = content_in[0]
    inputs = jnp.concatenate([content, query_in[0]], axis=0)
    cotangent = jnp.concatenate([content_cotangent[0], query_cotangent[0]], axis=0)
    segment = segment_ids[0]
    rank = order_rank[0]
    zeros = jnp.zeros((2 * SEG, 6), jnp.int32)
    side = jnp.concatenate(
        [
            jnp.concatenate([segment, segment])[:, None],
            jnp.concatenate([rank, rank - 1])[:, None],
            zeros,
        ],
        axis=1,
    )
    key_side = jnp.concatenate([jnp.zeros((MEM, 8), jnp.int32), side[:SEG]], axis=0)
    live = jnp.arange(SEG, dtype=jnp.int32) < sequence_lengths[0]
    key_rank = jnp.where(live, rank, 2 * SEG)[None, :]

    positions = sinusoid()
    relative = low(mm(positions, w_rel, nn))
    frame = jnp.concatenate([past, content], axis=0)
    keys = low(mm(frame, w_key, nn))
    values = low(mm(frame, w_value, nn))
    projected = mm(inputs, w_query, nn)
    query_content = low(projected + wide(bias_content))
    query_position = low(projected + wide(bias_position))
    query_segment = low(projected + wide(bias_segment))
    mixture, inverse, probs = attention_forward(
        query_content, query_position, query_segment, keys, values, relative, segment_embed,
        side, key_side, key_rank,
    )
    rows = jnp.stack(
        [wide(t) for t in (gain_one, shift_one, gain_two, shift_two, bias_outer)]
        + [jnp.zeros((D,), jnp.float32)] * 3
    )
    (
        final_out, active_low, grad_outer_low, grad_inner_low, grad_attended, grad_mixture,
        normed_low, grad_residual, token_sums, inner_bias_sum,
    ) = token_layer(
        inputs, mixture, cotangent, w_out, w_inner, w_outer, wide(bias_inner)[None], rows
    )
    grad_outer_w = low(mm(active_low, grad_outer_low, tn))
    grad_inner_w = low(mm(normed_low, grad_inner_low, tn))
    grad_mixture, grad_outer_w, grad_inner_w = lax.optimization_barrier(
        (grad_mixture, grad_outer_w, grad_inner_w)
    )
    outer_sum, inner_sum = [wide(t) for t in lax.psum((grad_outer_w, grad_inner_w), both)]
    grad_projected, grad_keys, grad_values, grad_relative, small = attention_backward(
        0, PAIRS, probs, grad_mixture, mixture, inverse, query_content, query_position,
        query_segment, keys, values, relative, segment_embed, side, key_side,
    )
    sums = [
        Sum(low(mm(left, right, tn)), order)
        for left, right, order in (
            (mixture, grad_attended, 0), (inputs, grad_projected, 1), (frame, grad_keys, 0),
            (frame, grad_values, 1), (positions, grad_relative, 0),
        )
    ]
    vectors = Small(
        jnp.concatenate([small[:5], token_sums[:5], inner_bias_sum.reshape(-1, D),
                         jnp.zeros((2, D), jnp.float32)], axis=0)
    )
    for item in sums + [vectors]:
        while item.at < item.stages:
            item.step()
    out_sum, query_sum, key_sum, value_sum, rel_sum = [settle(item) for item in sums]
    grad_inputs = grad_residual + mm(grad_projected, w_query, nt)
    grad_content = (
        grad_inputs[:SEG] + mm(grad_keys[MEM:], w_key, nt) + mm(grad_values[MEM:], w_value, nt)
    )
    vectors = vectors.state
    names = ("content", "position", "segment", "embed0", "embed1", "gain1", "shift1", "gain2", "shift2", "outer")
    pieces = {name: vectors[index] for index, name in enumerate(names)}
    pieces["embed"] = vectors[3:5]
    pieces["inner"] = vectors[10:14].reshape(-1)
    return (
        low(final_out[None, :SEG]), low(final_out[None, SEG:]),
        low(grad_content[None]), low(grad_inputs[None, SEG:]),
        query_sum, key_sum, value_sum, out_sum, rel_sum,
        pieces["content"], pieces["position"], pieces["segment"], pieces["embed"].reshape(2, D),
        pieces["gain1"], pieces["shift1"], inner_sum, pieces["inner"], outer_sum, pieces["outer"],
        pieces["gain2"], pieces["shift2"],
    )


def solution(mesh):
    both = ("batch", "mem")
    rows = P(both, None, None)
    return jax.shard_map(
        shards,
        mesh=mesh,
        in_specs=(rows, rows, P("batch", "mem", None), P(both), P(both, None), P(both, None))
        + (P(),) * 17
        + (rows, rows),
        out_specs=(rows,) * 4 + (P(),) * 17,
        check_vma=False,
    )
```

time: 619 us -> 489 us (0.79)
  waiting for transfers between devices: 209 us -> 104 us
  matrix products: 138 us -> 48.3 us
  starting transfers between devices: 6.63 us -> 93.3 us
  blocking collectives: 43.4 us -> 0 us
  Pallas kernels: 140 us -> 175 us
  local copies, waits for them, and re-layouts: 23 us -> 15.5 us
    psum x1, waiting for transfers between devices: 209 us -> 60.2 us  [shards(): lax.psum((grad_outer_w, grad_inner_w), both)]
    dot_general x20 -> x14, matrix products: 138 us -> 48.3 us  [mm(): lax.dot_general(left, right, dims, preferred_element_type=jnp.float32)]
    ppermute x0 -> x65, starting transfers between devices: none -> 86.8 us  [the longest x30 51.9 us: along(): lax.ppermute(tensor, 'mem', [(i, (i + shift) % ring) for i in range(ring)])]
    ppermute x0 -> x65, waiting for transfers between devices: none -> 43.7 us  [the longest x33 41.1 us: across(): return lax.ppermute(tensor, 'batch', [(i, i ^ bit) for i in range(count)])]
    psum x1 -> x0, blocking collectives: 43.4 us -> none  [shards(): vectors = lax.psum(vectors, both)]
    pallas_call x2 -> x8, Pallas kernels: 140 us -> 175 us  [the longest x1 69.6 us: attention_backward(): pl.pallas_call(backward_kernel, grid=(pairs,), in_specs=[pl.BlockSpec((No...]
    unnamed x122 -> x127, local copies, waits for them, and re-layouts: 14.5 us -> 1.27 us
    convert_element_type x16 -> x5, other arithmetic: 21.1 us -> 12 us  [shards(): wide = lambda tensor: tensor.astype(jnp.float32)]
  transfers between devices with their start and end apart: 2 -> 67, of which waited for: 1 -> 14; matrix products, arithmetic and copies ran while one was open for 7% -> 10% of each run, Pallas kernels for 0% -> 3%
where the time goes in v2:
time: 489 us; the launch traced here: 483 us
  Pallas kernels  175 us (36%)
  waiting for transfers between devices  104 us (21%)
  starting transfers between devices  93.3 us (19%)
  matrix products  48.3 us (10%)
  other arithmetic  31.1 us (6%)
  between operations  16.4 us (3%)
  local copies, waits for them, and re-layouts  15.5 us (3%)
    pallas_call x1, Pallas kernels, attention_backward(): pl.pallas_call(backward_kernel, grid=(pairs,), in_specs=[pl.BlockSpec((No...  69.6 us
    psum x1, waiting for transfers between devices, shards(): lax.psum((grad_outer_w, grad_inner_w), both)  60.2 us
    ppermute x30, starting transfers between devices, along(): lax.ppermute(tensor, 'mem', [(i, (i + shift) % ring) for i in range(ring)])  51.9 us
    pallas_call x1, Pallas kernels, attention_forward(): pl.pallas_call(forward_kernel, grid=(PAIRS,), in_specs=[pair(2 * SEG), pa...  51 us
    dot_general x14, matrix products, mm(): lax.dot_general(left, right, dims, preferred_element_type=jnp.float32)  48.3 us
    pallas_call x1, Pallas kernels, token_layer(): pl.pallas_call(token_kernel, grid=(count // TOKENS,), in_specs=[tile(D),...  41.6 us
    ppermute x33, waiting for transfers between devices, across(): return lax.ppermute(tensor, 'batch', [(i, i ^ bit) for i in range(count)])  41.1 us
    ppermute x33, starting transfers between devices, across(): return lax.ppermute(tensor, 'batch', [(i, i ^ bit) for i in range(count)])  29.9 us
  transfers between devices with their start and end apart: 67, of which 14 were waited for; matrix products, arithmetic and copies ran while one was open for 10% of the time, Pallas kernels for 3%

profile of v2, /device:TPU:0, one launch (start us, length us, event | category | flops | bytes accessed | tf_op | source)
XLA Modules:
  0.0 483.0 jit_solution(13785727646637192882)
XLA Ops:
  7.2 6.5 %all-to-all-start = ((bf16[4,96,768]{2,1,0:T(8,128)(2,1)}), bf16[4,96,768]{2,1,0:T(8,128)(2,1)S(1)}, u32[]{:S(2)}, u32[]{:S(2)}) async-start(bf16[4,96,768]{2,1,0:T(8,128)(2,1)} %param.27), calls=%async_computation | async-start | bytes 1179648 | tf_op jit(solution)/shard_map/all_to_all | solution.py:600
  17.6 4.1 pad_maximum_fusion.1
  24.4 4.9 %convolution_convert_fusion.2 = bf16[1408,768]{1,0:T(8,128)(2,1)} fusion(bf16[768,768]{1,0:T(8,128)(2,1)} %param.35, bf16[1408,384]{1,0:T(8,128)(2,1)} %bitcast.46, bf16[1408,384]{1,0:T(8,128)(2,1)S(1)} %bitcast.44), kind=kOutput, calls=%fused_computation.2 | convolution fusion | flops 1666351104 | bytes 5505024 | tf_op jit(solution)/shard_map/dot_general | solution.py:31
  29.4 3.7 add_convert_fusion
  33.1 3.7 convolution_convert_fusion.3.v_ref
  39.2 51.0 %attention_forward.1 = (bf16[1024,768]{1,0:T(8,128)(2,1)}, f32[1024,768]{1,0:T(8,128)}, bf16[6,2,1024,896]{3,2,1,0:T(8,128)(2,1)}) custom-call(bf16[1024,768]{1,0:T(8,128)(2,1)} %get-tuple-element.85.qc_ref, bf16[1024,768]{1,0:T(8,128)(2,1)} %get-tuple-element.84.qp_ref, bf16[1024,768]{1,0:T(8,128)(2,1)} %get-tuple-element.83.qs_ref, ...), custom_call_target="tpu_custom_call" | custom-call | flops 30000001024 | bytes 30000000 | tf_op jit(solution)/shard_map/attention_forward/pallas_call | solution.py:126
  90.1 41.6 %token_layer.1 = (bf16[1024,768]{1,0:T(8,128)(2,1)}, bf16[1024,3072]{1,0:T(8,128)(2,1)}, bf16[1024,768]{1,0:T(8,128)(2,1)}, bf16[1024,3072]{1,0:T(8,128)(2,1)}, ...) custom-call(bf16[1024,768]{1,0:T(8,128)(2,1)} %get-tuple-element.193, ...), custom_call_target="tpu_custom_call" | custom-call | flops 22000001024 | bytes 40000000 | tf_op jit(solution)/shard_map/token_layer/pallas_call | solution.py:410
  131.8 9.9 %convolution_convert_fusion = bf16[768,3072]{1,0:T(8,128)(2,1)} fusion(bf16[1024,768]{1,0:T(8,128)(2,1)} %get-tuple-element.49, bf16[1024,3072]{1,0:T(8,128)(2,1)} %get-tuple-element.50), kind=kOutput, calls=%fused_computation | convolution fusion | flops 4834197504 | bytes 12582912 | tf_op jit(solution)/shard_map/dot_general | solution.py:31
  141.7 6.9 %convolution_convert_fusion.1 = bf16[3072,768]{1,0:T(8,128)(2,1)} fusion(bf16[1024,3072]{1,0:T(8,128)(2,1)S(1)} %copy-done.49, bf16[1024,768]{1,0:T(8,128)(2,1)S(1)} %copy-done.50), kind=kOutput, calls=%fused_computation.1 | convolution fusion | flops 4834197504 | bytes 12582912 | tf_op jit(solution)/shard_map/dot_general | solution.py:31
  148.6 69.6 %attention_backward.1 = (bf16[1024,768]{1,0:T(8,128)(2,1)}, bf16[896,768]{1,0:T(8,128)(2,1)}, bf16[896,768]{1,0:T(8,128)(2,1)}, bf16[11,128,768]{2,1,0:T(8,128)(2,1)}, f32[8,768]{1,0:T(8,128)}) custom-call(bf16[6,2,1024,896]{3,2,1,0:T(8,128)(2,1)} %get-tuple-element.45.prob_ref, bf16[1024,768]{1,0:T(8,128)(2,1)} %get-tuple-element.51.dmix_ref, ...), custom_call_target="tpu_custom_call" | custom-call | flops 41999998976 | bytes 36000000 | tf_op jit(solution)/shard_map/attention_backward/pallas_call | solution.py:276
  218.3 4.0 convolution_convert_fusion.8
  227.8 4.5 convolution_convert_fusion.5
  278.9 4.9 %collective-permute-done.49 = bf16[192,768]{1,0:T(8,128)(2,1)S(1)} collective-permute-done((bf16[192,768]{1,0:T(8,128)(2,1)S(1)}, bf16[192,768]{1,0:T(8,128)(2,1)S(1)}, u32[]{:S(2)}, u32[]{:S(2)}) %collective-permute-start.49) | collective-permute-done | bytes 294944 | tf_op jit(solution)/shard_map/ppermute | solution.py:453
  285.5 10.9 %collective-permute-done.37 = bf16[192,768]{1,0:T(8,128)(2,1)S(1)} collective-permute-done((bf16[192,768]{1,0:T(8,128)(2,1)S(1)}, bf16[192,768]{1,0:T(8,128)(2,1)S(1)}, u32[]{:S(2)}, u32[]{:S(2)}) %collective-permute-start.37) | collective-permute-done | bytes 294944 | tf_op jit(solution)/shard_map/ppermute | solution.py:453
  299.8 6.3 %collective-permute-done.13 = bf16[192,768]{1,0:T(8,128)(2,1)S(1)} collective-permute-done((bf16[192,768]{1,0:T(8,128)(2,1)S(1)}, bf16[192,768]{1,0:T(8,128)(2,1)S(1)}, u32[]{:S(2)}, u32[]{:S(2)}) %collective-permute-start.13) | collective-permute-done | bytes 294944 | tf_op jit(solution)/shard_map/ppermute | solution.py:453
  329.3 5.0 %collective-permute-start.4 = (bf16[24,768]{1,0:T(8,128)(2,1)S(1)}, bf16[24,768]{1,0:T(8,128)(2,1)S(1)}, u32[]{:S(2)}, u32[]{:S(2)}) collective-permute-start(bf16[24,768]{1,0:T(8,128)(2,1)S(1)} %get-tuple-element.129), channel_id=1, source_target_pairs={{0,2},{1,3},{2,0},{3,1},{4,6},{5,7},{6,4},{7,5},{8,10},{9,11},{10,... | collective-permute-start | bytes 110600 | tf_op jit(solution)/shard_map/ppermute | solution.py:458
  339.3 3.3 collective-permute-start.56
  342.8 3.7 collective-permute-start.43
  348.9 3.2 collective-permute-start.32
  381.7 4.8 collective-permute-done.46
  386.6 3.0 collective-permute-done.22
  403.7 60.2 %all-reduce.4.cloned.1.call-done = (bf16[768,3072]{1,0:T(8,128)(2,1)}, bf16[3072,768]{1,0:T(8,128)(2,1)}) async-done(((bf16[768,3072]{1,0:T(8,128)(2,1)}, bf16[3072,768]{1,0:T(8,128)(2,1)}), (bf16[768,3072]{1,0:T(8,128)(2,1)}, bf16[3072,768]{1,0:T(8,128)(2,1)})) %all-reduce.4.cloned.1.call-update) | async-done | bytes 9437200 | tf_op jit(solution)/shard_map/psum | solution.py:647
  463.9 7.5 %convert_element_type.400 = f32[768,3072]{1,0:T(8,128)} convert(bf16[768,3072]{1,0:T(8,128)(2,1)} %get-tuple-element.71) | non-fusion elementwise | flops 2359296 | bytes 14155776 | tf_op jit(solution)/shard_map/convert_element_type | solution.py:597
  471.4 4.5 convert_element_type.401
  (361 shorter events, 139.1 us)
Async XLA Ops:
  7.2 25.8 %all-to-all-start = ((bf16[4,96,768]{2,1,0:T(8,128)(2,1)}), bf16[4,96,768]{2,1,0:T(8,128)(2,1)S(1)}, u32[]{:S(2)}, u32[]{:S(2)}) async-start(bf16[4,96,768]{2,1,0:T(8,128)(2,1)} %param.27), calls=%async_computation | async-start | bytes 1179648 | tf_op jit(solution)/shard_map/all_to_all | solution.py:600
  13.7 450.2 %all-reduce.4.cloned.1.call-start = ((), (), s32[]{:S(2)}) async-start(), calls=%async_computation.1 | async-start | bytes 18874368 | tf_op jit(solution)/shard_map/psum | solution.py:647
  227.7 16.6 %collective-permute-start.60 = (f32[16,768]{1,0:T(8,128)S(1)}, f32[16,768]{1,0:T(8,128)S(1)}, u32[]{:S(2)}, u32[]{:S(2)}) collective-permute-start(f32[16,768]{1,0:T(8,128)S(1)} %pad_maximum_fusion.11), channel_id=1, source_target_pairs={{0,4},{4,0},{8,12},{12,8},{16,20},{20,16},{24,28},{28,24},{1,5},{5... | collective-permute-start | bytes 147464 | tf_op jit(solution)/shard_map/ppermute | solution.py:453
  233.2 32.9 %collective-permute-start.48 = (bf16[384,768]{1,0:T(8,128)(2,1)}, bf16[384,768]{1,0:T(8,128)(2,1)}, u32[]{:S(2)}, u32[]{:S(2)}) collective-permute-start(bf16[384,768]{1,0:T(8,128)(2,1)} %constant_dynamic-slice_fusion.5), channel_id=1, source_target_pairs={{0,4},{4,0},{8,12},{12,8},{16,20},{20,16},{24,28},{28,24},{1,5},{5... | collective-permute-start | bytes 1769480 | tf_op jit(solution)/shard_map/ppermute | solution.py:453
  237.6 33.6 %collective-permute-start.24 = (bf16[384,768]{1,0:T(8,128)(2,1)}, bf16[384,768]{1,0:T(8,128)(2,1)}, u32[]{:S(2)}, u32[]{:S(2)}) collective-permute-start(bf16[384,768]{1,0:T(8,128)(2,1)} %constant_dynamic-slice_fusion.17), channel_id=1, source_target_pairs={{0,4},{4,0},{8,12},{12,8},{16,20},{20,16},{24,28},{28,24},{1,5},{5... | collective-permute-start | bytes 1769480 | tf_op jit(solution)/shard_map/ppermute | solution.py:453
  238.5 35.7 %collective-permute-start.12 = (bf16[384,768]{1,0:T(8,128)(2,1)}, bf16[384,768]{1,0:T(8,128)(2,1)}, u32[]{:S(2)}, u32[]{:S(2)}) collective-permute-start(bf16[384,768]{1,0:T(8,128)(2,1)} %constant_dynamic-slice_fusion.23), channel_id=1, source_target_pairs={{0,4},{4,0},{8,12},{12,8},{16,20},{20,16},{24,28},{28,24},{1,5},{5... | collective-permute-start | bytes 1769480 | tf_op jit(solution)/shard_map/ppermute | solution.py:453
  251.0 18.2 %collective-permute-start.36 = (bf16[384,768]{1,0:T(8,128)(2,1)}, bf16[384,768]{1,0:T(8,128)(2,1)}, u32[]{:S(2)}, u32[]{:S(2)}) collective-permute-start(bf16[384,768]{1,0:T(8,128)(2,1)} %constant_dynamic-slice_fusion.11), channel_id=1, source_target_pairs={{0,4},{4,0},{8,12},{12,8},{16,20},{20,16},{24,28},{28,24},{1,5},{5... | collective-permute-start | bytes 1769480 | tf_op jit(solution)/shard_map/ppermute | solution.py:453
  262.8 14.2 %collective-permute-start = (bf16[384,768]{1,0:T(8,128)(2,1)}, bf16[384,768]{1,0:T(8,128)(2,1)}, u32[]{:S(2)}, u32[]{:S(2)}) collective-permute-start(bf16[384,768]{1,0:T(8,128)(2,1)} %constant_dynamic-slice_fusion.29), channel_id=1, source_target_pairs={{0,4},{4,0},{8,12},{12,8},{16,20},{20,16},{24,28},{28,24},{1,5},{5... | collective-permute-start | bytes 1769480 | tf_op jit(solution)/shard_map/ppermute | solution.py:453
  267.5 16.2 %collective-permute-start.49 = (bf16[192,768]{1,0:T(8,128)(2,1)S(1)}, bf16[192,768]{1,0:T(8,128)(2,1)S(1)}, u32[]{:S(2)}, u32[]{:S(2)}) collective-permute-start(bf16[192,768]{1,0:T(8,128)(2,1)S(1)} %constant_dynamic-slice_fusion.4), channel_id=1, source_target_pairs={{0,8},{4,12},{8,0},{12,4},{16,24},{20,28},{24,16},{28,20},{1,9},{5... | collective-permute-start | bytes 884744 | tf_op jit(solution)/shard_map/ppermute | solution.py:453
  270.4 25.9 %collective-permute-start.37 = (bf16[192,768]{1,0:T(8,128)(2,1)S(1)}, bf16[192,768]{1,0:T(8,128)(2,1)S(1)}, u32[]{:S(2)}, u32[]{:S(2)}) collective-permute-start(bf16[192,768]{1,0:T(8,128)(2,1)S(1)} %constant_dynamic-slice_fusion.10), channel_id=1, source_target_pairs={{0,8},{4,12},{8,0},{12,4},{16,24},{20,28},{24,16},{28,20},{1,9},{5... | collective-permute-start | bytes 884744 | tf_op jit(solution)/shard_map/ppermute | solution.py:453
  272.5 25.7 %collective-permute-start.25 = (bf16[192,768]{1,0:T(8,128)(2,1)S(1)}, bf16[192,768]{1,0:T(8,128)(2,1)S(1)}, u32[]{:S(2)}, u32[]{:S(2)}) collective-permute-start(bf16[192,768]{1,0:T(8,128)(2,1)S(1)} %constant_dynamic-slice_fusion.16), channel_id=1, source_target_pairs={{0,16},{4,20},{8,24},{12,28},{16,0},{20,4},{24,8},{28,12},{1,17},{... | collective-permute-start | bytes 884744 | tf_op jit(solution)/shard_map/ppermute | solution.py:453
  275.4 30.7 %collective-permute-start.13 = (bf16[192,768]{1,0:T(8,128)(2,1)S(1)}, bf16[192,768]{1,0:T(8,128)(2,1)S(1)}, u32[]{:S(2)}, u32[]{:S(2)}) collective-permute-start(bf16[192,768]{1,0:T(8,128)(2,1)S(1)} %constant_dynamic-slice_fusion.22), channel_id=1, source_target_pairs={{0,8},{4,12},{8,0},{12,4},{16,24},{20,28},{24,16},{28,20},{1,9},{5... | collective-permute-start | bytes 884744 | tf_op jit(solution)/shard_map/ppermute | solution.py:453
  278.3 29.5 %collective-permute-start.1 = (bf16[192,768]{1,0:T(8,128)(2,1)S(1)}, bf16[192,768]{1,0:T(8,128)(2,1)S(1)}, u32[]{:S(2)}, u32[]{:S(2)}) collective-permute-start(bf16[192,768]{1,0:T(8,128)(2,1)S(1)} %constant_dynamic-slice_fusion.28), channel_id=1, source_target_pairs={{0,16},{4,20},{8,24},{12,28},{16,0},{20,4},{24,8},{28,12},{1,17},{... | collective-permute-start | bytes 884744 | tf_op jit(solution)/shard_map/ppermute | solution.py:453
  283.8 24.7 %collective-permute-start.50 = (bf16[96,768]{1,0:T(8,128)(2,1)S(1)}, bf16[96,768]{1,0:T(8,128)(2,1)S(1)}, u32[]{:S(2)}, u32[]{:S(2)}) collective-permute-start(bf16[96,768]{1,0:T(8,128)(2,1)S(1)} %constant_dynamic-slice_fusion.3), channel_id=1, source_target_pairs={{0,16},{4,20},{8,24},{12,28},{16,0},{20,4},{24,8},{28,12},{1,17},{... | collective-permute-start | bytes 442376 | tf_op jit(solution)/shard_map/ppermute | solution.py:453
  296.5 13.6 %collective-permute-start.38 = (bf16[96,768]{1,0:T(8,128)(2,1)S(1)}, bf16[96,768]{1,0:T(8,128)(2,1)S(1)}, u32[]{:S(2)}, u32[]{:S(2)}) collective-permute-start(bf16[96,768]{1,0:T(8,128)(2,1)S(1)} %constant_dynamic-slice_fusion.9), channel_id=1, source_target_pairs={{0,16},{4,20},{8,24},{12,28},{16,0},{20,4},{24,8},{28,12},{1,17},{... | collective-permute-start | bytes 442376 | tf_op jit(solution)/shard_map/ppermute | solution.py:453
  298.3 17.1 %collective-permute-start.26 = (bf16[96,768]{1,0:T(8,128)(2,1)S(1)}, bf16[96,768]{1,0:T(8,128)(2,1)S(1)}, u32[]{:S(2)}, u32[]{:S(2)}) collective-permute-start(bf16[96,768]{1,0:T(8,128)(2,1)S(1)} %constant_dynamic-slice_fusion.15), channel_id=1, source_target_pairs={{0,8},{4,12},{8,0},{12,4},{16,24},{20,28},{24,16},{28,20},{1,9},{5... | collective-permute-start | bytes 442376 | tf_op jit(solution)/shard_map/ppermute | solution.py:453
  329.3 13.6 %collective-permute-start.4 = (bf16[24,768]{1,0:T(8,128)(2,1)S(1)}, bf16[24,768]{1,0:T(8,128)(2,1)S(1)}, u32[]{:S(2)}, u32[]{:S(2)}) collective-permute-start(bf16[24,768]{1,0:T(8,128)(2,1)S(1)} %get-tuple-element.129), channel_id=1, source_target_pairs={{0,2},{1,3},{2,0},{3,1},{4,6},{5,7},{6,4},{7,5},{8,10},{9,11},{10,... | collective-permute-start | bytes 110600 | tf_op jit(solution)/shard_map/ppermute | solution.py:458
  336.4 11.8 %collective-permute-start.55 = (bf16[24,768]{1,0:T(8,128)(2,1)S(1)}, bf16[24,768]{1,0:T(8,128)(2,1)S(1)}, u32[]{:S(2)}, u32[]{:S(2)}) collective-permute-start(bf16[24,768]{1,0:T(8,128)(2,1)S(1)} %get-tuple-element.74), channel_id=1, source_target_pairs={{0,2},{1,3},{2,0},{3,1},{4,6},{5,7},{6,4},{7,5},{8,10},{9,11},{10,... | collective-permute-start | bytes 110600 | tf_op jit(solution)/shard_map/ppermute | solution.py:458
  363.8 12.4 %collective-permute-start.21 = (bf16[96,768]{1,0:T(8,128)(2,1)S(1)}, bf16[96,768]{1,0:T(8,128)(2,1)S(1)}, u32[]{:S(2)}, u32[]{:S(2)}) collective-permute-start(bf16[96,768]{1,0:T(8,128)(2,1)S(1)} %pad_maximum_fusion.7), channel_id=1, source_target_pairs={{0,16},{4,20},{8,24},{12,28},{16,0},{20,4},{24,8},{28,12},{1,17},{... | collective-permute-start | bytes 442376 | tf_op jit(solution)/shard_map/ppermute | solution.py:453
  368.1 13.4 %collective-permute-start.58 = (bf16[192,768]{1,0:T(8,128)(2,1)S(1)}, bf16[192,768]{1,0:T(8,128)(2,1)S(1)}, u32[]{:S(2)}, u32[]{:S(2)}) collective-permute-start(bf16[192,768]{1,0:T(8,128)(2,1)S(1)} %get-tuple-element.102), channel_id=1, source_target_pairs={{0,8},{4,12},{8,0},{12,4},{16,24},{20,28},{24,16},{28,20},{1,9},{5... | collective-permute-start | bytes 884744 | tf_op jit(solution)/shard_map/ppermute | solution.py:453
  370.9 15.5 %collective-permute-start.46 = (bf16[192,768]{1,0:T(8,128)(2,1)S(1)}, bf16[192,768]{1,0:T(8,128)(2,1)S(1)}, u32[]{:S(2)}, u32[]{:S(2)}) collective-permute-start(bf16[192,768]{1,0:T(8,128)(2,1)S(1)} %get-tuple-element.108), channel_id=1, source_target_pairs={{0,8},{4,12},{8,0},{12,4},{16,24},{20,28},{24,16},{28,20},{1,9},{5... | collective-permute-start | bytes 884744 | tf_op jit(solution)/shard_map/ppermute | solution.py:453
  371.0 18.7 %collective-permute-start.34 = (bf16[192,768]{1,0:T(8,128)(2,1)S(1)}, bf16[192,768]{1,0:T(8,128)(2,1)S(1)}, u32[]{:S(2)}, u32[]{:S(2)}) collective-permute-start(bf16[192,768]{1,0:T(8,128)(2,1)S(1)} %get-tuple-element.114), channel_id=1, source_target_pairs={{0,16},{4,20},{8,24},{12,28},{16,0},{20,4},{24,8},{28,12},{1,17},{... | collective-permute-start | bytes 884744 | tf_op jit(solution)/shard_map/ppermute | solution.py:453
  376.2 13.4 %collective-permute-start.22 = (bf16[192,768]{1,0:T(8,128)(2,1)S(1)}, bf16[192,768]{1,0:T(8,128)(2,1)S(1)}, u32[]{:S(2)}, u32[]{:S(2)}) collective-permute-start(bf16[192,768]{1,0:T(8,128)(2,1)S(1)} %get-tuple-element.120), channel_id=1, source_target_pairs={{0,8},{4,12},{8,0},{12,4},{16,24},{20,28},{24,16},{28,20},{1,9},{5... | collective-permute-start | bytes 884744 | tf_op jit(solution)/shard_map/ppermute | solution.py:453
  376.3 14.1 %collective-permute-start.10 = (bf16[192,768]{1,0:T(8,128)(2,1)S(1)}, bf16[192,768]{1,0:T(8,128)(2,1)S(1)}, u32[]{:S(2)}, u32[]{:S(2)}) collective-permute-start(bf16[192,768]{1,0:T(8,128)(2,1)S(1)} %get-tuple-element.126), channel_id=1, source_target_pairs={{0,16},{4,20},{8,24},{12,28},{16,0},{20,4},{24,8},{28,12},{1,17},{... | collective-permute-start | bytes 884744 | tf_op jit(solution)/shard_map/ppermute | solution.py:453
  (94 other events, 721.8 us)
Sparse Core Ops, SparseCore 0:
  261.4 202.4 all-reduce.3

commit v3 on v2

--- a/solution.py
+++ b/solution.py
@@ -156,10 +156,9 @@
 
 def backward_kernel(
     prob_ref, dmix_ref, mix_ref, inv_ref, qc_ref, qp_ref, qs_ref, k_ref, v_ref, rel_ref, emb_ref,
-    side_ref, key_side_ref,
-    dproj_ref, dk_ref, dv_ref, drel_ref, small_ref,
-    kcat, dk_acc, dv_acc, drel_acc,
+    side_ref, key_side_ref, inputs_ref, frame_ref, positions_ref, *rest,
 ):
+    dproj_ref, dk_ref, dv_ref, small_ref, bucket_ref, kcat, dk_acc, dv_acc, drel_acc = rest[-9:]
     kcat[:, :PAIR] = k_ref[...]
     kcat[:, PAIR:] = jnp.where((key_side_ref[:, 0:1] == 0) == lane_low(KEYS), 1.0, 0.0).astype(
         jnp.bfloat16
@@ -259,38 +258,51 @@
             small_ref[row : row + 1, :] += jnp.sum(value, axis=0, keepdims=True)
         return carry
 
-    lax.fori_loop(0, SEG // SUB, block, 0)
-    dk_ref[...] = dk_acc[...].T.astype(jnp.bfloat16)
-    dv_ref[...] = (dv_acc[...].T * (1.0 / SCALE)).astype(jnp.bfloat16)
-    for part in range(REL // SUB):
-        drel_ref[part] = drel_acc[part].T.astype(jnp.bfloat16)
+    lax.fori_loop(0, SEG // SUB, block, 0, unroll=True)
+    dk_low = dk_acc[...].astype(jnp.bfloat16)
+    dv_low = (dv_acc[...] * (1.0 / SCALE)).astype(jnp.bfloat16)
+    dk_ref[...] = dk_low.T
+    dv_ref[...] = dv_low.T
+    drel_low = jnp.concatenate(
+        [drel_acc[part] for part in range(REL // SUB)], axis=1
+    ).astype(jnp.bfloat16)
+    grads = (
+        mm(dproj_ref[...], inputs_ref[...], tn), mm(dk_low, frame_ref[...], nn),
+        mm(dv_low, frame_ref[...], nn), mm(drel_low, positions_ref[...], nn),
+    )
+    for index, grad in enumerate(grads):
+        bucket_ref[index * PAIR : (index + 1) * PAIR, :] = grad.astype(jnp.bfloat16)
 
 
 def attention_backward(
-    base, pairs, prob, dmix, mix, inv, qc, qp, qs, keys, values, rel, emb, side, key_side
+    first, count, bucket_block, chain, prob, dmix, mix, inv, qc, qp, qs, keys, values, rel, emb, side,
+    key_side, inputs, frame, positions,
 ):
-    pair = lambda rows: pl.BlockSpec((rows, PAIR), lambda p: (0, base + p))
-    pair_out = lambda rows: pl.BlockSpec((rows, PAIR), lambda p: (0, p))
-    rel_block = pl.BlockSpec((REL // SUB, SUB, PAIR), lambda p: (0, 0, base + p))
-    lanes = pairs * PAIR
-    outs = pl.pallas_call(
+    pair = lambda rows: pl.BlockSpec((rows, PAIR), lambda p: (0, first + p))
+    rel_block = pl.BlockSpec((REL // SUB, SUB, PAIR), lambda p: (0, 0, first + p))
+    bucket_rows = chain[4] if isinstance(chain[4], int) else chain[4].shape[0]
+    passed = [item for item in chain if not isinstance(item, int) and item is not None]
+    places = [at for at, item in enumerate(chain) if not isinstance(item, int) and item is not None]
+    return pl.pallas_call(
         backward_kernel,
-        grid=(pairs,),
+        grid=(count,),
         in_specs=[
-            pl.BlockSpec((None, 2, 2 * SEG, KEYS), lambda p: (base + p, 0, 0, 0)),
+            pl.BlockSpec((None, 2, 2 * SEG, KEYS), lambda p: (first + p, 0, 0, 0)),
             pair(2 * SEG), pair(2 * SEG), pair(2 * SEG), pair(2 * SEG), pair(2 * SEG), pair(2 * SEG),
             pair(KEYS), pair(KEYS), rel_block, pair(2), whole(*side.shape), whole(*key_side.shape),
-        ],
+            whole(2 * SEG, D), whole(KEYS, D), whole(REL, D),
+        ]
+        + [pl.BlockSpec(memory_space=pl.ANY)] * len(passed),
         out_specs=[
-            pair_out(2 * SEG), pair_out(KEYS), pair_out(KEYS),
-            pl.BlockSpec((REL // SUB, SUB, PAIR), lambda p: (0, 0, p)), pair_out(8),
+            pair(2 * SEG), pair(KEYS), pair(KEYS), pair(8),
+            pl.BlockSpec((4 * PAIR, D), lambda p: (bucket_block + p, 0)),
         ],
         out_shape=[
-            jax.ShapeDtypeStruct((2 * SEG, lanes), jnp.bfloat16),
-            jax.ShapeDtypeStruct((KEYS, lanes), jnp.bfloat16),
-            jax.ShapeDtypeStruct((KEYS, lanes), jnp.bfloat16),
-            jax.ShapeDtypeStruct((REL // SUB, SUB, lanes), jnp.bfloat16),
-            jax.ShapeDtypeStruct((8, lanes), jnp.float32),
+            jax.ShapeDtypeStruct((2 * SEG, D), jnp.bfloat16),
+            jax.ShapeDtypeStruct((KEYS, D), jnp.bfloat16),
+            jax.ShapeDtypeStruct((KEYS, D), jnp.bfloat16),
+            jax.ShapeDtypeStruct((8, D), jnp.float32),
+            jax.ShapeDtypeStruct((bucket_rows, D), jnp.bfloat16),
         ],
         scratch_shapes=[
             pltpu.VMEM((KEYS, 2 * PAIR), jnp.bfloat16),
@@ -298,18 +310,18 @@
             pltpu.VMEM((PAIR, KEYS), jnp.float32),
             pltpu.VMEM((REL // SUB, PAIR, SUB), jnp.float32),
         ],
+        input_output_aliases={16 + index: at for index, at in enumerate(places)},
         compiler_params=pltpu.CompilerParams(
             dimension_semantics=("arbitrary",), vmem_limit_bytes=VMEM_BYTES
         ),
         cost_estimate=pl.CostEstimate(
-            flops=pairs * 7000000000, transcendentals=0, bytes_accessed=pairs * 6000000
+            flops=count * 8000000000, transcendentals=0, bytes_accessed=count * 8000000
         ),
         name="attention_backward",
     )(
         prob, dmix, mix, inv, qc, qp, qs, keys, values, rel.reshape(REL // SUB, SUB, D), emb, side,
-        key_side,
-    )
-    return outs[0], outs[1], outs[2], outs[3].reshape(REL, lanes), outs[4]
+        key_side, inputs, frame, positions, *passed,
+    )
 
 
 norm_epsilon = 1e-06
@@ -448,9 +460,13 @@
     return lax.axis_index("batch") // bit % 2
 
 
-def across(tensor, bit):
+def across(tensor, bits):
     count = lax.axis_size("batch")
-    return lax.ppermute(tensor, "batch", [(i, i ^ bit) for i in range(count)])
+    return lax.ppermute(tensor, "batch", [(i, i ^ bits[i & 1]) for i in range(count)])
+
+
+def own_digit(bits):
+    return jnp.where(digit(1) == 1, digit(bits[1]), digit(bits[0]))
 
 
 def along(tensor, shift):
@@ -463,9 +479,9 @@
 
 
 class Sum:
-    def __init__(self, tensor, order):
+    def __init__(self, tensor):
         bits = chip_bits()
-        self.bits = [1] + (bits if order == 0 else bits[::-1])
+        self.bits = [(1, 1)] + list(zip(bits, bits[::-1]))
         self.state = tensor
         self.at = 0
         self.stages = 2 * len(self.bits) + 2
@@ -476,7 +492,7 @@
         if self.at < count:
             bit = self.bits[self.at]
             half = tensor.shape[0] // 2
-            mine = digit(bit)
+            mine = own_digit(bit)
             got = across(rows_of(tensor, (1 - mine) * half, half), bit)
             kept = rows_of(tensor, mine * half, half)
             self.state = (kept.astype(jnp.float32) + got.astype(jnp.float32)).astype(jnp.bfloat16)
@@ -500,74 +516,64 @@
         weight = ring * lax.axis_size("batch") // 2
         index = jnp.arange(2 * weight, dtype=jnp.int32)
         place = (lax.axis_index("mem") - index % ring) % ring
-        for bit in self.bits:
-            place = place + (index // weight % 2 + digit(bit)) % 2 * weight
+        core = index // weight % 2
+        for even, odd in self.bits:
+            own = jnp.where(core == 1, digit(odd), digit(even))
+            place = place + (index // weight % 2 + own) % 2 * weight
             weight //= 2
         return place
 
 
-class Small:
-    def __init__(self, tensor):
-        self.state = tensor
-        self.at = 0
-        self.bits = [1] + chip_bits()
-        self.mem_bits = []
-        bit = 1
-        while bit < lax.axis_size("mem"):
-            self.mem_bits.append(bit)
-            bit *= 2
-        self.stages = len(self.bits) + len(self.mem_bits)
-
-    def step(self):
-        ring = lax.axis_size("mem")
-        if self.at < len(self.bits):
-            got = across(self.state, self.bits[self.at])
-        else:
-            bit = self.mem_bits[self.at - len(self.bits)]
-            got = lax.ppermute(self.state, "mem", [(i, i ^ bit) for i in range(ring)])
-        self.state = self.state + got
-        self.at += 1
-
-
-def together(active, tree):
-    states, tree = lax.optimization_barrier(([item.state for item in active], tree))
-    for item, state in zip(active, states):
-        item.state = state
-    return tree
-
-
-def step_all(active):
-    for item in active:
-        if item.at < item.stages:
-            item.step()
-
-
-def settle_kernel(place_ref, in_ref, out_ref):
-    rows = in_ref.shape[0] // place_ref.shape[0]
-    per_step = out_ref.shape[0] // rows
-    for item in range(per_step):
-        start = pl.multiple_of(place_ref[pl.program_id(0) * per_step + item] * rows, 8)
-        out_ref[item * rows : (item + 1) * rows, :] = in_ref[pl.ds(start, rows), :].astype(jnp.float32)
-
-
-def settle(item):
+def placed(item):
     tensor, place = item.state, item.places()
     blocks = place.shape[0]
+    if tensor.shape[0] // blocks % 8:
+        tensor = tensor.reshape(blocks, -1, tensor.shape[1])[place].reshape(tensor.shape)
+        place = jnp.arange(8, dtype=jnp.int32)
+    return tensor, place
+
+
+def block_of(place_ref, in_ref, index):
+    rows = in_ref.shape[0] // place_ref.shape[0]
+    start = pl.multiple_of(place_ref[index] * rows, 8)
+    return in_ref[pl.ds(start, rows), :].astype(jnp.float32)
+
+
+def settle_pairs_kernel(place_ref, in_ref, *rest):
+    outs, full = rest[:-1], rest[-1]
+    rows = in_ref.shape[0] // place_ref.shape[0]
+    grads = PAIRS * 4 * PAIR
+
+    @pl.when(pl.program_id(0) == 0)
+    def _():
+        for item in range(place_ref.shape[0]):
+            full[item * rows : (item + 1) * rows, :] = block_of(place_ref, in_ref, item)
+        outs[4][...] = full[grads : grads + D, :]
+        outs[5][...] = full[grads + D : grads + D + outs[5].shape[0], :]
+
+    for index in range(4):
+        start = pl.multiple_of((pl.program_id(0) * 4 + index) * PAIR, PAIR)
+        outs[index][...] = full[pl.ds(start, PAIR), :].T
+
+
+def settle_pairs(item):
+    tensor, place = placed(item)
     rows, lanes = tensor.shape
-    if rows // blocks % 8:
-        return tensor.reshape(blocks, -1, lanes)[place].reshape(rows, lanes).astype(jnp.float32)
-    steps = 4
+    square = jax.ShapeDtypeStruct((D, D), jnp.float32)
+    whole_out = lambda count: pl.BlockSpec((count, lanes), lambda i, p: (0, 0))
     return pl.pallas_call(
-        settle_kernel,
+        settle_pairs_kernel,
         grid_spec=pltpu.PrefetchScalarGridSpec(
             num_scalar_prefetch=1,
-            grid=(steps,),
+            grid=(PAIRS,),
             in_specs=[pl.BlockSpec((rows, lanes), lambda i, p: (0, 0))],
-            out_specs=pl.BlockSpec((rows // steps, lanes), lambda i, p: (i, 0)),
+            out_specs=[pl.BlockSpec((lanes, PAIR), lambda i, p: (0, i))] * 4
+            + [whole_out(D), whole_out(VECTORS)],
+            scratch_shapes=[pltpu.VMEM((rows, lanes), jnp.float32)],
         ),
-        out_shape=jax.ShapeDtypeStruct((rows, lanes), jnp.float32),
+        out_shape=[square] * 5 + [jax.ShapeDtypeStruct((VECTORS, lanes), jnp.float32)],
         compiler_params=pltpu.CompilerParams(vmem_limit_bytes=48 * 1024 * 1024),
-        name="settle",
+        name="settle_pairs",
     )(place, tensor)
 
 
@@ -585,6 +591,87 @@
     sine = sin_coarse * cos_fine - cos_coarse * sin_fine
     cosine = cos_coarse * cos_fine + sin_coarse * sin_fine
     return jnp.concatenate([sine, cosine], axis=-1).reshape(REL, D).astype(jnp.bfloat16)
+
+
+EXTRA = 256
+VECTORS = 24
+
+
+WIDE = 512
+
+
+def wide_grads_kernel(outer_ref, active_ref, low_ref, inner_ref, out_ref, left):
+    part = pl.program_id(0)
+
+    @pl.when(pl.program_id(1) == 0)
+    def _():
+        @pl.when(part == 0)
+        def _():
+            left[...] = outer_ref[...].T
+
+        @pl.when(part == 1)
+        def _():
+            left[...] = low_ref[...].T
+
+    @pl.when(part == 0)
+    def _():
+        out_ref[...] = mm(left[...], active_ref[...], nn).astype(jnp.bfloat16)
+
+    @pl.when(part == 1)
+    def _():
+        out_ref[...] = mm(left[...], inner_ref[...], nn).astype(jnp.bfloat16)
+
+
+def wide_grads(grad_outer, active, normed_low, grad_inner):
+    tokens, hidden = active.shape
+    steps = hidden // WIDE
+    return pl.pallas_call(
+        wide_grads_kernel,
+        grid=(2, steps),
+        in_specs=[
+            pl.BlockSpec((tokens, D), lambda p, i: (0, 0)),
+            pl.BlockSpec((tokens, WIDE), lambda p, i: (0, jnp.where(p == 0, i, steps - 1))),
+            pl.BlockSpec((tokens, D), lambda p, i: (0, 0)),
+            pl.BlockSpec((tokens, WIDE), lambda p, i: (0, jnp.where(p == 0, 0, i))),
+        ],
+        out_specs=pl.BlockSpec((D, WIDE), lambda p, i: (p, i)),
+        out_shape=jax.ShapeDtypeStruct((2 * D, hidden), jnp.bfloat16),
+        scratch_shapes=[pltpu.VMEM((D, tokens), jnp.bfloat16)],
+        compiler_params=pltpu.CompilerParams(
+            dimension_semantics=("arbitrary",) * 2, vmem_limit_bytes=VMEM_BYTES
+        ),
+        cost_estimate=pl.CostEstimate(
+            flops=9700000000, transcendentals=0, bytes_accessed=25000000
+        ),
+        name="wide_grads",
+    )(grad_outer, active, normed_low, grad_inner)
+
+
+def widen_kernel(outer_ref, inner_ref, outer_out, inner_out):
+    outer_out[...] = outer_ref[...].astype(jnp.float32).T
+    inner_out[...] = inner_ref[...].astype(jnp.float32)
+
+
+def widen(summed):
+    hidden = summed.shape[1]
+    return pl.pallas_call(
+        widen_kernel,
+        grid=(hidden // WIDE,),
+        in_specs=[
+            pl.BlockSpec((D, WIDE), lambda i: (0, i)),
+            pl.BlockSpec((D, WIDE), lambda i: (1, i)),
+        ],
+        out_specs=[
+            pl.BlockSpec((WIDE, D), lambda i: (i, 0)),
+            pl.BlockSpec((D, WIDE), lambda i: (0, i)),
+        ],
+        out_shape=[
+            jax.ShapeDtypeStruct((hidden, D), jnp.float32),
+            jax.ShapeDtypeStruct((D, hidden), jnp.float32),
+        ],
+        compiler_params=pltpu.CompilerParams(vmem_limit_bytes=VMEM_BYTES),
+        name="widen",
+    )(summed, summed)
 
 
 def shards(
@@ -639,43 +726,62 @@
     ) = token_layer(
         inputs, mixture, cotangent, w_out, w_inner, w_outer, wide(bias_inner)[None], rows
     )
-    grad_outer_w = low(mm(active_low, grad_outer_low, tn))
-    grad_inner_w = low(mm(normed_low, grad_inner_low, tn))
-    grad_mixture, grad_outer_w, grad_inner_w = lax.optimization_barrier(
-        (grad_mixture, grad_outer_w, grad_inner_w)
-    )
-    outer_sum, inner_sum = [wide(t) for t in lax.psum((grad_outer_w, grad_inner_w), both)]
-    grad_projected, grad_keys, grad_values, grad_relative, small = attention_backward(
-        0, PAIRS, probs, grad_mixture, mixture, inverse, query_content, query_position,
-        query_segment, keys, values, relative, segment_embed, side, key_side,
-    )
-    sums = [
-        Sum(low(mm(left, right, tn)), order)
-        for left, right, order in (
-            (mixture, grad_attended, 0), (inputs, grad_projected, 1), (frame, grad_keys, 0),
-            (frame, grad_values, 1), (positions, grad_relative, 0),
+    low_mm = lambda left, right: low(mm(left, right, tn))
+    wide_sum = wide_grads(grad_outer_low, active_low, normed_low, grad_inner_low)
+    wide_sum, grad_mixture, grad_attended = lax.optimization_barrier(
+        (wide_sum, grad_mixture, grad_attended)
+    )
+    wide_sum = lax.psum(wide_sum, both)
+    group_rows = PAIRS * 4 * PAIR
+
+    def attention_part(operands):
+        (
+            probs, grad_mixture, mixture, inverse, query_content, query_position, query_segment,
+            keys, values, relative, side, key_side, inputs, frame, positions, grad_attended,
+            token_sums, inner_bias_sum, segment_embed, grad_residual, w_query, w_key, w_value,
+        ) = operands
+        grad_projected, grad_keys, grad_values, small, bucket = attention_backward(
+            0, PAIRS, 0, [None] * 4 + [group_rows + D + EXTRA], probs, grad_mixture, mixture,
+            inverse, query_content, query_position, query_segment, keys, values, relative,
+            segment_embed, side, key_side, inputs, frame, positions,
         )
-    ]
-    vectors = Small(
-        jnp.concatenate([small[:5], token_sums[:5], inner_bias_sum.reshape(-1, D),
-                         jnp.zeros((2, D), jnp.float32)], axis=0)
-    )
-    for item in sums + [vectors]:
-        while item.at < item.stages:
-            item.step()
-    out_sum, query_sum, key_sum, value_sum, rel_sum = [settle(item) for item in sums]
-    grad_inputs = grad_residual + mm(grad_projected, w_query, nt)
-    grad_content = (
-        grad_inputs[:SEG] + mm(grad_keys[MEM:], w_key, nt) + mm(grad_values[MEM:], w_value, nt)
-    )
-    vectors = vectors.state
-    names = ("content", "position", "segment", "embed0", "embed1", "gain1", "shift1", "gain2", "shift2", "outer")
-    pieces = {name: vectors[index] for index, name in enumerate(names)}
-    pieces["embed"] = vectors[3:5]
-    pieces["inner"] = vectors[10:14].reshape(-1)
+        vectors = jnp.concatenate(
+            [token_sums, inner_bias_sum.reshape(-1, D), jnp.zeros((4, D), jnp.float32), small], axis=0
+        )
+        vectors = jnp.pad(vectors, ((0, EXTRA - vectors.shape[0]), (0, 0)))
+        others = jnp.concatenate([low_mm(mixture, grad_attended), low(vectors)], axis=0)
+        rest = Sum(lax.dynamic_update_slice(bucket, others, (group_rows, 0)))
+        while rest.at < rest.stages:
+            rest.step()
+        grad_inputs = grad_residual + mm(grad_projected, w_query, nt)
+        grad_content = (
+            grad_inputs[:SEG] + mm(grad_keys[MEM:], w_key, nt) + mm(grad_values[MEM:], w_value, nt)
+        )
+        return low(grad_content), low(grad_inputs[SEG:]), rest.state
+
+    operands = (
+        probs, grad_mixture, mixture, inverse, query_content, query_position, query_segment, keys,
+        values, relative, side, key_side, inputs, frame, positions, grad_attended, token_sums,
+        inner_bias_sum, segment_embed, grad_residual, w_query, w_key, w_value,
+    )
+    shapes = jax.eval_shape(attention_part, operands)
+    grad_content, grad_query, gathered = lax.cond(
+        sequence_lengths[0] > -1,
+        attention_part,
+        lambda operands: tuple(jnp.zeros(item.shape, item.dtype) for item in shapes),
+        operands,
+    )
+    rest = Sum(gathered)
+    outer_sum, inner_sum = widen(wide_sum)
+    query_sum, key_sum, value_sum, rel_sum, out_sum, vectors = settle_pairs(rest)
+    pieces = {
+        "gain1": vectors[0], "shift1": vectors[1], "gain2": vectors[2], "shift2": vectors[3],
+        "outer": vectors[4], "inner": vectors[8:12].reshape(-1), "content": vectors[16],
+        "position": vectors[17], "segment": vectors[18], "embed": vectors[19:21],
+    }
     return (
         low(final_out[None, :SEG]), low(final_out[None, SEG:]),
-        low(grad_content[None]), low(grad_inputs[None, SEG:]),
+        grad_content[None], grad_query[None],
         query_sum, key_sum, value_sum, out_sum, rel_sum,
         pieces["content"], pieces["position"], pieces["segment"], pieces["embed"].reshape(2, D),
         pieces["gain1"], pieces["shift1"], inner_sum, pieces["inner"], outer_sum, pieces["outer"],

time: 489 us -> 427 us (0.87)
  starting transfers between devices: 93.3 us -> 20.4 us
  matrix products: 48.3 us -> 21.6 us
  Pallas kernels: 175 us -> 197 us
  waiting for transfers between devices: 104 us -> 115 us
  local copies, waits for them, and re-layouts: 15.5 us -> 23.8 us
  other arithmetic: 31.1 us -> 24.8 us
    psum x1, waiting for transfers between devices: 60.2 us -> 0.01 us  [shards(): wide_sum = lax.psum(wide_sum, both)]
    ppermute x30 -> x6, waiting for transfers between devices: 0.36 us -> 45.3 us  [along(): lax.ppermute(tensor, 'mem', [(i, (i + shift) % ring) for i in range(ring)])]
    ppermute x30 -> x6, starting transfers between devices: 51.9 us -> 7.85 us  [along(): lax.ppermute(tensor, 'mem', [(i, (i + shift) % ring) for i in range(ring)])]
    ppermute x35 -> x6, starting transfers between devices: 34.9 us -> 6.13 us  [across(): lax.ppermute(tensor, 'batch', [(i, i ^ bits[i & 1]) for i in range(count)])]
    dot_general x14 -> x8, matrix products: 48.3 us -> 21.6 us  [mm(): lax.dot_general(left, right, dims, preferred_element_type=jnp.float32)]
    ppermute x35 -> x6, waiting for transfers between devices: 43.4 us -> 70 us  [across(): lax.ppermute(tensor, 'batch', [(i, i ^ bits[i & 1]) for i in range(count)])]
    pallas_call x6 -> x4, Pallas kernels: 82 us -> 105 us  [the longest x1 65 us: attention_backward(): pl.pallas_call(backward_kernel, grid=(count,), in_specs=[pl.BlockSpec((No...]
    convert_element_type x5 -> x3, other arithmetic: 12 us -> 0.01 us  [shards(): wide = lambda tensor: tensor.astype(jnp.float32)]
  transfers between devices with their start and end apart: 67 -> 14, of which waited for: 14 -> 11; matrix products, arithmetic and copies ran while one was open for 10% -> 14% of each run, Pallas kernels for 3% -> 18%
where the time goes in v3:
time: 427 us; the launch traced here: 419 us
  Pallas kernels  197 us (46%)
  waiting for transfers between devices  115 us (27%)
  other arithmetic  24.8 us (6%)
  local copies, waits for them, and re-layouts  23.8 us (6%)
  matrix products  21.6 us (5%)
  starting transfers between devices  20.4 us (5%)
  between operations  15.7 us (4%)
    ppermute x6, waiting for transfers between devices, across(): lax.ppermute(tensor, 'batch', [(i, i ^ bits[i & 1]) for i in range(count)])  70 us
    pallas_call x1, Pallas kernels, attention_backward(): pl.pallas_call(backward_kernel, grid=(count,), in_specs=[pl.BlockSpec((No...  65 us
    pallas_call x1, Pallas kernels, attention_forward(): pl.pallas_call(forward_kernel, grid=(PAIRS,), in_specs=[pair(2 * SEG), pa...  49.8 us
    ppermute x6, waiting for transfers between devices, along(): lax.ppermute(tensor, 'mem', [(i, (i + shift) % ring) for i in range(ring)])  45.3 us
    pallas_call x1, Pallas kernels, token_layer(): pl.pallas_call(token_kernel, grid=(count // TOKENS,), in_specs=[tile(D),...  41.9 us
    dot_general x8, matrix products, mm(): lax.dot_general(left, right, dims, preferred_element_type=jnp.float32)  21.6 us
    pallas_call x1, Pallas kernels, wide_grads(): pl.pallas_call(wide_grads_kernel, grid=(2, steps), in_specs=[pl.BlockSpec...  19.1 us
    pallas_call x1, Pallas kernels, widen(): pl.pallas_call(widen_kernel, grid=(hidden // WIDE,), in_specs=[pl.BlockSp...  11.4 us
  transfers between devices with their start and end apart: 14, of which 11 were waited for; matrix products, arithmetic and copies ran while one was open for 14% of the time, Pallas kernels for 18%

profile of v3, /device:TPU:0, one launch (start us, length us, event | category | flops | bytes accessed | tf_op | source)
XLA Modules:
  0.0 419.3 jit_solution(7944554731080088826)
XLA Ops:
  7.2 6.5 %all-to-all-start = ((bf16[4,96,768]{2,1,0:T(8,128)(2,1)}), bf16[4,96,768]{2,1,0:T(8,128)(2,1)}, u32[]{:S(2)}, u32[]{:S(2)}) async-start(bf16[4,96,768]{2,1,0:T(8,128)(2,1)} %param.29), calls=%async_computation | async-start | bytes 1179648 | tf_op jit(solution)/shard_map/all_to_all | solution.py:687
  27.6 3.2 convolution_convert_fusion.1
  30.8 3.7 add_convert_fusion.4
  34.5 3.9 convolution_convert_fusion.3.k_ref
  38.4 3.4 convolution_convert_fusion.2.v_ref
  41.8 49.8 %attention_forward.1 = (bf16[1024,768]{1,0:T(8,128)(2,1)}, f32[1024,768]{1,0:T(8,128)}, bf16[6,2,1024,896]{3,2,1,0:T(8,128)(2,1)}) custom-call(bf16[1024,768]{1,0:T(8,128)(2,1)} %get-tuple-element.205.qc_ref, bf16[1024,768]{1,0:T(8,128)(2,1)} %get-tuple-element.204.qp_ref, bf16[1024,768]{1,0:T(8,128)(2,1)} %get-tuple-element.203.qs_ref, ...), custom_call_target="tpu_custom_call" | custom-call | flops 30000001024 | bytes 30000000 | tf_op jit(solution)/shard_map/attention_forward/pallas_call | solution.py:126
  91.6 41.9 %token_layer.1 = (bf16[1024,768]{1,0:T(8,128)(2,1)}, bf16[1024,3072]{1,0:T(8,128)(2,1)}, bf16[1024,768]{1,0:T(8,128)(2,1)}, bf16[1024,3072]{1,0:T(8,128)(2,1)}, ...) custom-call(bf16[1024,768]{1,0:T(8,128)(2,1)} %pad_maximum_fusion.3., ...), custom_call_target="tpu_custom_call" | custom-call | flops 22000001024 | bytes 40000000 | tf_op jit(solution)/shard_map/token_layer/pallas_call | solution.py:422
  133.5 19.1 %wide_grads.1 = bf16[1536,3072]{1,0:T(8,128)(2,1)} custom-call(bf16[1024,768]{1,0:T(8,128)(2,1)} %get-tuple-element.127.outer_ref, bf16[1024,3072]{1,0:T(8,128)(2,1)} %get-tuple-element.128.active_ref, bf16[1024,768]{1,0:T(8,128)(2,1)} %get-tuple-element.129.low_ref, bf16[1024,3072]{1,0:T(8,128)(2,1)} %get-tuple-element.130.inner_ref), custom_call_target="tpu_custom_call" | custom-call | flops 9699999744 | bytes 25000000 | tf_op jit(solution)/shard_map/wide_grads/pallas_call | solution.py:628
  156.6 229.1 %conditional.1 = (bf16[4096,768]{1,0:T(8,128)(2,1)}, bf16[1,512,768]{2,1,0:T(8,128)(2,1)S(1)}, bf16[1,512,768]{2,1,0:T(8,128)(2,1)S(1)}) conditional(s32[]{:T(128)} %convert_element_type.128, () %tuple.21, (bf16[1408,768]{1,0:T(8,128)(2,1)}, bf16[6,2,1024,896]{3,2,1,0:T(8,128)(2,1)}, bf16[1024,768]{1,0:T(8,128)(2,1)}, bf16[1024,768]{1,0:T(8,128)(2,1)}, ...), branch_computations={%region_0.1_spmd, %region_1.2_spmd} | conditional | flops 51646259200 | bytes 216769824 | solution.py:768
  157.7 4.3 %convolution_convert_fusion = bf16[768,768]{1,0:T(8,128)(2,1)} fusion(bf16[1024,768]{1,0:T(8,128)(2,1)} %get-tuple-element.50.mix_ref, bf16[1024,768]{1,0:T(8,128)(2,1)} %get-tuple-element.65), kind=kOutput, calls=%fused_computation.12 | convolution fusion | flops 1208549376 | bytes 4325376 | tf_op jit(solution)/shard_map/cond/branch_1_fun/dot_general | solution.py:31
  162.0 65.0 %attention_backward.1 = (bf16[1024,768]{1,0:T(8,128)(2,1)}, bf16[896,768]{1,0:T(8,128)(2,1)}, bf16[896,768]{1,0:T(8,128)(2,1)}, f32[8,768]{1,0:T(8,128)}, bf16[4096,768]{1,0:T(8,128)(2,1)}) custom-call(bf16[6,2,1024,896]{3,2,1,0:T(8,128)(2,1)} %get-tuple-element.48.prob_ref, bf16[1024,768]{1,0:T(8,128)(2,1)} %get-tuple-element.49.dmix_ref, ...), custom_call_target="tpu_custom_call" | custom-call | flops 48000000000 | bytes 48000000 | tf_op jit(solution)/shard_map/cond/branch_1_fun/attention_backward/pallas_call | solution.py:286
  232.7 5.7 %collective-permute-done = bf16[2048,768]{1,0:T(8,128)(2,1)} collective-permute-done((bf16[2048,768]{1,0:T(8,128)(2,1)S(1)}, bf16[2048,768]{1,0:T(8,128)(2,1)}, u32[]{:S(2)}, u32[]{:S(2)}) %collective-permute-start) | collective-permute-done | bytes 3145760 | tf_op jit(solution)/shard_map/cond/branch_1_fun/ppermute | solution.py:465
  238.4 3.7 add_convert_fusion
  244.8 20.8 %collective-permute-done.1 = bf16[1024,768]{1,0:T(8,128)(2,1)} collective-permute-done((bf16[1024,768]{1,0:T(8,128)(2,1)}, bf16[1024,768]{1,0:T(8,128)(2,1)}, u32[]{:S(2)}, u32[]{:S(2)}) %collective-permute-start.1) | collective-permute-done | bytes 1572896 | tf_op jit(solution)/shard_map/cond/branch_1_fun/ppermute | solution.py:465
  271.4 16.8 %collective-permute-done.2 = bf16[512,768]{1,0:T(8,128)(2,1)S(1)} collective-permute-done((bf16[512,768]{1,0:T(8,128)(2,1)S(1)}, bf16[512,768]{1,0:T(8,128)(2,1)S(1)}, u32[]{:S(2)}, u32[]{:S(2)}) %collective-permute-start.2) | collective-permute-done | bytes 786464 | tf_op jit(solution)/shard_map/cond/branch_1_fun/ppermute | solution.py:465
  294.9 4.8 %collective-permute-done.3 = bf16[128,768]{1,0:T(8,128)(2,1)S(1)} collective-permute-done((bf16[128,768]{1,0:T(8,128)(2,1)S(1)}, bf16[128,768]{1,0:T(8,128)(2,1)S(1)}, u32[]{:S(2)}, u32[]{:S(2)}) %collective-permute-start.3) | collective-permute-done | bytes 196640 | tf_op jit(solution)/shard_map/cond/branch_1_fun/ppermute | solution.py:474
  299.7 3.4 collective-permute-done.5
  303.1 12.7 %collective-permute-done.4 = bf16[128,768]{1,0:T(8,128)(2,1)S(1)} collective-permute-done((bf16[128,768]{1,0:T(8,128)(2,1)S(1)}, bf16[128,768]{1,0:T(8,128)(2,1)S(1)}, u32[]{:S(2)}, u32[]{:S(2)}) %collective-permute-start.4) | collective-permute-done | bytes 196640 | tf_op jit(solution)/shard_map/cond/branch_1_fun/ppermute | solution.py:474
  318.5 9.0 %collective-permute-done.8 = bf16[128,768]{1,0:T(8,128)(2,1)S(1)} collective-permute-done((bf16[128,768]{1,0:T(8,128)(2,1)S(1)}, bf16[128,768]{1,0:T(8,128)(2,1)S(1)}, u32[]{:S(2)}, u32[]{:S(2)}) %collective-permute-start.8) | collective-permute-done | bytes 196640 | tf_op jit(solution)/shard_map/cond/branch_1_fun/ppermute | solution.py:474
  327.5 14.9 %collective-permute-done.7 = bf16[128,768]{1,0:T(8,128)(2,1)S(1)} collective-permute-done((bf16[128,768]{1,0:T(8,128)(2,1)S(1)}, bf16[128,768]{1,0:T(8,128)(2,1)S(1)}, u32[]{:S(2)}, u32[]{:S(2)}) %collective-permute-start.7) | collective-permute-done | bytes 196640 | tf_op jit(solution)/shard_map/cond/branch_1_fun/ppermute | solution.py:474
  347.3 7.7 %collective-permute-done.9 = bf16[512,768]{1,0:T(8,128)(2,1)S(1)} collective-permute-done((bf16[512,768]{1,0:T(8,128)(2,1)S(1)}, bf16[512,768]{1,0:T(8,128)(2,1)S(1)}, u32[]{:S(2)}, u32[]{:S(2)}) %collective-permute-start.9) | collective-permute-done | bytes 786464 | tf_op jit(solution)/shard_map/cond/branch_1_fun/ppermute | solution.py:465
  357.5 19.0 %collective-permute-done.10 = bf16[1024,768]{1,0:T(8,128)(2,1)S(1)} collective-permute-done((bf16[1024,768]{1,0:T(8,128)(2,1)S(1)}, bf16[1024,768]{1,0:T(8,128)(2,1)S(1)}, u32[]{:S(2)}, u32[]{:S(2)}) %collective-permute-start.10) | collective-permute-done | bytes 1572896 | tf_op jit(solution)/shard_map/cond/branch_1_fun/ppermute | solution.py:465
  387.5 10.0 %settle_pairs.1 = (f32[768,768]{1,0:T(8,128)}, f32[768,768]{1,0:T(8,128)}, f32[768,768]{1,0:T(8,128)}, f32[768,768]{1,0:T(8,128)}, f32[768,768]{1,0:T(8,128)}, /*index=5*/f32[24,768]{1,0:T(8,128)S(1)}) custom-call(s32[32]{0:T(128)S(1)} %fusion.19.place_ref, bf16[4096,768]{1,0:T(8,128)(2,1)} %get-tuple-element.141.in_ref), custom_call_target="tpu_custom_call" | custom-call | tf_op jit(solution)/shard_map/settle_pairs/pallas_call | solution.py:564
  400.6 11.4 %widen.1 = (f32[3072,768]{1,0:T(8,128)}, f32[768,3072]{1,0:T(8,128)}) custom-call(bf16[1536,3072]{1,0:T(8,128)(2,1)} %all-reduce.4.cloned.1.call-done.outer_ref.inner_ref, bf16[1536,3072]{1,0:T(8,128)(2,1)} %all-reduce.4.cloned.1.call-done.outer_ref.inner_ref), custom_call_target="tpu_custom_call" | custom-call | tf_op jit(solution)/shard_map/widen/pallas_call | solution.py:657
  (148 shorter events, 62.6 us)
Async XLA Ops:
  7.2 20.4 %copy-start = (bf16[768,768]{1,0:T(8,128)(2,1)S(1)}, bf16[768,768]{1,0:T(8,128)(2,1)}, u32[]{:S(2)}) copy-start(bf16[768,768]{1,0:T(8,128)(2,1)} %param.37) | copy-start | bytes 3538948
  7.2 27.3 %all-to-all-start = ((bf16[4,96,768]{2,1,0:T(8,128)(2,1)}), bf16[4,96,768]{2,1,0:T(8,128)(2,1)}, u32[]{:S(2)}, u32[]{:S(2)}) async-start(bf16[4,96,768]{2,1,0:T(8,128)(2,1)} %param.29), calls=%async_computation | async-start | bytes 1179648 | tf_op jit(solution)/shard_map/all_to_all | solution.py:687
  13.7 386.9 %all-reduce.4.cloned.1.call-start = ((), (), s32[]{:S(2)}) async-start(), calls=%async_computation.1 | async-start | bytes 18874368 | tf_op jit(solution)/shard_map/psum | solution.py:734
  18.4 3.7 copy-start.14
  18.4 3.7 copy-start.15
  30.8 3.7 copy-start.4
  34.5 3.9 copy-start.10
  38.4 3.4 copy-start.17
  38.4 3.4 copy-start.30
  232.6 5.9 %collective-permute-start = (bf16[2048,768]{1,0:T(8,128)(2,1)S(1)}, bf16[2048,768]{1,0:T(8,128)(2,1)}, u32[]{:S(2)}, u32[]{:S(2)}) collective-permute-start(bf16[2048,768]{1,0:T(8,128)(2,1)S(1)} %constant_dynamic-slice_fusion.5), channel_id=1, source_target_pairs={{0,4},{4,0},{8,12},{12,8},{16,20},{20,16},{24,28},{28,24},{1,5},{5... | collective-permute-start | bytes 9437192 | tf_op jit(solution)/shard_map/cond/branch_1_fun/ppermute | solution.py:465
  243.3 22.3 %collective-permute-start.1 = (bf16[1024,768]{1,0:T(8,128)(2,1)}, bf16[1024,768]{1,0:T(8,128)(2,1)}, u32[]{:S(2)}, u32[]{:S(2)}) collective-permute-start(bf16[1024,768]{1,0:T(8,128)(2,1)} %constant_dynamic-slice_fusion.4), channel_id=1, source_target_pairs={{0,8},{4,20},{8,0},{12,28},{16,24},{20,4},{24,16},{28,12},{1,9},{5... | collective-permute-start | bytes 4718600 | tf_op jit(solution)/shard_map/cond/branch_1_fun/ppermute | solution.py:465
  269.8 18.4 %collective-permute-start.2 = (bf16[512,768]{1,0:T(8,128)(2,1)S(1)}, bf16[512,768]{1,0:T(8,128)(2,1)S(1)}, u32[]{:S(2)}, u32[]{:S(2)}) collective-permute-start(bf16[512,768]{1,0:T(8,128)(2,1)S(1)} %constant_dynamic-slice_fusion.3), channel_id=1, source_target_pairs={{0,16},{4,12},{8,24},{12,4},{16,0},{20,28},{24,8},{28,20},{1,17},{... | collective-permute-start | bytes 2359304 | tf_op jit(solution)/shard_map/cond/branch_1_fun/ppermute | solution.py:465
  289.6 10.1 %collective-permute-start.3 = (bf16[128,768]{1,0:T(8,128)(2,1)S(1)}, bf16[128,768]{1,0:T(8,128)(2,1)S(1)}, u32[]{:S(2)}, u32[]{:S(2)}) collective-permute-start(bf16[128,768]{1,0:T(8,128)(2,1)S(1)} %get-tuple-element.189), channel_id=1, source_target_pairs={{0,1},{1,2},{2,3},{3,0},{4,5},{5,6},{6,7},{7,4},{8,9},{9,10},{10,1... | collective-permute-start | bytes 589832 | tf_op jit(solution)/shard_map/cond/branch_1_fun/ppermute | solution.py:474
  291.7 11.4 %collective-permute-start.5 = (bf16[128,768]{1,0:T(8,128)(2,1)S(1)}, bf16[128,768]{1,0:T(8,128)(2,1)S(1)}, u32[]{:S(2)}, u32[]{:S(2)}) collective-permute-start(bf16[128,768]{1,0:T(8,128)(2,1)S(1)} %get-tuple-element.190), channel_id=1, source_target_pairs={{0,3},{1,0},{2,1},{3,2},{4,7},{5,4},{6,5},{7,6},{8,11},{9,8},{10,9... | collective-permute-start | bytes 589832 | tf_op jit(solution)/shard_map/cond/branch_1_fun/ppermute | solution.py:474
  293.8 22.0 %collective-permute-start.4 = (bf16[128,768]{1,0:T(8,128)(2,1)S(1)}, bf16[128,768]{1,0:T(8,128)(2,1)S(1)}, u32[]{:S(2)}, u32[]{:S(2)}) collective-permute-start(bf16[128,768]{1,0:T(8,128)(2,1)S(1)} %get-tuple-element.191), channel_id=1, source_target_pairs={{0,2},{1,3},{2,0},{3,1},{4,6},{5,7},{6,4},{7,5},{8,10},{9,11},{10,... | collective-permute-start | bytes 589832 | tf_op jit(solution)/shard_map/cond/branch_1_fun/ppermute | solution.py:474
  315.9 11.5 %collective-permute-start.8 = (bf16[128,768]{1,0:T(8,128)(2,1)S(1)}, bf16[128,768]{1,0:T(8,128)(2,1)S(1)}, u32[]{:S(2)}, u32[]{:S(2)}) collective-permute-start(bf16[128,768]{1,0:T(8,128)(2,1)S(1)} %get-tuple-element.183), channel_id=1, source_target_pairs={{0,3},{1,0},{2,1},{3,2},{4,7},{5,4},{6,5},{7,6},{8,11},{9,8},{10,9... | collective-permute-start | bytes 589832 | tf_op jit(solution)/shard_map/cond/branch_1_fun/ppermute | solution.py:474
  317.8 24.5 %collective-permute-start.7 = (bf16[128,768]{1,0:T(8,128)(2,1)S(1)}, bf16[128,768]{1,0:T(8,128)(2,1)S(1)}, u32[]{:S(2)}, u32[]{:S(2)}) collective-permute-start(bf16[128,768]{1,0:T(8,128)(2,1)S(1)} %get-tuple-element.183), channel_id=1, source_target_pairs={{0,2},{1,3},{2,0},{3,1},{4,6},{5,7},{6,4},{7,5},{8,10},{9,11},{10,... | collective-permute-start | bytes 589832 | tf_op jit(solution)/shard_map/cond/branch_1_fun/ppermute | solution.py:474
  317.8 25.0 %collective-permute-start.6 = (bf16[128,768]{1,0:T(8,128)(2,1)S(1)}, bf16[128,768]{1,0:T(8,128)(2,1)S(1)}, u32[]{:S(2)}, u32[]{:S(2)}) collective-permute-start(bf16[128,768]{1,0:T(8,128)(2,1)S(1)} %get-tuple-element.183), channel_id=1, source_target_pairs={{0,1},{1,2},{2,3},{3,0},{4,5},{5,6},{6,7},{7,4},{8,9},{9,10},{10,1... | collective-permute-start | bytes 589832 | tf_op jit(solution)/shard_map/cond/branch_1_fun/ppermute | solution.py:474
  342.9 12.1 %collective-permute-start.9 = (bf16[512,768]{1,0:T(8,128)(2,1)S(1)}, bf16[512,768]{1,0:T(8,128)(2,1)S(1)}, u32[]{:S(2)}, u32[]{:S(2)}) collective-permute-start(bf16[512,768]{1,0:T(8,128)(2,1)S(1)} %pad_maximum_fusion), channel_id=1, source_target_pairs={{0,16},{4,12},{8,24},{12,4},{16,0},{20,28},{24,8},{28,20},{1,17},{... | collective-permute-start | bytes 2359304 | tf_op jit(solution)/shard_map/cond/branch_1_fun/ppermute | solution.py:465
  355.0 22.8 %copy-start.9 = (bf16[768,768]{1,0:T(8,128)(2,1)S(1)}, bf16[768,768]{1,0:T(8,128)(2,1)}, u32[]{:S(2)}) copy-start(bf16[768,768]{1,0:T(8,128)(2,1)} %get-tuple-element.71) | copy-start | bytes 3538948 | tf_op jit(solution)/shard_map/cond
  356.0 20.4 %collective-permute-start.10 = (bf16[1024,768]{1,0:T(8,128)(2,1)S(1)}, bf16[1024,768]{1,0:T(8,128)(2,1)S(1)}, u32[]{:S(2)}, u32[]{:S(2)}) collective-permute-start(bf16[1024,768]{1,0:T(8,128)(2,1)S(1)} %get-tuple-element.188), channel_id=1, source_target_pairs={{0,8},{4,20},{8,0},{12,28},{16,24},{20,4},{24,16},{28,12},{1,9},{5... | collective-permute-start | bytes 4718600 | tf_op jit(solution)/shard_map/cond/branch_1_fun/ppermute | solution.py:465
  377.8 5.7 %collective-permute-start.11 = (bf16[2048,768]{1,0:T(8,128)(2,1)S(1)}, bf16[2048,768]{1,0:T(8,128)(2,1)S(1)}, u32[]{:S(2)}, u32[]{:S(2)}) collective-permute-start(bf16[2048,768]{1,0:T(8,128)(2,1)S(1)} %get-tuple-element.184), channel_id=1, source_target_pairs={{0,4},{4,0},{8,12},{12,8},{16,20},{20,16},{24,28},{28,24},{1,5},{5... | collective-permute-start | bytes 9437192 | tf_op jit(solution)/shard_map/cond/branch_1_fun/ppermute | solution.py:465
  387.4 11.9 %copy-start.6 = (bf16[1024,768]{1,0:T(8,128)(2,1)S(1)}, bf16[1024,768]{1,0:T(8,128)(2,1)}, u32[]{:S(2)}) copy-start(bf16[1024,768]{1,0:T(8,128)(2,1)} %get-tuple-element.125) | copy-start | bytes 4718596
  400.6 11.4 %copy-start.1 = (bf16[768,768]{1,0:T(8,128)(2,1)S(1)}, bf16[768,768]{1,0:T(8,128)(2,1)}, u32[]{:S(2)}) copy-start(bf16[768,768]{1,0:T(8,128)(2,1)} %param.37) | copy-start | bytes 3538948
  (22 other events, 40.4 us)
Sparse Core Ops, SparseCore 0:
  152.7 218.3 all-reduce.3

commit v4 on v3

--- a/solution.py
+++ b/solution.py
@@ -524,6 +524,13 @@
         return place
 
 
+def together(active, tree):
+    states, tree = lax.optimization_barrier(([item.state for item in active], tree))
+    for item, state in zip(active, states):
+        item.state = state
+    return tree
+
+
 def placed(item):
     tensor, place = item.state, item.places()
     blocks = place.shape[0]
@@ -540,41 +547,41 @@
 
 
 def settle_pairs_kernel(place_ref, in_ref, *rest):
-    outs, full = rest[:-1], rest[-1]
+    outs, full = rest[-6:-1], rest[-1]
     rows = in_ref.shape[0] // place_ref.shape[0]
-    grads = PAIRS * 4 * PAIR
 
     @pl.when(pl.program_id(0) == 0)
     def _():
         for item in range(place_ref.shape[0]):
             full[item * rows : (item + 1) * rows, :] = block_of(place_ref, in_ref, item)
-        outs[4][...] = full[grads : grads + D, :]
-        outs[5][...] = full[grads + D : grads + D + outs[5].shape[0], :]
+        grads = PAIRS // 2 * 4 * PAIR
+        outs[4][...] = full[grads : grads + outs[4].shape[0], :]
 
     for index in range(4):
         start = pl.multiple_of((pl.program_id(0) * 4 + index) * PAIR, PAIR)
         outs[index][...] = full[pl.ds(start, PAIR), :].T
 
 
-def settle_pairs(item):
+def settle_pairs(item, first, count, earlier, after):
     tensor, place = placed(item)
     rows, lanes = tensor.shape
     square = jax.ShapeDtypeStruct((D, D), jnp.float32)
-    whole_out = lambda count: pl.BlockSpec((count, lanes), lambda i, p: (0, 0))
     return pl.pallas_call(
         settle_pairs_kernel,
         grid_spec=pltpu.PrefetchScalarGridSpec(
             num_scalar_prefetch=1,
-            grid=(PAIRS,),
-            in_specs=[pl.BlockSpec((rows, lanes), lambda i, p: (0, 0))],
-            out_specs=[pl.BlockSpec((lanes, PAIR), lambda i, p: (0, i))] * 4
-            + [whole_out(D), whole_out(VECTORS)],
+            grid=(count,),
+            in_specs=[pl.BlockSpec((rows, lanes), lambda i, p: (0, 0))]
+            + [pl.BlockSpec(memory_space=pl.ANY)] * len(earlier),
+            out_specs=[pl.BlockSpec((lanes, PAIR), lambda i, p: (0, first + i))] * 4
+            + [pl.BlockSpec((after, lanes), lambda i, p: (0, 0))],
             scratch_shapes=[pltpu.VMEM((rows, lanes), jnp.float32)],
         ),
-        out_shape=[square] * 5 + [jax.ShapeDtypeStruct((VECTORS, lanes), jnp.float32)],
+        out_shape=[square] * 4 + [jax.ShapeDtypeStruct((after, lanes), jnp.float32)],
+        input_output_aliases={2 + index: index for index in range(len(earlier))},
         compiler_params=pltpu.CompilerParams(vmem_limit_bytes=48 * 1024 * 1024),
         name="settle_pairs",
-    )(place, tensor)
+    )(place, tensor, *earlier)
 
 
 def sinusoid():
@@ -732,32 +739,46 @@
         (wide_sum, grad_mixture, grad_attended)
     )
     wide_sum = lax.psum(wide_sum, both)
-    group_rows = PAIRS * 4 * PAIR
-
     def attention_part(operands):
         (
             probs, grad_mixture, mixture, inverse, query_content, query_position, query_segment,
             keys, values, relative, side, key_side, inputs, frame, positions, grad_attended,
             token_sums, inner_bias_sum, segment_embed, grad_residual, w_query, w_key, w_value,
         ) = operands
-        grad_projected, grad_keys, grad_values, small, bucket = attention_backward(
-            0, PAIRS, 0, [None] * 4 + [group_rows + D + EXTRA], probs, grad_mixture, mixture,
-            inverse, query_content, query_position, query_segment, keys, values, relative,
+        common = (
+            mixture, inverse, query_content, query_position, query_segment, keys, values, relative,
             segment_embed, side, key_side, inputs, frame, positions,
         )
+        half = PAIRS // 2
+        group_rows = half * 4 * PAIR
+        chain = attention_backward(
+            0, half, 0, [None] * 4 + [group_rows + D], probs, grad_mixture, *common
+        )
+        early = Sum(lax.dynamic_update_slice(chain[4], low_mm(mixture, grad_attended), (group_rows, 0)))
+        early.step()
+        chain, grad_mixture = together([early], (list(chain[:4]), grad_mixture))
+        early.step()
+        chain = attention_backward(
+            half, half, 0, chain + [group_rows + EXTRA], probs, grad_mixture, *common
+        )
+        grad_projected, grad_keys, grad_values, small, bucket = together([early], list(chain))
         vectors = jnp.concatenate(
             [token_sums, inner_bias_sum.reshape(-1, D), jnp.zeros((4, D), jnp.float32), small], axis=0
         )
         vectors = jnp.pad(vectors, ((0, EXTRA - vectors.shape[0]), (0, 0)))
-        others = jnp.concatenate([low_mm(mixture, grad_attended), low(vectors)], axis=0)
-        rest = Sum(lax.dynamic_update_slice(bucket, others, (group_rows, 0)))
-        while rest.at < rest.stages:
-            rest.step()
+        late = Sum(lax.dynamic_update_slice(bucket, low(vectors), (group_rows, 0)))
+        while late.at < late.stages:
+            late.step()
+            if early.at < early.stages:
+                early.step()
+                together([late, early], ())
+        *sums, out_sum = settle_pairs(early, 0, half, (), D)
+        *sums, vectors = settle_pairs(late, half, half, sums, VECTORS)
         grad_inputs = grad_residual + mm(grad_projected, w_query, nt)
         grad_content = (
             grad_inputs[:SEG] + mm(grad_keys[MEM:], w_key, nt) + mm(grad_values[MEM:], w_value, nt)
         )
-        return low(grad_content), low(grad_inputs[SEG:]), rest.state
+        return low(grad_content), low(grad_inputs[SEG:]), sums, out_sum, vectors
 
     operands = (
         probs, grad_mixture, mixture, inverse, query_content, query_position, query_segment, keys,
@@ -765,15 +786,14 @@
         inner_bias_sum, segment_embed, grad_residual, w_query, w_key, w_value,
     )
     shapes = jax.eval_shape(attention_part, operands)
-    grad_content, grad_query, gathered = lax.cond(
+    grad_content, grad_query, sums, out_sum, vectors = lax.cond(
         sequence_lengths[0] > -1,
         attention_part,
-        lambda operands: tuple(jnp.zeros(item.shape, item.dtype) for item in shapes),
+        lambda operands: jax.tree.map(lambda item: jnp.zeros(item.shape, item.dtype), shapes),
         operands,
     )
-    rest = Sum(gathered)
+    query_sum, key_sum, value_sum, rel_sum = sums
     outer_sum, inner_sum = widen(wide_sum)
-    query_sum, key_sum, value_sum, rel_sum, out_sum, vectors = settle_pairs(rest)
     pieces = {
         "gain1": vectors[0], "shift1": vectors[1], "gain2": vectors[2], "shift2": vectors[3],
         "outer": vectors[4], "inner": vectors[8:12].reshape(-1), "content": vectors[16],

time: 427 us -> 400 us (0.937)
  waiting for transfers between devices: 115 us -> 76 us
  starting transfers between devices: 20.4 us -> 36.6 us
  Pallas kernels: 197 us -> 204 us
  local copies, waits for them, and re-layouts: 23.8 us -> 17.3 us
    ppermute x6 -> x12, waiting for transfers between devices: 70 us -> 32.4 us  [across(): lax.ppermute(tensor, 'batch', [(i, i ^ bits[i & 1]) for i in range(count)])]
    ppermute x6 -> x12, starting transfers between devices: 7.85 us -> 20.1 us  [along(): lax.ppermute(tensor, 'mem', [(i, (i + shift) % ring) for i in range(ring)])]
    pallas_call x1 -> x2, Pallas kernels: 65 us -> 72.6 us  [attention_backward(): pl.pallas_call(backward_kernel, grid=(count,), in_specs=[pl.BlockSpec((No...]
    cond x19 -> x18, local copies, waits for them, and re-layouts: 6.35 us -> 1.41 us
    ppermute x6 -> x12, starting transfers between devices: 6.13 us -> 10.1 us  [across(): lax.ppermute(tensor, 'batch', [(i, i ^ bits[i & 1]) for i in range(count)])]
    ppermute x6 -> x12, waiting for transfers between devices: 45.3 us -> 43.5 us  [along(): lax.ppermute(tensor, 'mem', [(i, (i + shift) % ring) for i in range(ring)])]
    pallas_call x1 -> x2, Pallas kernels: 10 us -> 8.67 us  [settle_pairs(): pl.pallas_call(settle_pairs_kernel, grid_spec=pltpu.PrefetchScalarGridSpe...]
  transfers between devices with their start and end apart: 14 -> 26, of which waited for: 11 -> 15; matrix products, arithmetic and copies ran while one was open for 14% -> 13% of each run, Pallas kernels for 18% -> 21%
where the time goes in v4:
time: 400 us; the launch traced here: 394 us
  Pallas kernels  204 us (51%)
  waiting for transfers between devices  76 us (19%)
  starting transfers between devices  36.6 us (9%)
  matrix products  22.6 us (6%)
  other arithmetic  21.5 us (5%)
  local copies, waits for them, and re-layouts  17.3 us (4%)
  between operations  15.4 us (4%)
    pallas_call x2, Pallas kernels, attention_backward(): pl.pallas_call(backward_kernel, grid=(count,), in_specs=[pl.BlockSpec((No...  72.6 us
    pallas_call x1, Pallas kernels, attention_forward(): pl.pallas_call(forward_kernel, grid=(PAIRS,), in_specs=[pair(2 * SEG), pa...  49.8 us
    ppermute x12, waiting for transfers between devices, along(): lax.ppermute(tensor, 'mem', [(i, (i + shift) % ring) for i in range(ring)])  43.5 us
    pallas_call x1, Pallas kernels, token_layer(): pl.pallas_call(token_kernel, grid=(count // TOKENS,), in_specs=[tile(D),...  41.9 us
    ppermute x12, waiting for transfers between devices, across(): lax.ppermute(tensor, 'batch', [(i, i ^ bits[i & 1]) for i in range(count)])  32.4 us
    dot_general x8, matrix products, mm(): lax.dot_general(left, right, dims, preferred_element_type=jnp.float32)  22.6 us
    ppermute x12, starting transfers between devices, along(): lax.ppermute(tensor, 'mem', [(i, (i + shift) % ring) for i in range(ring)])  20.1 us
    pallas_call x1, Pallas kernels, wide_grads(): pl.pallas_call(wide_grads_kernel, grid=(2, steps), in_specs=[pl.BlockSpec...  19.3 us
  transfers between devices with their start and end apart: 26, of which 15 were waited for; matrix products, arithmetic and copies ran while one was open for 13% of the time, Pallas kernels for 21%

profile of v4, /device:TPU:0, one launch (start us, length us, event | category | flops | bytes accessed | tf_op | source)
XLA Modules:
  0.0 393.6 jit_solution(11941690824870982115)
XLA Ops:
  7.2 6.5 %all-to-all-start = ((bf16[4,96,768]{2,1,0:T(8,128)(2,1)}), bf16[4,96,768]{2,1,0:T(8,128)(2,1)}, u32[]{:S(2)}, u32[]{:S(2)}) async-start(bf16[4,96,768]{2,1,0:T(8,128)(2,1)} %param.29), calls=%async_computation | async-start | bytes 1179648 | tf_op jit(solution)/shard_map/all_to_all | solution.py:694
  42.0 49.8 %attention_forward.1 = (bf16[1024,768]{1,0:T(8,128)(2,1)}, f32[1024,768]{1,0:T(8,128)}, bf16[6,2,1024,896]{3,2,1,0:T(8,128)(2,1)}) custom-call(bf16[1024,768]{1,0:T(8,128)(2,1)} %get-tuple-element.286.qc_ref, bf16[1024,768]{1,0:T(8,128)(2,1)} %get-tuple-element.285.qp_ref, bf16[1024,768]{1,0:T(8,128)(2,1)} %get-tuple-element.284.qs_ref, ...), custom_call_target="tpu_custom_call" | custom-call | flops 30000001024 | bytes 30000000 | tf_op jit(solution)/shard_map/attention_forward/pallas_call | solution.py:126
  91.8 41.9 %token_layer.1 = (bf16[1024,768]{1,0:T(8,128)(2,1)}, bf16[1024,3072]{1,0:T(8,128)(2,1)}, bf16[1024,768]{1,0:T(8,128)(2,1)}, bf16[1024,3072]{1,0:T(8,128)(2,1)}, ...) custom-call(bf16[1024,768]{1,0:T(8,128)(2,1)} %pad_maximum_fusion.10, ...), custom_call_target="tpu_custom_call" | custom-call | flops 22000001024 | bytes 40000000 | tf_op jit(solution)/shard_map/token_layer/pallas_call | solution.py:422
  133.6 19.3 %wide_grads.1 = bf16[1536,3072]{1,0:T(8,128)(2,1)} custom-call(bf16[1024,768]{1,0:T(8,128)(2,1)} %get-tuple-element.193.outer_ref, bf16[1024,3072]{1,0:T(8,128)(2,1)} %get-tuple-element.194.active_ref, bf16[1024,768]{1,0:T(8,128)(2,1)} %get-tuple-element.195.low_ref, bf16[1024,3072]{1,0:T(8,128)(2,1)} %get-tuple-element.196.inner_ref), custom_call_target="tpu_custom_call" | custom-call | flops 9699999744 | bytes 25000000 | tf_op jit(solution)/shard_map/wide_grads/pallas_call | solution.py:635
  156.9 215.3 %conditional.1 = (f32[768,768]{1,0:T(8,128)}, f32[768,768]{1,0:T(8,128)}, f32[768,768]{1,0:T(8,128)}, f32[768,768]{1,0:T(8,128)}, f32[768,768]{1,0:T(8,128)}, /*...) conditional(s32[]{:T(128)} %convert_element_type.170, () %tuple.31, ...), branch_computations={%region_0.1_spmd, %region_1.2_spmd} | conditional | flops 51666321408 | bytes 228002400 | solution.py:789
  158.1 36.3 %attention_backward.2 = (bf16[1024,768]{1,0:T(8,128)(2,1)}, bf16[896,768]{1,0:T(8,128)(2,1)}, bf16[896,768]{1,0:T(8,128)(2,1)}, f32[8,768]{1,0:T(8,128)}, bf16[2304,768]{1,0:T(8,128)(2,1)}) custom-call(bf16[6,2,1024,896]{3,2,1,0:T(8,128)(2,1)} %get-tuple-element.67.prob_ref, bf16[1024,768]{1,0:T(8,128)(2,1)} %get-tuple-element.90.dmix_ref, ...), custom_call_target="tpu_custom_call" | custom-call | flops 24000000000 | bytes 24000000 | tf_op jit(solution)/shard_map/cond/branch_1_fun/attention_backward/pallas_call | solution.py:286
  194.4 4.4 %fusion.2 = bf16[2304,768]{1,0:T(8,128)(2,1)} fusion(bf16[2304,768]{1,0:T(8,128)(2,1)} %get-tuple-element.83, bf16[1024,768]{1,0:T(8,128)(2,1)} %get-tuple-element.69.mix_ref, bf16[1024,768]{1,0:T(8,128)(2,1)} %get-tuple-element.84), kind=kOutput, calls=%fused_computation.12 | convolution fusion | flops 1208549376 | bytes 4325376 | tf_op jit(solution)/shard_map/cond/branch_1_fun/dot_general | solution.py:31
  208.4 36.3 %attention_backward.3 = (bf16[1024,768]{1,0:T(8,128)(2,1)}, bf16[896,768]{1,0:T(8,128)(2,1)}, bf16[896,768]{1,0:T(8,128)(2,1)}, f32[8,768]{1,0:T(8,128)}, bf16[1792,768]{1,0:T(8,128)(2,1)}) custom-call(bf16[6,2,1024,896]{3,2,1,0:T(8,128)(2,1)} %get-tuple-element.67.prob_ref, ...), custom_call_target="tpu_custom_call", output_to_operand_aliasing={{0}: (16, {}), {1}: (17, {}), {2}: (18, {}), {3}: (19, {})} | custom-call | flops 24000000000 | bytes 24000000 | tf_op jit(solution)/shard_map/cond/branch_1_fun/attention_backward/pallas_call | solution.py:286
  249.2 7.1 %collective-permute-done.3 = bf16[288,768]{1,0:T(8,128)(2,1)S(1)} collective-permute-done((bf16[288,768]{1,0:T(8,128)(2,1)S(1)}, bf16[288,768]{1,0:T(8,128)(2,1)S(1)}, u32[]{:S(2)}, u32[]{:S(2)}) %collective-permute-start.3) | collective-permute-done | bytes 442400 | tf_op jit(solution)/shard_map/cond/branch_1_fun/ppermute | solution.py:465
  265.1 3.9 collective-permute-done.5
  271.8 5.5 %collective-permute-done.6 = bf16[72,768]{1,0:T(8,128)(2,1)S(1)} collective-permute-done((bf16[72,768]{1,0:T(8,128)(2,1)S(1)}, bf16[72,768]{1,0:T(8,128)(2,1)S(1)}, u32[]{:S(2)}, u32[]{:S(2)}) %collective-permute-start.6) | collective-permute-done | bytes 110624 | tf_op jit(solution)/shard_map/cond/branch_1_fun/ppermute | solution.py:474
  281.8 7.0 %collective-permute-done.11 = bf16[72,768]{1,0:T(8,128)(2,1)S(1)} collective-permute-done((bf16[72,768]{1,0:T(8,128)(2,1)S(1)}, bf16[72,768]{1,0:T(8,128)(2,1)S(1)}, u32[]{:S(2)}, u32[]{:S(2)}) %collective-permute-start.11) | collective-permute-done | bytes 110624 | tf_op jit(solution)/shard_map/cond/branch_1_fun/ppermute | solution.py:474
  288.8 6.7 %collective-permute-done.10 = bf16[72,768]{1,0:T(8,128)(2,1)S(1)} collective-permute-done((bf16[72,768]{1,0:T(8,128)(2,1)S(1)}, bf16[72,768]{1,0:T(8,128)(2,1)S(1)}, u32[]{:S(2)}, u32[]{:S(2)}) %collective-permute-start.10) | collective-permute-done | bytes 110624 | tf_op jit(solution)/shard_map/cond/branch_1_fun/ppermute | solution.py:474
  296.9 4.8 %collective-permute-start.12 = (bf16[56,768]{1,0:T(8,128)(2,1)S(1)}, bf16[56,768]{1,0:T(8,128)(2,1)S(1)}, u32[]{:S(2)}, u32[]{:S(2)}) collective-permute-start(bf16[56,768]{1,0:T(8,128)(2,1)S(1)} %get-tuple-element.267), channel_id=1, source_target_pairs={{0,1},{1,2},{2,3},{3,0},{4,5},{5,6},{6,7},{7,4},{8,9},{9,10},{10,1... | collective-permute-start | bytes 258056 | tf_op jit(solution)/shard_map/cond/branch_1_fun/ppermute | solution.py:474
  301.7 4.2 %collective-permute-start.13 = (bf16[56,768]{1,0:T(8,128)(2,1)S(1)}, bf16[56,768]{1,0:T(8,128)(2,1)S(1)}, u32[]{:S(2)}, u32[]{:S(2)}) collective-permute-start(bf16[56,768]{1,0:T(8,128)(2,1)S(1)} %get-tuple-element.269), channel_id=1, source_target_pairs={{0,2},{1,3},{2,0},{3,1},{4,6},{5,7},{6,4},{7,5},{8,10},{9,11},{10,... | collective-permute-start | bytes 258056 | tf_op jit(solution)/shard_map/cond/branch_1_fun/ppermute | solution.py:474
  306.9 5.7 %collective-permute-done.13 = bf16[56,768]{1,0:T(8,128)(2,1)S(1)} collective-permute-done((bf16[56,768]{1,0:T(8,128)(2,1)S(1)}, bf16[56,768]{1,0:T(8,128)(2,1)S(1)}, u32[]{:S(2)}, u32[]{:S(2)}) %collective-permute-start.13) | collective-permute-done | bytes 86048 | tf_op jit(solution)/shard_map/cond/branch_1_fun/ppermute | solution.py:474
  316.3 4.1 %collective-permute-done.18 = bf16[56,768]{1,0:T(8,128)(2,1)S(1)} collective-permute-done((bf16[56,768]{1,0:T(8,128)(2,1)S(1)}, bf16[56,768]{1,0:T(8,128)(2,1)S(1)}, u32[]{:S(2)}, u32[]{:S(2)}) %collective-permute-start.18) | collective-permute-done | bytes 86048 | tf_op jit(solution)/shard_map/cond/branch_1_fun/ppermute | solution.py:474
  320.4 4.9 %collective-permute-done.17 = bf16[56,768]{1,0:T(8,128)(2,1)S(1)} collective-permute-done((bf16[56,768]{1,0:T(8,128)(2,1)S(1)}, bf16[56,768]{1,0:T(8,128)(2,1)S(1)}, u32[]{:S(2)}, u32[]{:S(2)}) %collective-permute-start.17) | collective-permute-done | bytes 86048 | tf_op jit(solution)/shard_map/cond/branch_1_fun/ppermute | solution.py:474
  327.2 4.5 %collective-permute-done.19 = bf16[576,768]{1,0:T(8,128)(2,1)S(1)} collective-permute-done((bf16[576,768]{1,0:T(8,128)(2,1)S(1)}, bf16[576,768]{1,0:T(8,128)(2,1)S(1)}, u32[]{:S(2)}, u32[]{:S(2)}) %collective-permute-start.19) | collective-permute-done | bytes 884768 | tf_op jit(solution)/shard_map/cond/branch_1_fun/ppermute | solution.py:465
  334.2 7.8 %collective-permute-done.20 = bf16[224,768]{1,0:T(8,128)(2,1)S(1)} collective-permute-done((bf16[224,768]{1,0:T(8,128)(2,1)S(1)}, bf16[224,768]{1,0:T(8,128)(2,1)S(1)}, u32[]{:S(2)}, u32[]{:S(2)}) %collective-permute-start.20) | collective-permute-done | bytes 344096 | tf_op jit(solution)/shard_map/cond/branch_1_fun/ppermute | solution.py:465
  343.8 9.4 %collective-permute-done.22 = bf16[448,768]{1,0:T(8,128)(2,1)S(1)} collective-permute-done((bf16[448,768]{1,0:T(8,128)(2,1)S(1)}, bf16[448,768]{1,0:T(8,128)(2,1)S(1)}, u32[]{:S(2)}, u32[]{:S(2)}) %collective-permute-start.22) | collective-permute-done | bytes 688160 | tf_op jit(solution)/shard_map/cond/branch_1_fun/ppermute | solution.py:465
  359.3 4.7 %settle_pairs.2 = (f32[768,768]{1,0:T(8,128)}, f32[768,768]{1,0:T(8,128)}, f32[768,768]{1,0:T(8,128)}, f32[768,768]{1,0:T(8,128)}, f32[768,768]{1,0:T(8,128)}) custom-call(s32[32]{0:T(128)S(1)} %fusion.17.place_ref, bf16[2304,768]{1,0:T(8,128)(2,1)S(1)} %pad_maximum_fusion.in_ref), custom_call_target="tpu_custom_call" | custom-call | tf_op jit(solution)/shard_map/cond/branch_1_fun/settle_pairs/pallas_call | solution.py:569
  364.2 4.0 %settle_pairs.3 = (f32[768,768]{1,0:T(8,128)}, f32[768,768]{1,0:T(8,128)}, f32[768,768]{1,0:T(8,128)}, f32[768,768]{1,0:T(8,128)}, f32[24,768]{1,0:T(8,128)}) custom-call(s32[32]{0:T(128)S(1)} %fusion.17.place_ref, bf16[1792,768]{1,0:T(8,128)(2,1)S(1)} %pad_maximum_fusion.1.in_ref, ...), custom_call_target="tpu_custom_call", output_to_operand_aliasing={{0}: (2, {}), {1}: (3, {}), {2}: (4, {}), {3}: (5, {})} | custom-call | tf_op jit(solution)/shard_map/cond/branch_1_fun/settle_pairs/pallas_call | solution.py:569
  375.0 11.4 %widen.1 = (f32[3072,768]{1,0:T(8,128)}, f32[768,3072]{1,0:T(8,128)}) custom-call(bf16[1536,3072]{1,0:T(8,128)(2,1)} %all-reduce.4.cloned.1.call-done.outer_ref.inner_ref, bf16[1536,3072]{1,0:T(8,128)(2,1)} %all-reduce.4.cloned.1.call-done.outer_ref.inner_ref), custom_call_target="tpu_custom_call" | custom-call | tf_op jit(solution)/shard_map/widen/pallas_call | solution.py:664
  (200 shorter events, 87.4 us)
Async XLA Ops:
  7.2 27.4 %all-to-all-start = ((bf16[4,96,768]{2,1,0:T(8,128)(2,1)}), bf16[4,96,768]{2,1,0:T(8,128)(2,1)}, u32[]{:S(2)}, u32[]{:S(2)}) async-start(bf16[4,96,768]{2,1,0:T(8,128)(2,1)} %param.29), calls=%async_computation | async-start | bytes 1179648 | tf_op jit(solution)/shard_map/all_to_all | solution.py:694
  13.7 361.4 %all-reduce.4.cloned.1.call-start = ((), (), s32[]{:S(2)}) async-start(), calls=%async_computation.1 | async-start | bytes 18874368 | tf_op jit(solution)/shard_map/psum | solution.py:741
  206.9 37.9 %collective-permute-start.1 = (bf16[576,768]{1,0:T(8,128)(2,1)S(1)}, bf16[576,768]{1,0:T(8,128)(2,1)S(1)}, u32[]{:S(2)}, u32[]{:S(2)}) collective-permute-start(bf16[576,768]{1,0:T(8,128)(2,1)S(1)} %constant_dynamic-slice_fusion.10), channel_id=1, source_target_pairs={{0,8},{4,20},{8,0},{12,28},{16,24},{20,4},{24,16},{28,12},{1,9},{5... | collective-permute-start | bytes 2654216 | tf_op jit(solution)/shard_map/cond/branch_1_fun/ppermute | solution.py:465
  247.8 8.6 %collective-permute-start.2 = (bf16[896,768]{1,0:T(8,128)(2,1)S(1)}, bf16[896,768]{1,0:T(8,128)(2,1)}, u32[]{:S(2)}, u32[]{:S(2)}) collective-permute-start(bf16[896,768]{1,0:T(8,128)(2,1)S(1)} %constant_dynamic-slice_fusion.9), channel_id=1, source_target_pairs={{0,4},{4,0},{8,12},{12,8},{16,20},{20,16},{24,28},{28,24},{1,5},{5... | collective-permute-start | bytes 4128776 | tf_op jit(solution)/shard_map/cond/branch_1_fun/ppermute | solution.py:465
  248.0 8.4 %collective-permute-start.3 = (bf16[288,768]{1,0:T(8,128)(2,1)S(1)}, bf16[288,768]{1,0:T(8,128)(2,1)S(1)}, u32[]{:S(2)}, u32[]{:S(2)}) collective-permute-start(bf16[288,768]{1,0:T(8,128)(2,1)S(1)} %constant_dynamic-slice_fusion.8), channel_id=1, source_target_pairs={{0,16},{4,12},{8,24},{12,4},{16,0},{20,28},{24,8},{28,20},{1,17},{... | collective-permute-start | bytes 1327112 | tf_op jit(solution)/shard_map/cond/branch_1_fun/ppermute | solution.py:465
  258.7 18.8 %collective-permute-start.4 = (bf16[448,768]{1,0:T(8,128)(2,1)S(1)}, bf16[448,768]{1,0:T(8,128)(2,1)}, u32[]{:S(2)}, u32[]{:S(2)}) collective-permute-start(bf16[448,768]{1,0:T(8,128)(2,1)S(1)} %constant_dynamic-slice_fusion.7), channel_id=1, source_target_pairs={{0,8},{4,20},{8,0},{12,28},{16,24},{20,4},{24,16},{28,12},{1,9},{5... | collective-permute-start | bytes 2064392 | tf_op jit(solution)/shard_map/cond/branch_1_fun/ppermute | solution.py:465
  259.6 9.4 %collective-permute-start.5 = (bf16[72,768]{1,0:T(8,128)(2,1)S(1)}, bf16[72,768]{1,0:T(8,128)(2,1)S(1)}, u32[]{:S(2)}, u32[]{:S(2)}) collective-permute-start(bf16[72,768]{1,0:T(8,128)(2,1)S(1)} %get-tuple-element.264), channel_id=1, source_target_pairs={{0,1},{1,2},{2,3},{3,0},{4,5},{5,6},{6,7},{7,4},{8,9},{9,10},{10,1... | collective-permute-start | bytes 331784 | tf_op jit(solution)/shard_map/cond/branch_1_fun/ppermute | solution.py:474
  262.2 9.7 %collective-permute-start.7 = (bf16[72,768]{1,0:T(8,128)(2,1)S(1)}, bf16[72,768]{1,0:T(8,128)(2,1)S(1)}, u32[]{:S(2)}, u32[]{:S(2)}) collective-permute-start(bf16[72,768]{1,0:T(8,128)(2,1)S(1)} %get-tuple-element.265), channel_id=1, source_target_pairs={{0,3},{1,0},{2,1},{3,2},{4,7},{5,4},{6,5},{7,6},{8,11},{9,8},{10,9... | collective-permute-start | bytes 331784 | tf_op jit(solution)/shard_map/cond/branch_1_fun/ppermute | solution.py:474
  264.0 13.3 %collective-permute-start.6 = (bf16[72,768]{1,0:T(8,128)(2,1)S(1)}, bf16[72,768]{1,0:T(8,128)(2,1)S(1)}, u32[]{:S(2)}, u32[]{:S(2)}) collective-permute-start(bf16[72,768]{1,0:T(8,128)(2,1)S(1)} %get-tuple-element.266), channel_id=1, source_target_pairs={{0,2},{1,3},{2,0},{3,1},{4,6},{5,7},{6,4},{7,5},{8,10},{9,11},{10,... | collective-permute-start | bytes 331784 | tf_op jit(solution)/shard_map/cond/branch_1_fun/ppermute | solution.py:474
  278.7 16.9 %collective-permute-start.8 = (bf16[224,768]{1,0:T(8,128)(2,1)S(1)}, bf16[224,768]{1,0:T(8,128)(2,1)S(1)}, u32[]{:S(2)}, u32[]{:S(2)}) collective-permute-start(bf16[224,768]{1,0:T(8,128)(2,1)S(1)} %constant_dynamic-slice_fusion.3), channel_id=1, source_target_pairs={{0,16},{4,12},{8,24},{12,4},{16,0},{20,28},{24,8},{28,20},{1,17},{... | collective-permute-start | bytes 1032200 | tf_op jit(solution)/shard_map/cond/branch_1_fun/ppermute | solution.py:465
  279.8 9.0 %collective-permute-start.11 = (bf16[72,768]{1,0:T(8,128)(2,1)S(1)}, bf16[72,768]{1,0:T(8,128)(2,1)S(1)}, u32[]{:S(2)}, u32[]{:S(2)}) collective-permute-start(bf16[72,768]{1,0:T(8,128)(2,1)S(1)} %add_convert_fusion.6), channel_id=1, source_target_pairs={{0,3},{1,0},{2,1},{3,2},{4,7},{5,4},{6,5},{7,6},{8,11},{9,8},{10,9... | collective-permute-start | bytes 331784 | tf_op jit(solution)/shard_map/cond/branch_1_fun/ppermute | solution.py:474
  281.1 14.5 %collective-permute-start.10 = (bf16[72,768]{1,0:T(8,128)(2,1)S(1)}, bf16[72,768]{1,0:T(8,128)(2,1)S(1)}, u32[]{:S(2)}, u32[]{:S(2)}) collective-permute-start(bf16[72,768]{1,0:T(8,128)(2,1)S(1)} %add_convert_fusion.6), channel_id=1, source_target_pairs={{0,2},{1,3},{2,0},{3,1},{4,6},{5,7},{6,4},{7,5},{8,10},{9,11},{10,... | collective-permute-start | bytes 331784 | tf_op jit(solution)/shard_map/cond/branch_1_fun/ppermute | solution.py:474
  281.1 14.5 %collective-permute-start.9 = (bf16[72,768]{1,0:T(8,128)(2,1)S(1)}, bf16[72,768]{1,0:T(8,128)(2,1)S(1)}, u32[]{:S(2)}, u32[]{:S(2)}) collective-permute-start(bf16[72,768]{1,0:T(8,128)(2,1)S(1)} %add_convert_fusion.6), channel_id=1, source_target_pairs={{0,1},{1,2},{2,3},{3,0},{4,5},{5,6},{6,7},{7,4},{8,9},{9,10},{10,1... | collective-permute-start | bytes 331784 | tf_op jit(solution)/shard_map/cond/branch_1_fun/ppermute | solution.py:474
  295.7 16.9 %collective-permute-start.15 = (bf16[288,768]{1,0:T(8,128)(2,1)S(1)}, bf16[288,768]{1,0:T(8,128)(2,1)S(1)}, u32[]{:S(2)}, u32[]{:S(2)}) collective-permute-start(bf16[288,768]{1,0:T(8,128)(2,1)S(1)} %pad_maximum_fusion.6), channel_id=1, source_target_pairs={{0,16},{4,12},{8,24},{12,4},{16,0},{20,28},{24,8},{28,20},{1,17},{... | collective-permute-start | bytes 1327112 | tf_op jit(solution)/shard_map/cond/branch_1_fun/ppermute | solution.py:465
  296.9 9.0 %collective-permute-start.12 = (bf16[56,768]{1,0:T(8,128)(2,1)S(1)}, bf16[56,768]{1,0:T(8,128)(2,1)S(1)}, u32[]{:S(2)}, u32[]{:S(2)}) collective-permute-start(bf16[56,768]{1,0:T(8,128)(2,1)S(1)} %get-tuple-element.267), channel_id=1, source_target_pairs={{0,1},{1,2},{2,3},{3,0},{4,5},{5,6},{6,7},{7,4},{8,9},{9,10},{10,1... | collective-permute-start | bytes 258056 | tf_op jit(solution)/shard_map/cond/branch_1_fun/ppermute | solution.py:474
  301.7 10.9 %collective-permute-start.13 = (bf16[56,768]{1,0:T(8,128)(2,1)S(1)}, bf16[56,768]{1,0:T(8,128)(2,1)S(1)}, u32[]{:S(2)}, u32[]{:S(2)}) collective-permute-start(bf16[56,768]{1,0:T(8,128)(2,1)S(1)} %get-tuple-element.269), channel_id=1, source_target_pairs={{0,2},{1,3},{2,0},{3,1},{4,6},{5,7},{6,4},{7,5},{8,10},{9,11},{10,... | collective-permute-start | bytes 258056 | tf_op jit(solution)/shard_map/cond/branch_1_fun/ppermute | solution.py:474
  312.7 19.1 %collective-permute-start.19 = (bf16[576,768]{1,0:T(8,128)(2,1)S(1)}, bf16[576,768]{1,0:T(8,128)(2,1)S(1)}, u32[]{:S(2)}, u32[]{:S(2)}) collective-permute-start(bf16[576,768]{1,0:T(8,128)(2,1)S(1)} %pad_maximum_fusion.4), channel_id=1, source_target_pairs={{0,8},{4,20},{8,0},{12,28},{16,24},{20,4},{24,16},{28,12},{1,9},{5... | collective-permute-start | bytes 2654216 | tf_op jit(solution)/shard_map/cond/branch_1_fun/ppermute | solution.py:465
  312.8 7.6 %collective-permute-start.18 = (bf16[56,768]{1,0:T(8,128)(2,1)S(1)}, bf16[56,768]{1,0:T(8,128)(2,1)S(1)}, u32[]{:S(2)}, u32[]{:S(2)}) collective-permute-start(bf16[56,768]{1,0:T(8,128)(2,1)S(1)} %add_convert_fusion.7), channel_id=1, source_target_pairs={{0,3},{1,0},{2,1},{3,2},{4,7},{5,4},{6,5},{7,6},{8,11},{9,8},{10,9... | collective-permute-start | bytes 258056 | tf_op jit(solution)/shard_map/cond/branch_1_fun/ppermute | solution.py:474
  315.7 9.7 %collective-permute-start.17 = (bf16[56,768]{1,0:T(8,128)(2,1)S(1)}, bf16[56,768]{1,0:T(8,128)(2,1)S(1)}, u32[]{:S(2)}, u32[]{:S(2)}) collective-permute-start(bf16[56,768]{1,0:T(8,128)(2,1)S(1)} %add_convert_fusion.7), channel_id=1, source_target_pairs={{0,2},{1,3},{2,0},{3,1},{4,6},{5,7},{6,4},{7,5},{8,10},{9,11},{10,... | collective-permute-start | bytes 258056 | tf_op jit(solution)/shard_map/cond/branch_1_fun/ppermute | solution.py:474
  315.7 11.5 %collective-permute-start.16 = (bf16[56,768]{1,0:T(8,128)(2,1)S(1)}, bf16[56,768]{1,0:T(8,128)(2,1)S(1)}, u32[]{:S(2)}, u32[]{:S(2)}) collective-permute-start(bf16[56,768]{1,0:T(8,128)(2,1)S(1)} %add_convert_fusion.7), channel_id=1, source_target_pairs={{0,1},{1,2},{2,3},{3,0},{4,5},{5,6},{6,7},{7,4},{8,9},{9,10},{10,1... | collective-permute-start | bytes 258056 | tf_op jit(solution)/shard_map/cond/branch_1_fun/ppermute | solution.py:474
  331.9 10.1 %collective-permute-start.21 = (bf16[1152,768]{1,0:T(8,128)(2,1)S(1)}, bf16[1152,768]{1,0:T(8,128)(2,1)S(1)}, u32[]{:S(2)}, u32[]{:S(2)}) collective-permute-start(bf16[1152,768]{1,0:T(8,128)(2,1)S(1)} %pad_maximum_fusion.2), channel_id=1, source_target_pairs={{0,4},{4,0},{8,12},{12,8},{16,20},{20,16},{24,28},{28,24},{1,5},{5... | collective-permute-start | bytes 5308424 | tf_op jit(solution)/shard_map/cond/branch_1_fun/ppermute | solution.py:465
  332.8 9.1 %collective-permute-start.20 = (bf16[224,768]{1,0:T(8,128)(2,1)S(1)}, bf16[224,768]{1,0:T(8,128)(2,1)S(1)}, u32[]{:S(2)}, u32[]{:S(2)}) collective-permute-start(bf16[224,768]{1,0:T(8,128)(2,1)S(1)} %pad_maximum_fusion.7), channel_id=1, source_target_pairs={{0,16},{4,12},{8,24},{12,4},{16,0},{20,28},{24,8},{28,20},{1,17},{... | collective-permute-start | bytes 1032200 | tf_op jit(solution)/shard_map/cond/branch_1_fun/ppermute | solution.py:465
  342.3 11.0 %collective-permute-start.22 = (bf16[448,768]{1,0:T(8,128)(2,1)S(1)}, bf16[448,768]{1,0:T(8,128)(2,1)S(1)}, u32[]{:S(2)}, u32[]{:S(2)}) collective-permute-start(bf16[448,768]{1,0:T(8,128)(2,1)S(1)} %pad_maximum_fusion.5), channel_id=1, source_target_pairs={{0,8},{4,20},{8,0},{12,28},{16,24},{20,4},{24,16},{28,12},{1,9},{5... | collective-permute-start | bytes 2064392 | tf_op jit(solution)/shard_map/cond/branch_1_fun/ppermute | solution.py:465
  353.4 10.6 %collective-permute-start.23 = (bf16[896,768]{1,0:T(8,128)(2,1)S(1)}, bf16[896,768]{1,0:T(8,128)(2,1)S(1)}, u32[]{:S(2)}, u32[]{:S(2)}) collective-permute-start(bf16[896,768]{1,0:T(8,128)(2,1)S(1)} %pad_maximum_fusion.3), channel_id=1, source_target_pairs={{0,4},{4,0},{8,12},{12,8},{16,20},{20,16},{24,28},{28,24},{1,5},{5... | collective-permute-start | bytes 4128776 | tf_op jit(solution)/shard_map/cond/branch_1_fun/ppermute | solution.py:465
  (43 other events, 318.6 us)
Sparse Core Ops, SparseCore 0:
  153.1 208.7 all-reduce.3

commit v5 on v4

--- a/solution.py
+++ b/solution.py
@@ -1,3 +1,5 @@
+import functools
+
 import jax
 import jax.numpy as jnp
 from jax import lax
@@ -44,12 +46,33 @@
     return jnp.concatenate([ref[pl.ds(start, SUB), :] for start in spans], axis=0)
 
 
+def spread(row_ref, out_ref):
+    for at in range(0, SEG, SUB):
+        block = jnp.broadcast_to(row_ref[:, at : at + SUB], (SUB, SUB))
+        out_ref[at : at + SUB, :] = block.T
+
+
+def twice_rows(ref, tile):
+    rows = ref[pl.ds(pl.multiple_of(tile * SUB, SUB), SUB), :]
+    return jnp.concatenate([rows, rows], axis=0)
+
+
+def key_segment_zero(seg_col):
+    return jnp.concatenate([jnp.ones((MEM, PAIR), jnp.bool_), seg_col[...] == 0], axis=0)
+
+
 def forward_kernel(
-    qc_ref, qp_ref, qs_ref, k_ref, v_ref, rel_ref, emb_ref, side_ref, key_side_ref, krank_ref,
-    mix_ref, inv_ref, prob_ref, kcat, vcat,
+    length_ref, qc_ref, qp_ref, qs_ref, k_ref, v_ref, rel_ref, emb_ref, seg_ref, rank_ref,
+    mix_ref, inv_ref, prob_ref, kcat, vcat, seg_col, rank_col,
 ):
-    low_keys = lane_low(KEYS)
-    same = key_side_ref[:, 0:1] == 0
+    @pl.when(pl.program_id(0) == 0)
+    def _():
+        spread(seg_ref, seg_col)
+        spread(rank_ref, rank_col)
+
+    same = key_segment_zero(seg_col)
+    live = lax.broadcasted_iota(jnp.int32, (1, SEG), 1) < length_ref[0]
+    krank = jnp.where(live, rank_ref[...], 2 * SEG)
     zero_row = emb_ref[0:1, :].astype(jnp.float32)
     one_row = emb_ref[1:2, :].astype(jnp.float32)
     zero_roll = pltpu.roll(zero_row, HEAD, 1)
@@ -75,9 +98,11 @@
         qp = both_rows(qp_ref, spans)
         qs = both_rows(qs_ref, spans)
         qs_roll = pltpu.roll(qs.astype(jnp.float32), HEAD, 1).astype(jnp.bfloat16)
-        side = both_rows(side_ref, spans)
-        seg_keep = (side[:, 0:1] == 0) == low
-        krank = krank_ref[...]
+        seg_keep = (twice_rows(seg_col, tile) == 0) == low
+        rank = twice_rows(rank_col, tile) - jnp.where(
+            lax.broadcasted_iota(jnp.int32, (ROWS, PAIR), 0) < SUB, 0, 1
+        )
+        rank = jnp.concatenate([rank] * (SEG // PAIR), axis=1)
         factor = SCALE * LOG2E
         window = rel_ref[pl.ds(3 - tile, WIN // SUB)].reshape(WIN, PAIR)
         grid = mm(
@@ -98,7 +123,7 @@
                     WIN - SUB + 1 + at, 1, stride=1, stride_axis=0,
                 )[:, :KEYS]
                 logit = score[row : row + CHUNK] + shifted
-                current = jnp.where(krank <= side[row : row + CHUNK, 1:2], logit[:, MEM:], FAR)
+                current = jnp.where(krank <= rank[row : row + CHUNK], logit[:, MEM:], FAR)
                 logit = jnp.concatenate([logit[:, :MEM], current], axis=1)
                 top = jnp.max(logit, axis=-1, keepdims=True)
                 soft = jnp.exp2((logit - top) * factor).astype(jnp.bfloat16)
@@ -121,15 +146,16 @@
     return pl.BlockSpec((rows, lanes), lambda p: (0, 0))
 
 
-def attention_forward(qc, qp, qs, keys, values, rel, emb, side, key_side, krank):
+def attention_forward(length, qc, qp, qs, keys, values, rel, emb, seg, rank):
     pair = lambda rows: pl.BlockSpec((rows, PAIR), lambda p: (0, p))
     return pl.pallas_call(
         forward_kernel,
         grid=(PAIRS,),
         in_specs=[
+            pl.BlockSpec(memory_space=pltpu.SMEM),
             pair(2 * SEG), pair(2 * SEG), pair(2 * SEG), pair(KEYS), pair(KEYS),
             pl.BlockSpec((REL // SUB, SUB, PAIR), lambda p: (0, 0, p)),
-            pair(2), whole(*side.shape), whole(*key_side.shape), whole(1, SEG),
+            pair(2), whole(1, SEG), whole(1, SEG),
         ],
         out_specs=[
             pair(2 * SEG), pair(2 * SEG),
@@ -143,6 +169,8 @@
         scratch_shapes=[
             pltpu.VMEM((2, KEYS, 2 * PAIR), jnp.bfloat16),
             pltpu.VMEM((KEYS, 2 * PAIR), jnp.bfloat16),
+            pltpu.VMEM((SEG, PAIR), jnp.int32),
+            pltpu.VMEM((SEG, PAIR), jnp.int32),
         ],
         compiler_params=pltpu.CompilerParams(
             dimension_semantics=("arbitrary",), vmem_limit_bytes=VMEM_BYTES
@@ -151,16 +179,21 @@
             flops=30000000000, transcendentals=11000000, bytes_accessed=30000000
         ),
         name="attention_forward",
-    )(qc, qp, qs, keys, values, rel.reshape(REL // SUB, SUB, D), emb, side, key_side, krank)
+    )(length, qc, qp, qs, keys, values, rel.reshape(REL // SUB, SUB, D), emb, seg, rank)
 
 
 def backward_kernel(
     prob_ref, dmix_ref, mix_ref, inv_ref, qc_ref, qp_ref, qs_ref, k_ref, v_ref, rel_ref, emb_ref,
-    side_ref, key_side_ref, inputs_ref, frame_ref, positions_ref, *rest,
+    seg_ref, inputs_ref, frame_ref, positions_ref, *rest,
 ):
-    dproj_ref, dk_ref, dv_ref, small_ref, bucket_ref, kcat, dk_acc, dv_acc, drel_acc = rest[-9:]
+    dproj_ref, dk_ref, dv_ref, small_ref, bucket_ref, kcat, dk_acc, dv_acc, drel_acc, seg_col = rest[-10:]
+
+    @pl.when(pl.program_id(0) == 0)
+    def _():
+        spread(seg_ref, seg_col)
+
     kcat[:, :PAIR] = k_ref[...]
-    kcat[:, PAIR:] = jnp.where((key_side_ref[:, 0:1] == 0) == lane_low(KEYS), 1.0, 0.0).astype(
+    kcat[:, PAIR:] = jnp.where(key_segment_zero(seg_col) == lane_low(KEYS), 1.0, 0.0).astype(
         jnp.bfloat16
     )
     dk_acc[...] = jnp.zeros_like(dk_acc)
@@ -187,7 +220,7 @@
         qp = both_rows(qp_ref, spans)
         qs = both_rows(qs_ref, spans).astype(jnp.float32)
         qp_turned = mm(flip, qp, nn).astype(jnp.bfloat16)
-        first = both_rows(side_ref, spans)[:, 0:1] == 0
+        first_rows = twice_rows(seg_col, tile) == 0
         emb = emb_ref[...].astype(jnp.float32)
         dm = jnp.concatenate([jnp.where(low, dmix, zero), jnp.where(low, zero, dmix)], axis=0)
         qc_both = jnp.concatenate([jnp.where(low, qc, zero), jnp.where(low, zero, qc)], axis=0)
@@ -247,8 +280,8 @@
         rolled = [pltpu.roll(part, HEAD, 1) for part in sums]
         key_zero = jnp.where(low, sums[0], rolled[1])
         key_one = jnp.where(low, rolled[0], sums[1])
-        near = jnp.where(first, key_zero, key_one)
-        other = jnp.where(first, key_one, key_zero)
+        near = jnp.where(first_rows, key_zero, key_one)
+        other = jnp.where(first_rows, key_one, key_zero)
         dqs_wide = (near * emb[0:1] + other * emb[1:2]).astype(jnp.bfloat16).astype(jnp.float32)
         dproj = (dqc_wide + dqp_wide + dqs_wide).astype(jnp.bfloat16)
         for index, start in enumerate(spans):
@@ -275,8 +308,8 @@
 
 
 def attention_backward(
-    first, count, bucket_block, chain, prob, dmix, mix, inv, qc, qp, qs, keys, values, rel, emb, side,
-    key_side, inputs, frame, positions,
+    first, count, bucket_block, chain, prob, dmix, mix, inv, qc, qp, qs, keys, values, rel, emb, seg,
+    inputs, frame, positions,
 ):
     pair = lambda rows: pl.BlockSpec((rows, PAIR), lambda p: (0, first + p))
     rel_block = pl.BlockSpec((REL // SUB, SUB, PAIR), lambda p: (0, 0, first + p))
@@ -289,7 +322,7 @@
         in_specs=[
             pl.BlockSpec((None, 2, 2 * SEG, KEYS), lambda p: (first + p, 0, 0, 0)),
             pair(2 * SEG), pair(2 * SEG), pair(2 * SEG), pair(2 * SEG), pair(2 * SEG), pair(2 * SEG),
-            pair(KEYS), pair(KEYS), rel_block, pair(2), whole(*side.shape), whole(*key_side.shape),
+            pair(KEYS), pair(KEYS), rel_block, pair(2), whole(1, SEG),
             whole(2 * SEG, D), whole(KEYS, D), whole(REL, D),
         ]
         + [pl.BlockSpec(memory_space=pl.ANY)] * len(passed),
@@ -309,8 +342,9 @@
             pltpu.VMEM((PAIR, KEYS), jnp.float32),
             pltpu.VMEM((PAIR, KEYS), jnp.float32),
             pltpu.VMEM((REL // SUB, PAIR, SUB), jnp.float32),
-        ],
-        input_output_aliases={16 + index: at for index, at in enumerate(places)},
+            pltpu.VMEM((SEG, PAIR), jnp.int32),
+        ],
+        input_output_aliases={15 + index: at for index, at in enumerate(places)},
         compiler_params=pltpu.CompilerParams(
             dimension_semantics=("arbitrary",), vmem_limit_bytes=VMEM_BYTES
         ),
@@ -319,8 +353,8 @@
         ),
         name="attention_backward",
     )(
-        prob, dmix, mix, inv, qc, qp, qs, keys, values, rel.reshape(REL // SUB, SUB, D), emb, side,
-        key_side, inputs, frame, positions, *passed,
+        prob, dmix, mix, inv, qc, qp, qs, keys, values, rel.reshape(REL // SUB, SUB, D), emb, seg,
+        inputs, frame, positions, *passed,
     )
 
 
@@ -546,7 +580,7 @@
     return in_ref[pl.ds(start, rows), :].astype(jnp.float32)
 
 
-def settle_pairs_kernel(place_ref, in_ref, *rest):
+def settle_pairs_kernel(count, place_ref, in_ref, *rest):
     outs, full = rest[-6:-1], rest[-1]
     rows = in_ref.shape[0] // place_ref.shape[0]
 
@@ -554,7 +588,7 @@
     def _():
         for item in range(place_ref.shape[0]):
             full[item * rows : (item + 1) * rows, :] = block_of(place_ref, in_ref, item)
-        grads = PAIRS // 2 * 4 * PAIR
+        grads = count * 4 * PAIR
         outs[4][...] = full[grads : grads + outs[4].shape[0], :]
 
     for index in range(4):
@@ -567,7 +601,7 @@
     rows, lanes = tensor.shape
     square = jax.ShapeDtypeStruct((D, D), jnp.float32)
     return pl.pallas_call(
-        settle_pairs_kernel,
+        functools.partial(settle_pairs_kernel, count),
         grid_spec=pltpu.PrefetchScalarGridSpec(
             num_scalar_prefetch=1,
             grid=(count,),
@@ -601,57 +635,11 @@
 
 
 EXTRA = 256
+FIRST = 3
 VECTORS = 24
 
 
 WIDE = 512
-
-
-def wide_grads_kernel(outer_ref, active_ref, low_ref, inner_ref, out_ref, left):
-    part = pl.program_id(0)
-
-    @pl.when(pl.program_id(1) == 0)
-    def _():
-        @pl.when(part == 0)
-        def _():
-            left[...] = outer_ref[...].T
-
-        @pl.when(part == 1)
-        def _():
-            left[...] = low_ref[...].T
-
-    @pl.when(part == 0)
-    def _():
-        out_ref[...] = mm(left[...], active_ref[...], nn).astype(jnp.bfloat16)
-
-    @pl.when(part == 1)
-    def _():
-        out_ref[...] = mm(left[...], inner_ref[...], nn).astype(jnp.bfloat16)
-
-
-def wide_grads(grad_outer, active, normed_low, grad_inner):
-    tokens, hidden = active.shape
-    steps = hidden // WIDE
-    return pl.pallas_call(
-        wide_grads_kernel,
-        grid=(2, steps),
-        in_specs=[
-            pl.BlockSpec((tokens, D), lambda p, i: (0, 0)),
-            pl.BlockSpec((tokens, WIDE), lambda p, i: (0, jnp.where(p == 0, i, steps - 1))),
-            pl.BlockSpec((tokens, D), lambda p, i: (0, 0)),
-            pl.BlockSpec((tokens, WIDE), lambda p, i: (0, jnp.where(p == 0, 0, i))),
-        ],
-        out_specs=pl.BlockSpec((D, WIDE), lambda p, i: (p, i)),
-        out_shape=jax.ShapeDtypeStruct((2 * D, hidden), jnp.bfloat16),
-        scratch_shapes=[pltpu.VMEM((D, tokens), jnp.bfloat16)],
-        compiler_params=pltpu.CompilerParams(
-            dimension_semantics=("arbitrary",) * 2, vmem_limit_bytes=VMEM_BYTES
-        ),
-        cost_estimate=pl.CostEstimate(
-            flops=9700000000, transcendentals=0, bytes_accessed=25000000
-        ),
-        name="wide_grads",
-    )(grad_outer, active, normed_low, grad_inner)
 
 
 def widen_kernel(outer_ref, inner_ref, outer_out, inner_out):
@@ -659,14 +647,14 @@
     inner_out[...] = inner_ref[...].astype(jnp.float32)
 
 
-def widen(summed):
-    hidden = summed.shape[1]
+def widen(outer, inner):
+    hidden = inner.shape[1]
     return pl.pallas_call(
         widen_kernel,
         grid=(hidden // WIDE,),
         in_specs=[
             pl.BlockSpec((D, WIDE), lambda i: (0, i)),
-            pl.BlockSpec((D, WIDE), lambda i: (1, i)),
+            pl.BlockSpec((D, WIDE), lambda i: (0, i)),
         ],
         out_specs=[
             pl.BlockSpec((WIDE, D), lambda i: (i, 0)),
@@ -678,7 +666,7 @@
         ],
         compiler_params=pltpu.CompilerParams(vmem_limit_bytes=VMEM_BYTES),
         name="widen",
-    )(summed, summed)
+    )(outer, inner)
 
 
 def shards(
@@ -695,21 +683,6 @@
     content = content_in[0]
     inputs = jnp.concatenate([content, query_in[0]], axis=0)
     cotangent = jnp.concatenate([content_cotangent[0], query_cotangent[0]], axis=0)
-    segment = segment_ids[0]
-    rank = order_rank[0]
-    zeros = jnp.zeros((2 * SEG, 6), jnp.int32)
-    side = jnp.concatenate(
-        [
-            jnp.concatenate([segment, segment])[:, None],
-            jnp.concatenate([rank, rank - 1])[:, None],
-            zeros,
-        ],
-        axis=1,
-    )
-    key_side = jnp.concatenate([jnp.zeros((MEM, 8), jnp.int32), side[:SEG]], axis=0)
-    live = jnp.arange(SEG, dtype=jnp.int32) < sequence_lengths[0]
-    key_rank = jnp.where(live, rank, 2 * SEG)[None, :]
-
     positions = sinusoid()
     relative = low(mm(positions, w_rel, nn))
     frame = jnp.concatenate([past, content], axis=0)
@@ -720,8 +693,8 @@
     query_position = low(projected + wide(bias_position))
     query_segment = low(projected + wide(bias_segment))
     mixture, inverse, probs = attention_forward(
-        query_content, query_position, query_segment, keys, values, relative, segment_embed,
-        side, key_side, key_rank,
+        sequence_lengths, query_content, query_position, query_segment, keys, values, relative,
+        segment_embed, segment_ids, order_rank,
     )
     rows = jnp.stack(
         [wide(t) for t in (gain_one, shift_one, gain_two, shift_two, bias_outer)]
@@ -734,78 +707,80 @@
         inputs, mixture, cotangent, w_out, w_inner, w_outer, wide(bias_inner)[None], rows
     )
     low_mm = lambda left, right: low(mm(left, right, tn))
-    wide_sum = wide_grads(grad_outer_low, active_low, normed_low, grad_inner_low)
-    wide_sum, grad_mixture, grad_attended = lax.optimization_barrier(
-        (wide_sum, grad_mixture, grad_attended)
-    )
-    wide_sum = lax.psum(wide_sum, both)
+    grad_outer_w = low_mm(grad_outer_low, active_low)
+    grad_inner_w = low_mm(normed_low, grad_inner_low)
+    grad_outer_w, grad_inner_w, grad_mixture, grad_attended = lax.optimization_barrier(
+        (grad_outer_w, grad_inner_w, grad_mixture, grad_attended)
+    )
+    outer_sum, inner_sum = lax.psum((grad_outer_w, grad_inner_w), both)
+
     def attention_part(operands):
         (
             probs, grad_mixture, mixture, inverse, query_content, query_position, query_segment,
-            keys, values, relative, side, key_side, inputs, frame, positions, grad_attended,
-            token_sums, inner_bias_sum, segment_embed, grad_residual, w_query, w_key, w_value,
+            keys, values, relative, segment_ids, inputs, frame, positions, grad_attended,
+            token_sums, inner_bias_sum, segment_embed, grad_residual, w_query, w_key, w_value, final_out,
         ) = operands
         common = (
             mixture, inverse, query_content, query_position, query_segment, keys, values, relative,
-            segment_embed, side, key_side, inputs, frame, positions,
-        )
-        half = PAIRS // 2
-        group_rows = half * 4 * PAIR
+            segment_embed, segment_ids, inputs, frame, positions,
+        )
+        rows_of_pairs = lambda count: count * 4 * PAIR
+        half, other = FIRST, PAIRS - FIRST
         chain = attention_backward(
-            0, half, 0, [None] * 4 + [group_rows + D], probs, grad_mixture, *common
-        )
-        early = Sum(lax.dynamic_update_slice(chain[4], low_mm(mixture, grad_attended), (group_rows, 0)))
+            0, half, 0, [None] * 4 + [rows_of_pairs(half) + D], probs, grad_mixture, *common
+        )
+        early = Sum(lax.dynamic_update_slice(chain[4], low_mm(mixture, grad_attended), (rows_of_pairs(half), 0)))
         early.step()
         chain, grad_mixture = together([early], (list(chain[:4]), grad_mixture))
         early.step()
         chain = attention_backward(
-            half, half, 0, chain + [group_rows + EXTRA], probs, grad_mixture, *common
+            half, other, 0, chain + [rows_of_pairs(other) + EXTRA], probs, grad_mixture, *common
         )
         grad_projected, grad_keys, grad_values, small, bucket = together([early], list(chain))
         vectors = jnp.concatenate(
             [token_sums, inner_bias_sum.reshape(-1, D), jnp.zeros((4, D), jnp.float32), small], axis=0
         )
         vectors = jnp.pad(vectors, ((0, EXTRA - vectors.shape[0]), (0, 0)))
-        late = Sum(lax.dynamic_update_slice(bucket, low(vectors), (group_rows, 0)))
+        late = Sum(lax.dynamic_update_slice(bucket, low(vectors), (rows_of_pairs(other), 0)))
         while late.at < late.stages:
             late.step()
             if early.at < early.stages:
                 early.step()
                 together([late, early], ())
-        *sums, out_sum = settle_pairs(early, 0, half, (), D)
-        *sums, vectors = settle_pairs(late, half, half, sums, VECTORS)
+                if early.at == early.stages:
+                    *sums, out_sum = settle_pairs(early, 0, half, (), D)
+                    sums, out_sum = together([late], (sums, out_sum))
+        *sums, vectors = settle_pairs(late, half, other, sums, VECTORS)
+        vectors = [vectors[index] for index in (16, 17, 18)] + [vectors[19:21]] + [
+            vectors[index] for index in (0, 1, 4, 2, 3)
+        ] + [vectors[8:12].reshape(-1)]
+        finals = (final_out[None, :SEG], final_out[None, SEG:])
         grad_inputs = grad_residual + mm(grad_projected, w_query, nt)
         grad_content = (
             grad_inputs[:SEG] + mm(grad_keys[MEM:], w_key, nt) + mm(grad_values[MEM:], w_value, nt)
         )
-        return low(grad_content), low(grad_inputs[SEG:]), sums, out_sum, vectors
+        return low(grad_content), low(grad_inputs[SEG:]), sums, out_sum, vectors, finals
 
     operands = (
         probs, grad_mixture, mixture, inverse, query_content, query_position, query_segment, keys,
-        values, relative, side, key_side, inputs, frame, positions, grad_attended, token_sums,
-        inner_bias_sum, segment_embed, grad_residual, w_query, w_key, w_value,
+        values, relative, segment_ids, inputs, frame, positions, grad_attended, token_sums,
+        inner_bias_sum, segment_embed, grad_residual, w_query, w_key, w_value, final_out,
     )
     shapes = jax.eval_shape(attention_part, operands)
-    grad_content, grad_query, sums, out_sum, vectors = lax.cond(
+    grad_content, grad_query, sums, out_sum, vectors, finals = lax.cond(
         sequence_lengths[0] > -1,
         attention_part,
         lambda operands: jax.tree.map(lambda item: jnp.zeros(item.shape, item.dtype), shapes),
         operands,
     )
     query_sum, key_sum, value_sum, rel_sum = sums
-    outer_sum, inner_sum = widen(wide_sum)
-    pieces = {
-        "gain1": vectors[0], "shift1": vectors[1], "gain2": vectors[2], "shift2": vectors[3],
-        "outer": vectors[4], "inner": vectors[8:12].reshape(-1), "content": vectors[16],
-        "position": vectors[17], "segment": vectors[18], "embed": vectors[19:21],
-    }
+    outer_sum, inner_sum = widen(outer_sum, inner_sum)
+    content_sum, position_sum, segment_sum, embed_sum, gain1, shift1, bias, gain2, shift2, hidden = vectors
     return (
-        low(final_out[None, :SEG]), low(final_out[None, SEG:]),
-        grad_content[None], grad_query[None],
+        *finals, grad_content[None], grad_query[None],
         query_sum, key_sum, value_sum, out_sum, rel_sum,
-        pieces["content"], pieces["position"], pieces["segment"], pieces["embed"].reshape(2, D),
-        pieces["gain1"], pieces["shift1"], inner_sum, pieces["inner"], outer_sum, pieces["outer"],
-        pieces["gain2"], pieces["shift2"],
+        content_sum, position_sum, segment_sum, embed_sum, gain1, shift1, inner_sum, hidden,
+        outer_sum, bias, gain2, shift2,
     )
 
 

time: 400 us -> 382 us (0.955)
  Pallas kernels: 204 us -> 184 us
  matrix products: 22.6 us -> 38.8 us
  local copies, waits for them, and re-layouts: 17.3 us -> 9.26 us
  other arithmetic: 21.5 us -> 16.9 us
    pallas_call x4 -> x3, Pallas kernels: 77.7 us -> 57.4 us  [the longest x1 48.8 us: attention_forward(): pl.pallas_call(forward_kernel, grid=(PAIRS,), in_specs=[pl.BlockSpec(memo...]
    dot_general x8 -> x10, matrix products: 22.6 us -> 38.8 us  [mm(): lax.dot_general(left, right, dims, preferred_element_type=jnp.float32)]
  transfers between devices with their start and end apart: 26 -> 26, of which waited for: 15 -> 16; matrix products, arithmetic and copies ran while one was open for 13% -> 10% of each run, Pallas kernels for 21% -> 22%
where the time goes in v5:
time: 382 us; the launch traced here: 376 us
  Pallas kernels  184 us (48%)
  waiting for transfers between devices  72.4 us (19%)
  matrix products  38.8 us (10%)
  starting transfers between devices  38.5 us (10%)
  other arithmetic  16.9 us (4%)
  between operations  15.5 us (4%)
  local copies, waits for them, and re-layouts  9.26 us (2%)
    pallas_call x2, Pallas kernels, attention_backward(): pl.pallas_call(backward_kernel, grid=(count,), in_specs=[pl.BlockSpec((No...  73.2 us
    pallas_call x1, Pallas kernels, attention_forward(): pl.pallas_call(forward_kernel, grid=(PAIRS,), in_specs=[pl.BlockSpec(memo...  48.8 us
    pallas_call x1, Pallas kernels, token_layer(): pl.pallas_call(token_kernel, grid=(count // TOKENS,), in_specs=[tile(D),...  41.9 us
    ppermute x12, waiting for transfers between devices, along(): lax.ppermute(tensor, 'mem', [(i, (i + shift) % ring) for i in range(ring)])  41.8 us
    dot_general x10, matrix products, mm(): lax.dot_general(left, right, dims, preferred_element_type=jnp.float32)  38.8 us
    ppermute x12, waiting for transfers between devices, across(): lax.ppermute(tensor, 'batch', [(i, i ^ bits[i & 1]) for i in range(count)])  29.1 us
    ppermute x12, starting transfers between devices, along(): lax.ppermute(tensor, 'mem', [(i, (i + shift) % ring) for i in range(ring)])  18.1 us
    ppermute x12, starting transfers between devices, across(): lax.ppermute(tensor, 'batch', [(i, i ^ bits[i & 1]) for i in range(count)])  13.9 us
  transfers between devices with their start and end apart: 26, of which 16 were waited for; matrix products, arithmetic and copies ran while one was open for 10% of the time, Pallas kernels for 22%

profile of v5, /device:TPU:0, one launch (start us, length us, event | category | flops | bytes accessed | tf_op | source)
XLA Modules:
  0.0 375.9 jit_solution(4421406346756706886)
XLA Ops:
  7.2 6.5 %all-to-all-start = ((bf16[4,96,768]{2,1,0:T(8,128)(2,1)}), bf16[4,96,768]{2,1,0:T(8,128)(2,1)}, u32[]{:S(2)}, u32[]{:S(2)}) async-start(bf16[4,96,768]{2,1,0:T(8,128)(2,1)} %param.29), calls=%async_computation | async-start | bytes 1179648 | tf_op jit(solution)/shard_map/all_to_all | solution.py:682
  29.7 3.9 %convolution_convert_fusion.5.k_ref = bf16[896,768]{1,0:T(8,128)(2,1)} fusion(bf16[768,768]{1,0:T(8,128)(2,1)} %param.34, bf16[512,768]{1,0:T(8,128)(2,1)S(1)} %bitcast.39, bf16[384,768]{1,0:T(8,128)(2,1)} %bitcast.10), kind=kOutput, calls=%fused_computation.113 | convolution fusion | flops 1060405248 | bytes 3932160 | tf_op jit(solution)/shard_map/dot_general | solution.py:33
  37.0 48.8 %attention_forward.1 = (bf16[1024,768]{1,0:T(8,128)(2,1)}, f32[1024,768]{1,0:T(8,128)}, bf16[6,2,1024,896]{3,2,1,0:T(8,128)(2,1)}) custom-call(s32[1]{0:T(128)S(6)} %copy.104.length_ref, bf16[1024,768]{1,0:T(8,128)(2,1)} %get-tuple-element.238.qc_ref, bf16[1024,768]{1,0:T(8,128)(2,1)} %get-tuple-element.237.qp_ref, ...), custom_call_target="tpu_custom_call" | custom-call | flops 30000001024 | bytes 30000000 | tf_op jit(solution)/shard_map/attention_forward/pallas_call | solution.py:151
  85.8 41.9 %token_layer.1 = (bf16[1024,768]{1,0:T(8,128)(2,1)}, bf16[1024,3072]{1,0:T(8,128)(2,1)}, bf16[1024,768]{1,0:T(8,128)(2,1)}, bf16[1024,3072]{1,0:T(8,128)(2,1)}, ...) custom-call(bf16[1024,768]{1,0:T(8,128)(2,1)} %pad_maximum_fusion.10, ...), custom_call_target="tpu_custom_call" | custom-call | flops 22000001024 | bytes 40000000 | tf_op jit(solution)/shard_map/token_layer/pallas_call | solution.py:456
  127.7 9.6 %convolution_convert_fusion.2 = bf16[768,3072]{1,0:T(8,128)(2,1)} fusion(bf16[1024,768]{1,0:T(8,128)(2,1)} %get-tuple-element.182, bf16[1024,3072]{1,0:T(8,128)(2,1)} %get-tuple-element.183), kind=kOutput, calls=%fused_computation.104 | convolution fusion | flops 4834197504 | bytes 12582912 | tf_op jit(solution)/shard_map/dot_general | solution.py:33
  137.3 6.8 %convolution_convert_fusion.1 = bf16[768,3072]{1,0:T(8,128)(2,1)} fusion(bf16[1024,768]{1,0:T(8,128)(2,1)S(1)} %copy-done.43, bf16[1024,3072]{1,0:T(8,128)(2,1)S(1)} %copy-done.42), kind=kOutput, calls=%fused_computation.103 | convolution fusion | flops 4834197504 | bytes 12582912 | tf_op jit(solution)/shard_map/dot_general | solution.py:33
  148.0 209.2 %conditional.1 = (f32[768,768]{1,0:T(8,128)}, f32[768,768]{1,0:T(8,128)}, f32[768,768]{1,0:T(8,128)}, f32[768,768]{1,0:T(8,128)}, f32[768,768]{1,0:T(8,128)}, /*...) conditional(s32[]{:T(128)} %bitcast.5, () %tuple.30, ...), branch_computations={%region_0.0_spmd, %region_1.0_spmd} | conditional | flops 51666313216 | bytes 237361696 | solution.py:770
  148.0 36.9 %attention_backward.2 = (bf16[1024,768]{1,0:T(8,128)(2,1)}, bf16[896,768]{1,0:T(8,128)(2,1)}, bf16[896,768]{1,0:T(8,128)(2,1)}, f32[8,768]{1,0:T(8,128)}, bf16[2304,768]{1,0:T(8,128)(2,1)}) custom-call(bf16[6,2,1024,896]{3,2,1,0:T(8,128)(2,1)} %get-tuple-element.48.prob_ref, bf16[1024,768]{1,0:T(8,128)(2,1)} %get-tuple-element.70.dmix_ref, ...), custom_call_target="tpu_custom_call" | custom-call | flops 24000000000 | bytes 24000000 | tf_op jit(solution)/shard_map/cond/branch_1_fun/attention_backward/pallas_call | solution.py:319
  184.9 4.4 %fusion.2 = bf16[2304,768]{1,0:T(8,128)(2,1)} fusion(bf16[2304,768]{1,0:T(8,128)(2,1)} %get-tuple-element.63, bf16[1024,768]{1,0:T(8,128)(2,1)} %get-tuple-element.50.mix_ref, bf16[1024,768]{1,0:T(8,128)(2,1)} %get-tuple-element.64), kind=kOutput, calls=%fused_computation.12 | convolution fusion | flops 1208549376 | bytes 4325376 | tf_op jit(solution)/shard_map/cond/branch_1_fun/dot_general | solution.py:33
  199.0 36.3 %attention_backward.3 = (bf16[1024,768]{1,0:T(8,128)(2,1)}, bf16[896,768]{1,0:T(8,128)(2,1)}, bf16[896,768]{1,0:T(8,128)(2,1)}, f32[8,768]{1,0:T(8,128)}, bf16[1792,768]{1,0:T(8,128)(2,1)}) custom-call(bf16[6,2,1024,896]{3,2,1,0:T(8,128)(2,1)} %get-tuple-element.48.prob_ref, ...), custom_call_target="tpu_custom_call", output_to_operand_aliasing={{0}: (15, {}), {1}: (16, {}), {2}: (17, {}), {3}: (18, {})} | custom-call | flops 24000000000 | bytes 24000000 | tf_op jit(solution)/shard_map/cond/branch_1_fun/attention_backward/pallas_call | solution.py:319
  240.1 6.8 %collective-permute-done.3 = bf16[288,768]{1,0:T(8,128)(2,1)S(1)} collective-permute-done((bf16[288,768]{1,0:T(8,128)(2,1)S(1)}, bf16[288,768]{1,0:T(8,128)(2,1)S(1)}, u32[]{:S(2)}, u32[]{:S(2)}) %collective-permute-start.3) | collective-permute-done | bytes 442400 | tf_op jit(solution)/shard_map/cond/branch_1_fun/ppermute | solution.py:499
  254.4 5.0 %collective-permute-done.5 = bf16[72,768]{1,0:T(8,128)(2,1)S(1)} collective-permute-done((bf16[72,768]{1,0:T(8,128)(2,1)S(1)}, bf16[72,768]{1,0:T(8,128)(2,1)S(1)}, u32[]{:S(2)}, u32[]{:S(2)}) %collective-permute-start.5) | collective-permute-done | bytes 110624 | tf_op jit(solution)/shard_map/cond/branch_1_fun/ppermute | solution.py:508
  261.3 5.4 %collective-permute-done.6 = bf16[72,768]{1,0:T(8,128)(2,1)S(1)} collective-permute-done((bf16[72,768]{1,0:T(8,128)(2,1)S(1)}, bf16[72,768]{1,0:T(8,128)(2,1)S(1)}, u32[]{:S(2)}, u32[]{:S(2)}) %collective-permute-start.6) | collective-permute-done | bytes 110624 | tf_op jit(solution)/shard_map/cond/branch_1_fun/ppermute | solution.py:508
  271.2 6.2 %collective-permute-done.11 = bf16[72,768]{1,0:T(8,128)(2,1)S(1)} collective-permute-done((bf16[72,768]{1,0:T(8,128)(2,1)S(1)}, bf16[72,768]{1,0:T(8,128)(2,1)S(1)}, u32[]{:S(2)}, u32[]{:S(2)}) %collective-permute-start.11) | collective-permute-done | bytes 110624 | tf_op jit(solution)/shard_map/cond/branch_1_fun/ppermute | solution.py:508
  277.3 7.4 %collective-permute-done.10 = bf16[72,768]{1,0:T(8,128)(2,1)S(1)} collective-permute-done((bf16[72,768]{1,0:T(8,128)(2,1)S(1)}, bf16[72,768]{1,0:T(8,128)(2,1)S(1)}, u32[]{:S(2)}, u32[]{:S(2)}) %collective-permute-start.10) | collective-permute-done | bytes 110624 | tf_op jit(solution)/shard_map/cond/branch_1_fun/ppermute | solution.py:508
  290.5 3.8 %collective-permute-start.13 = (bf16[56,768]{1,0:T(8,128)(2,1)S(1)}, bf16[56,768]{1,0:T(8,128)(2,1)S(1)}, u32[]{:S(2)}, u32[]{:S(2)}) collective-permute-start(bf16[56,768]{1,0:T(8,128)(2,1)S(1)} %get-tuple-element.235), channel_id=1, source_target_pairs={{0,2},{1,3},{2,0},{3,1},{4,6},{5,7},{6,4},{7,5},{8,10},{9,11},{10,... | collective-permute-start | bytes 258056 | tf_op jit(solution)/shard_map/cond/branch_1_fun/ppermute | solution.py:508
  295.5 4.8 %collective-permute-done.13 = bf16[56,768]{1,0:T(8,128)(2,1)S(1)} collective-permute-done((bf16[56,768]{1,0:T(8,128)(2,1)S(1)}, bf16[56,768]{1,0:T(8,128)(2,1)S(1)}, u32[]{:S(2)}, u32[]{:S(2)}) %collective-permute-start.13) | collective-permute-done | bytes 86048 | tf_op jit(solution)/shard_map/cond/branch_1_fun/ppermute | solution.py:508
  306.8 3.9 %collective-permute-done.18 = bf16[56,768]{1,0:T(8,128)(2,1)S(1)} collective-permute-done((bf16[56,768]{1,0:T(8,128)(2,1)S(1)}, bf16[56,768]{1,0:T(8,128)(2,1)S(1)}, u32[]{:S(2)}, u32[]{:S(2)}) %collective-permute-start.18) | collective-permute-done | bytes 86048 | tf_op jit(solution)/shard_map/cond/branch_1_fun/ppermute | solution.py:508
  310.7 3.9 %collective-permute-done.17 = bf16[56,768]{1,0:T(8,128)(2,1)S(1)} collective-permute-done((bf16[56,768]{1,0:T(8,128)(2,1)S(1)}, bf16[56,768]{1,0:T(8,128)(2,1)S(1)}, u32[]{:S(2)}, u32[]{:S(2)}) %collective-permute-start.17) | collective-permute-done | bytes 86048 | tf_op jit(solution)/shard_map/cond/branch_1_fun/ppermute | solution.py:508
  323.7 6.9 %collective-permute-done.20 = bf16[224,768]{1,0:T(8,128)(2,1)S(1)} collective-permute-done((bf16[224,768]{1,0:T(8,128)(2,1)S(1)}, bf16[224,768]{1,0:T(8,128)(2,1)S(1)}, u32[]{:S(2)}, u32[]{:S(2)}) %collective-permute-start.20) | collective-permute-done | bytes 344096 | tf_op jit(solution)/shard_map/cond/branch_1_fun/ppermute | solution.py:499
  330.9 4.7 %settle_pairs.2 = (f32[768,768]{1,0:T(8,128)}, f32[768,768]{1,0:T(8,128)}, f32[768,768]{1,0:T(8,128)}, f32[768,768]{1,0:T(8,128)}, f32[768,768]{1,0:T(8,128)}) custom-call(s32[32]{0:T(128)S(1)} %fusion.17.place_ref, bf16[2304,768]{1,0:T(8,128)(2,1)S(1)} %pad_maximum_fusion.in_ref), custom_call_target="tpu_custom_call" | custom-call | tf_op jit(solution)/shard_map/cond/branch_1_fun/settle_pairs/pallas_call | solution.py:603
  338.4 8.2 %collective-permute-done.22 = bf16[448,768]{1,0:T(8,128)(2,1)S(1)} collective-permute-done((bf16[448,768]{1,0:T(8,128)(2,1)S(1)}, bf16[448,768]{1,0:T(8,128)(2,1)S(1)}, u32[]{:S(2)}, u32[]{:S(2)}) %collective-permute-start.22) | collective-permute-done | bytes 688160 | tf_op jit(solution)/shard_map/cond/branch_1_fun/ppermute | solution.py:499
  352.8 4.0 %settle_pairs.3 = (f32[768,768]{1,0:T(8,128)}, f32[768,768]{1,0:T(8,128)}, f32[768,768]{1,0:T(8,128)}, f32[768,768]{1,0:T(8,128)}, f32[24,768]{1,0:T(8,128)S(1)}) custom-call(s32[32]{0:T(128)S(1)} %fusion.17.place_ref, bf16[1792,768]{1,0:T(8,128)(2,1)S(1)} %pad_maximum_fusion.1.in_ref, ...), custom_call_target="tpu_custom_call", output_to_operand_aliasing={{0}: (2, {}), {1}: (3, {}), {2}: (4, {}), {3}: (5, {})} | custom-call | tf_op jit(solution)/shard_map/cond/branch_1_fun/settle_pairs/pallas_call | solution.py:603
  357.3 11.4 %widen.1 = (f32[3072,768]{1,0:T(8,128)}, f32[768,3072]{1,0:T(8,128)}) custom-call(bf16[768,3072]{1,0:T(8,128)(2,1)} %get-tuple-element.226.outer_ref, bf16[768,3072]{1,0:T(8,128)(2,1)} %get-tuple-element.227.inner_ref), custom_call_target="tpu_custom_call" | custom-call | tf_op jit(solution)/shard_map/widen/pallas_call | solution.py:652
  (196 shorter events, 82.4 us)
Async XLA Ops:
  7.2 22.5 %all-to-all-start = ((bf16[4,96,768]{2,1,0:T(8,128)(2,1)}), bf16[4,96,768]{2,1,0:T(8,128)(2,1)}, u32[]{:S(2)}, u32[]{:S(2)}) async-start(bf16[4,96,768]{2,1,0:T(8,128)(2,1)} %param.29), calls=%async_computation | async-start | bytes 1179648 | tf_op jit(solution)/shard_map/all_to_all | solution.py:682
  13.7 343.6 %all-reduce.4.cloned.1.call-start = ((), (), s32[]{:S(2)}) async-start(), calls=%async_computation.1 | async-start | bytes 18874368 | tf_op jit(solution)/shard_map/psum | solution.py:715
  197.4 37.9 %collective-permute-start.1 = (bf16[576,768]{1,0:T(8,128)(2,1)S(1)}, bf16[576,768]{1,0:T(8,128)(2,1)S(1)}, u32[]{:S(2)}, u32[]{:S(2)}) collective-permute-start(bf16[576,768]{1,0:T(8,128)(2,1)S(1)} %constant_dynamic-slice_fusion.10), channel_id=1, source_target_pairs={{0,8},{4,20},{8,0},{12,28},{16,24},{20,4},{24,16},{28,12},{1,9},{5... | collective-permute-start | bytes 2654216 | tf_op jit(solution)/shard_map/cond/branch_1_fun/ppermute | solution.py:499
  238.4 8.6 %collective-permute-start.2 = (bf16[896,768]{1,0:T(8,128)(2,1)S(1)}, bf16[896,768]{1,0:T(8,128)(2,1)}, u32[]{:S(2)}, u32[]{:S(2)}) collective-permute-start(bf16[896,768]{1,0:T(8,128)(2,1)S(1)} %constant_dynamic-slice_fusion.9), channel_id=1, source_target_pairs={{0,4},{4,0},{8,12},{12,8},{16,20},{20,16},{24,28},{28,24},{1,5},{5... | collective-permute-start | bytes 4128776 | tf_op jit(solution)/shard_map/cond/branch_1_fun/ppermute | solution.py:499
  238.5 8.4 %collective-permute-start.3 = (bf16[288,768]{1,0:T(8,128)(2,1)S(1)}, bf16[288,768]{1,0:T(8,128)(2,1)S(1)}, u32[]{:S(2)}, u32[]{:S(2)}) collective-permute-start(bf16[288,768]{1,0:T(8,128)(2,1)S(1)} %constant_dynamic-slice_fusion.8), channel_id=1, source_target_pairs={{0,16},{4,12},{8,24},{12,4},{16,0},{20,28},{24,8},{28,20},{1,17},{... | collective-permute-start | bytes 1327112 | tf_op jit(solution)/shard_map/cond/branch_1_fun/ppermute | solution.py:499
  249.3 17.5 %collective-permute-start.4 = (bf16[448,768]{1,0:T(8,128)(2,1)S(1)}, bf16[448,768]{1,0:T(8,128)(2,1)}, u32[]{:S(2)}, u32[]{:S(2)}) collective-permute-start(bf16[448,768]{1,0:T(8,128)(2,1)S(1)} %constant_dynamic-slice_fusion.7), channel_id=1, source_target_pairs={{0,8},{4,20},{8,0},{12,28},{16,24},{20,4},{24,16},{28,12},{1,9},{5... | collective-permute-start | bytes 2064392 | tf_op jit(solution)/shard_map/cond/branch_1_fun/ppermute | solution.py:499
  250.6 8.9 %collective-permute-start.5 = (bf16[72,768]{1,0:T(8,128)(2,1)S(1)}, bf16[72,768]{1,0:T(8,128)(2,1)S(1)}, u32[]{:S(2)}, u32[]{:S(2)}) collective-permute-start(bf16[72,768]{1,0:T(8,128)(2,1)S(1)} %get-tuple-element.230), channel_id=1, source_target_pairs={{0,1},{1,2},{2,3},{3,0},{4,5},{5,6},{6,7},{7,4},{8,9},{9,10},{10,1... | collective-permute-start | bytes 331784 | tf_op jit(solution)/shard_map/cond/branch_1_fun/ppermute | solution.py:508
  250.6 10.7 %collective-permute-start.7 = (bf16[72,768]{1,0:T(8,128)(2,1)S(1)}, bf16[72,768]{1,0:T(8,128)(2,1)S(1)}, u32[]{:S(2)}, u32[]{:S(2)}) collective-permute-start(bf16[72,768]{1,0:T(8,128)(2,1)S(1)} %get-tuple-element.231), channel_id=1, source_target_pairs={{0,3},{1,0},{2,1},{3,2},{4,7},{5,4},{6,5},{7,6},{8,11},{9,8},{10,9... | collective-permute-start | bytes 331784 | tf_op jit(solution)/shard_map/cond/branch_1_fun/ppermute | solution.py:508
  254.4 12.2 %collective-permute-start.6 = (bf16[72,768]{1,0:T(8,128)(2,1)S(1)}, bf16[72,768]{1,0:T(8,128)(2,1)S(1)}, u32[]{:S(2)}, u32[]{:S(2)}) collective-permute-start(bf16[72,768]{1,0:T(8,128)(2,1)S(1)} %get-tuple-element.232), channel_id=1, source_target_pairs={{0,2},{1,3},{2,0},{3,1},{4,6},{5,7},{6,4},{7,5},{8,10},{9,11},{10,... | collective-permute-start | bytes 331784 | tf_op jit(solution)/shard_map/cond/branch_1_fun/ppermute | solution.py:508
  268.1 16.7 %collective-permute-start.8 = (bf16[224,768]{1,0:T(8,128)(2,1)S(1)}, bf16[224,768]{1,0:T(8,128)(2,1)S(1)}, u32[]{:S(2)}, u32[]{:S(2)}) collective-permute-start(bf16[224,768]{1,0:T(8,128)(2,1)S(1)} %constant_dynamic-slice_fusion.3), channel_id=1, source_target_pairs={{0,16},{4,12},{8,24},{12,4},{16,0},{20,28},{24,8},{28,20},{1,17},{... | collective-permute-start | bytes 1032200 | tf_op jit(solution)/shard_map/cond/branch_1_fun/ppermute | solution.py:499
  269.1 8.2 %collective-permute-start.11 = (bf16[72,768]{1,0:T(8,128)(2,1)S(1)}, bf16[72,768]{1,0:T(8,128)(2,1)S(1)}, u32[]{:S(2)}, u32[]{:S(2)}) collective-permute-start(bf16[72,768]{1,0:T(8,128)(2,1)S(1)} %add_convert_fusion.6), channel_id=1, source_target_pairs={{0,3},{1,0},{2,1},{3,2},{4,7},{5,4},{6,5},{7,6},{8,11},{9,8},{10,9... | collective-permute-start | bytes 331784 | tf_op jit(solution)/shard_map/cond/branch_1_fun/ppermute | solution.py:508
  270.2 14.6 %collective-permute-start.10 = (bf16[72,768]{1,0:T(8,128)(2,1)S(1)}, bf16[72,768]{1,0:T(8,128)(2,1)S(1)}, u32[]{:S(2)}, u32[]{:S(2)}) collective-permute-start(bf16[72,768]{1,0:T(8,128)(2,1)S(1)} %add_convert_fusion.6), channel_id=1, source_target_pairs={{0,2},{1,3},{2,0},{3,1},{4,6},{5,7},{6,4},{7,5},{8,10},{9,11},{10,... | collective-permute-start | bytes 331784 | tf_op jit(solution)/shard_map/cond/branch_1_fun/ppermute | solution.py:508
  270.2 14.6 %collective-permute-start.9 = (bf16[72,768]{1,0:T(8,128)(2,1)S(1)}, bf16[72,768]{1,0:T(8,128)(2,1)S(1)}, u32[]{:S(2)}, u32[]{:S(2)}) collective-permute-start(bf16[72,768]{1,0:T(8,128)(2,1)S(1)} %add_convert_fusion.6), channel_id=1, source_target_pairs={{0,1},{1,2},{2,3},{3,0},{4,5},{5,6},{6,7},{7,4},{8,9},{9,10},{10,1... | collective-permute-start | bytes 331784 | tf_op jit(solution)/shard_map/cond/branch_1_fun/ppermute | solution.py:508
  284.9 15.5 %collective-permute-start.15 = (bf16[288,768]{1,0:T(8,128)(2,1)S(1)}, bf16[288,768]{1,0:T(8,128)(2,1)S(1)}, u32[]{:S(2)}, u32[]{:S(2)}) collective-permute-start(bf16[288,768]{1,0:T(8,128)(2,1)S(1)} %pad_maximum_fusion.6), channel_id=1, source_target_pairs={{0,16},{4,12},{8,24},{12,4},{16,0},{20,28},{24,8},{28,20},{1,17},{... | collective-permute-start | bytes 1327112 | tf_op jit(solution)/shard_map/cond/branch_1_fun/ppermute | solution.py:499
  286.4 7.9 %collective-permute-start.12 = (bf16[56,768]{1,0:T(8,128)(2,1)S(1)}, bf16[56,768]{1,0:T(8,128)(2,1)S(1)}, u32[]{:S(2)}, u32[]{:S(2)}) collective-permute-start(bf16[56,768]{1,0:T(8,128)(2,1)S(1)} %get-tuple-element.233), channel_id=1, source_target_pairs={{0,1},{1,2},{2,3},{3,0},{4,5},{5,6},{6,7},{7,4},{8,9},{9,10},{10,1... | collective-permute-start | bytes 258056 | tf_op jit(solution)/shard_map/cond/branch_1_fun/ppermute | solution.py:508
  290.5 9.8 %collective-permute-start.13 = (bf16[56,768]{1,0:T(8,128)(2,1)S(1)}, bf16[56,768]{1,0:T(8,128)(2,1)S(1)}, u32[]{:S(2)}, u32[]{:S(2)}) collective-permute-start(bf16[56,768]{1,0:T(8,128)(2,1)S(1)} %get-tuple-element.235), channel_id=1, source_target_pairs={{0,2},{1,3},{2,0},{3,1},{4,6},{5,7},{6,4},{7,5},{8,10},{9,11},{10,... | collective-permute-start | bytes 258056 | tf_op jit(solution)/shard_map/cond/branch_1_fun/ppermute | solution.py:508
  300.5 20.0 %collective-permute-start.19 = (bf16[576,768]{1,0:T(8,128)(2,1)S(1)}, bf16[576,768]{1,0:T(8,128)(2,1)S(1)}, u32[]{:S(2)}, u32[]{:S(2)}) collective-permute-start(bf16[576,768]{1,0:T(8,128)(2,1)S(1)} %pad_maximum_fusion.4), channel_id=1, source_target_pairs={{0,8},{4,20},{8,0},{12,28},{16,24},{20,4},{24,16},{28,12},{1,9},{5... | collective-permute-start | bytes 2654216 | tf_op jit(solution)/shard_map/cond/branch_1_fun/ppermute | solution.py:499
  302.5 8.2 %collective-permute-start.18 = (bf16[56,768]{1,0:T(8,128)(2,1)S(1)}, bf16[56,768]{1,0:T(8,128)(2,1)S(1)}, u32[]{:S(2)}, u32[]{:S(2)}) collective-permute-start(bf16[56,768]{1,0:T(8,128)(2,1)S(1)} %add_convert_fusion.7), channel_id=1, source_target_pairs={{0,3},{1,0},{2,1},{3,2},{4,7},{5,4},{6,5},{7,6},{8,11},{9,8},{10,9... | collective-permute-start | bytes 258056 | tf_op jit(solution)/shard_map/cond/branch_1_fun/ppermute | solution.py:508
  306.2 8.4 %collective-permute-start.17 = (bf16[56,768]{1,0:T(8,128)(2,1)S(1)}, bf16[56,768]{1,0:T(8,128)(2,1)S(1)}, u32[]{:S(2)}, u32[]{:S(2)}) collective-permute-start(bf16[56,768]{1,0:T(8,128)(2,1)S(1)} %add_convert_fusion.7), channel_id=1, source_target_pairs={{0,2},{1,3},{2,0},{3,1},{4,6},{5,7},{6,4},{7,5},{8,10},{9,11},{10,... | collective-permute-start | bytes 258056 | tf_op jit(solution)/shard_map/cond/branch_1_fun/ppermute | solution.py:508
  306.2 10.5 %collective-permute-start.16 = (bf16[56,768]{1,0:T(8,128)(2,1)S(1)}, bf16[56,768]{1,0:T(8,128)(2,1)S(1)}, u32[]{:S(2)}, u32[]{:S(2)}) collective-permute-start(bf16[56,768]{1,0:T(8,128)(2,1)S(1)} %add_convert_fusion.7), channel_id=1, source_target_pairs={{0,1},{1,2},{2,3},{3,0},{4,5},{5,6},{6,7},{7,4},{8,9},{9,10},{10,1... | collective-permute-start | bytes 258056 | tf_op jit(solution)/shard_map/cond/branch_1_fun/ppermute | solution.py:508
  320.5 10.1 %collective-permute-start.21 = (bf16[1152,768]{1,0:T(8,128)(2,1)S(1)}, bf16[1152,768]{1,0:T(8,128)(2,1)S(1)}, u32[]{:S(2)}, u32[]{:S(2)}) collective-permute-start(bf16[1152,768]{1,0:T(8,128)(2,1)S(1)} %pad_maximum_fusion.2), channel_id=1, source_target_pairs={{0,4},{4,0},{8,12},{12,8},{16,20},{20,16},{24,28},{28,24},{1,5},{5... | collective-permute-start | bytes 5308424 | tf_op jit(solution)/shard_map/cond/branch_1_fun/ppermute | solution.py:499
  322.0 8.7 %collective-permute-start.20 = (bf16[224,768]{1,0:T(8,128)(2,1)S(1)}, bf16[224,768]{1,0:T(8,128)(2,1)S(1)}, u32[]{:S(2)}, u32[]{:S(2)}) collective-permute-start(bf16[224,768]{1,0:T(8,128)(2,1)S(1)} %pad_maximum_fusion.7), channel_id=1, source_target_pairs={{0,16},{4,12},{8,24},{12,4},{16,0},{20,28},{24,8},{28,20},{1,17},{... | collective-permute-start | bytes 1032200 | tf_op jit(solution)/shard_map/cond/branch_1_fun/ppermute | solution.py:499
  335.6 11.0 %collective-permute-start.22 = (bf16[448,768]{1,0:T(8,128)(2,1)S(1)}, bf16[448,768]{1,0:T(8,128)(2,1)S(1)}, u32[]{:S(2)}, u32[]{:S(2)}) collective-permute-start(bf16[448,768]{1,0:T(8,128)(2,1)S(1)} %pad_maximum_fusion.5), channel_id=1, source_target_pairs={{0,8},{4,20},{8,0},{12,28},{16,24},{20,4},{24,16},{28,12},{1,9},{5... | collective-permute-start | bytes 2064392 | tf_op jit(solution)/shard_map/cond/branch_1_fun/ppermute | solution.py:499
  346.7 6.0 %collective-permute-start.23 = (bf16[896,768]{1,0:T(8,128)(2,1)S(1)}, bf16[896,768]{1,0:T(8,128)(2,1)S(1)}, u32[]{:S(2)}, u32[]{:S(2)}) collective-permute-start(bf16[896,768]{1,0:T(8,128)(2,1)S(1)} %pad_maximum_fusion.3), channel_id=1, source_target_pairs={{0,4},{4,0},{8,12},{12,8},{16,20},{20,16},{24,28},{28,24},{1,5},{5... | collective-permute-start | bytes 4128776 | tf_op jit(solution)/shard_map/cond/branch_1_fun/ppermute | solution.py:499
  (46 other events, 308.3 us)
Sparse Core Ops, SparseCore 0:
  144.2 206.3 all-reduce.3

commit v6 on v5

--- a/solution.py
+++ b/solution.py
@@ -639,7 +639,7 @@
 VECTORS = 24
 
 
-WIDE = 512
+WIDE = 1024
 
 
 def widen_kernel(outer_ref, inner_ref, outer_out, inner_out):

time: 382 us -> 381 us (level)
  no operation moved by 1% of the time
where the time goes in v6:
time: 381 us; the launch traced here: 375 us
  Pallas kernels  183 us (48%)
  waiting for transfers between devices  75.6 us (20%)
  matrix products  39.1 us (10%)
  starting transfers between devices  35.4 us (9%)
  other arithmetic  16.9 us (4%)
  between operations  15.7 us (4%)
  local copies, waits for them, and re-layouts  9.27 us (2%)
    pallas_call x2, Pallas kernels, attention_backward(): pl.pallas_call(backward_kernel, grid=(count,), in_specs=[pl.BlockSpec((No...  73.2 us
    pallas_call x1, Pallas kernels, attention_forward(): pl.pallas_call(forward_kernel, grid=(PAIRS,), in_specs=[pl.BlockSpec(memo...  48.8 us
    pallas_call x1, Pallas kernels, token_layer(): pl.pallas_call(token_kernel, grid=(count // TOKENS,), in_specs=[tile(D),...  41.9 us
    ppermute x12, waiting for transfers between devices, along(): lax.ppermute(tensor, 'mem', [(i, (i + shift) % ring) for i in range(ring)])  41.2 us
    dot_general x10, matrix products, mm(): lax.dot_general(left, right, dims, preferred_element_type=jnp.float32)  39.1 us
    ppermute x12, waiting for transfers between devices, across(): lax.ppermute(tensor, 'batch', [(i, i ^ bits[i & 1]) for i in range(count)])  32.9 us
    ppermute x12, starting transfers between devices, along(): lax.ppermute(tensor, 'mem', [(i, (i + shift) % ring) for i in range(ring)])  18.1 us
    ppermute x12, starting transfers between devices, across(): lax.ppermute(tensor, 'batch', [(i, i ^ bits[i & 1]) for i in range(count)])  10.8 us
  transfers between devices with their start and end apart: 26, of which 16 were waited for; matrix products, arithmetic and copies ran while one was open for 10% of the time, Pallas kernels for 22%

profile of v6, /device:TPU:0, one launch (start us, length us, event | category | flops | bytes accessed | tf_op | source)
XLA Modules:
  0.0 375.3 jit_solution(11154185551339546048)
XLA Ops:
  7.2 6.5 %all-to-all-start = ((bf16[4,96,768]{2,1,0:T(8,128)(2,1)}), bf16[4,96,768]{2,1,0:T(8,128)(2,1)}, u32[]{:S(2)}, u32[]{:S(2)}) async-start(bf16[4,96,768]{2,1,0:T(8,128)(2,1)} %param.29), calls=%async_computation | async-start | bytes 1179648 | tf_op jit(solution)/shard_map/all_to_all | solution.py:682
  29.7 3.9 %convolution_convert_fusion.5.k_ref = bf16[896,768]{1,0:T(8,128)(2,1)} fusion(bf16[768,768]{1,0:T(8,128)(2,1)} %param.34, bf16[512,768]{1,0:T(8,128)(2,1)S(1)} %bitcast.39, bf16[384,768]{1,0:T(8,128)(2,1)} %bitcast.10), kind=kOutput, calls=%fused_computation.113 | convolution fusion | flops 1060405248 | bytes 3932160 | tf_op jit(solution)/shard_map/dot_general | solution.py:33
  37.0 48.8 %attention_forward.1 = (bf16[1024,768]{1,0:T(8,128)(2,1)}, f32[1024,768]{1,0:T(8,128)}, bf16[6,2,1024,896]{3,2,1,0:T(8,128)(2,1)}) custom-call(s32[1]{0:T(128)S(6)} %copy.104.length_ref, bf16[1024,768]{1,0:T(8,128)(2,1)} %get-tuple-element.238.qc_ref, bf16[1024,768]{1,0:T(8,128)(2,1)} %get-tuple-element.237.qp_ref, ...), custom_call_target="tpu_custom_call" | custom-call | flops 30000001024 | bytes 30000000 | tf_op jit(solution)/shard_map/attention_forward/pallas_call | solution.py:151
  85.8 41.9 %token_layer.1 = (bf16[1024,768]{1,0:T(8,128)(2,1)}, bf16[1024,3072]{1,0:T(8,128)(2,1)}, bf16[1024,768]{1,0:T(8,128)(2,1)}, bf16[1024,3072]{1,0:T(8,128)(2,1)}, ...) custom-call(bf16[1024,768]{1,0:T(8,128)(2,1)} %pad_maximum_fusion.10, ...), custom_call_target="tpu_custom_call" | custom-call | flops 22000001024 | bytes 40000000 | tf_op jit(solution)/shard_map/token_layer/pallas_call | solution.py:456
  127.7 9.8 %convolution_convert_fusion.2 = bf16[768,3072]{1,0:T(8,128)(2,1)} fusion(bf16[1024,768]{1,0:T(8,128)(2,1)} %get-tuple-element.182, bf16[1024,3072]{1,0:T(8,128)(2,1)} %get-tuple-element.183), kind=kOutput, calls=%fused_computation.104 | convolution fusion | flops 4834197504 | bytes 12582912 | tf_op jit(solution)/shard_map/dot_general | solution.py:33
  137.5 6.8 %convolution_convert_fusion.1 = bf16[768,3072]{1,0:T(8,128)(2,1)} fusion(bf16[1024,768]{1,0:T(8,128)(2,1)S(1)} %copy-done.43, bf16[1024,3072]{1,0:T(8,128)(2,1)S(1)} %copy-done.42), kind=kOutput, calls=%fused_computation.103 | convolution fusion | flops 4834197504 | bytes 12582912 | tf_op jit(solution)/shard_map/dot_general | solution.py:33
  148.3 209.3 %conditional.1 = (f32[768,768]{1,0:T(8,128)}, f32[768,768]{1,0:T(8,128)}, f32[768,768]{1,0:T(8,128)}, f32[768,768]{1,0:T(8,128)}, f32[768,768]{1,0:T(8,128)}, /*...) conditional(s32[]{:T(128)} %bitcast.5, () %tuple.30, ...), branch_computations={%region_0.0_spmd, %region_1.0_spmd} | conditional | flops 51666313216 | bytes 237361696 | solution.py:770
  148.3 36.8 %attention_backward.2 = (bf16[1024,768]{1,0:T(8,128)(2,1)}, bf16[896,768]{1,0:T(8,128)(2,1)}, bf16[896,768]{1,0:T(8,128)(2,1)}, f32[8,768]{1,0:T(8,128)}, bf16[2304,768]{1,0:T(8,128)(2,1)}) custom-call(bf16[6,2,1024,896]{3,2,1,0:T(8,128)(2,1)} %get-tuple-element.48.prob_ref, bf16[1024,768]{1,0:T(8,128)(2,1)} %get-tuple-element.70.dmix_ref, ...), custom_call_target="tpu_custom_call" | custom-call | flops 24000000000 | bytes 24000000 | tf_op jit(solution)/shard_map/cond/branch_1_fun/attention_backward/pallas_call | solution.py:319
  185.1 4.4 %fusion.2 = bf16[2304,768]{1,0:T(8,128)(2,1)} fusion(bf16[2304,768]{1,0:T(8,128)(2,1)} %get-tuple-element.63, bf16[1024,768]{1,0:T(8,128)(2,1)} %get-tuple-element.50.mix_ref, bf16[1024,768]{1,0:T(8,128)(2,1)} %get-tuple-element.64), kind=kOutput, calls=%fused_computation.12 | convolution fusion | flops 1208549376 | bytes 4325376 | tf_op jit(solution)/shard_map/cond/branch_1_fun/dot_general | solution.py:33
  199.4 36.3 %attention_backward.3 = (bf16[1024,768]{1,0:T(8,128)(2,1)}, bf16[896,768]{1,0:T(8,128)(2,1)}, bf16[896,768]{1,0:T(8,128)(2,1)}, f32[8,768]{1,0:T(8,128)}, bf16[1792,768]{1,0:T(8,128)(2,1)}) custom-call(bf16[6,2,1024,896]{3,2,1,0:T(8,128)(2,1)} %get-tuple-element.48.prob_ref, ...), custom_call_target="tpu_custom_call", output_to_operand_aliasing={{0}: (15, {}), {1}: (16, {}), {2}: (17, {}), {3}: (18, {})} | custom-call | flops 24000000000 | bytes 24000000 | tf_op jit(solution)/shard_map/cond/branch_1_fun/attention_backward/pallas_call | solution.py:319
  240.5 6.8 %collective-permute-done.3 = bf16[288,768]{1,0:T(8,128)(2,1)S(1)} collective-permute-done((bf16[288,768]{1,0:T(8,128)(2,1)S(1)}, bf16[288,768]{1,0:T(8,128)(2,1)S(1)}, u32[]{:S(2)}, u32[]{:S(2)}) %collective-permute-start.3) | collective-permute-done | bytes 442400 | tf_op jit(solution)/shard_map/cond/branch_1_fun/ppermute | solution.py:499
  254.9 5.1 %collective-permute-done.5 = bf16[72,768]{1,0:T(8,128)(2,1)S(1)} collective-permute-done((bf16[72,768]{1,0:T(8,128)(2,1)S(1)}, bf16[72,768]{1,0:T(8,128)(2,1)S(1)}, u32[]{:S(2)}, u32[]{:S(2)}) %collective-permute-start.5) | collective-permute-done | bytes 110624 | tf_op jit(solution)/shard_map/cond/branch_1_fun/ppermute | solution.py:508
  261.5 5.5 %collective-permute-done.6 = bf16[72,768]{1,0:T(8,128)(2,1)S(1)} collective-permute-done((bf16[72,768]{1,0:T(8,128)(2,1)S(1)}, bf16[72,768]{1,0:T(8,128)(2,1)S(1)}, u32[]{:S(2)}, u32[]{:S(2)}) %collective-permute-start.6) | collective-permute-done | bytes 110624 | tf_op jit(solution)/shard_map/cond/branch_1_fun/ppermute | solution.py:508
  271.4 6.2 %collective-permute-done.11 = bf16[72,768]{1,0:T(8,128)(2,1)S(1)} collective-permute-done((bf16[72,768]{1,0:T(8,128)(2,1)S(1)}, bf16[72,768]{1,0:T(8,128)(2,1)S(1)}, u32[]{:S(2)}, u32[]{:S(2)}) %collective-permute-start.11) | collective-permute-done | bytes 110624 | tf_op jit(solution)/shard_map/cond/branch_1_fun/ppermute | solution.py:508
  277.6 7.8 %collective-permute-done.10 = bf16[72,768]{1,0:T(8,128)(2,1)S(1)} collective-permute-done((bf16[72,768]{1,0:T(8,128)(2,1)S(1)}, bf16[72,768]{1,0:T(8,128)(2,1)S(1)}, u32[]{:S(2)}, u32[]{:S(2)}) %collective-permute-start.10) | collective-permute-done | bytes 110624 | tf_op jit(solution)/shard_map/cond/branch_1_fun/ppermute | solution.py:508
  286.6 4.0 %collective-permute-start.12 = (bf16[56,768]{1,0:T(8,128)(2,1)S(1)}, bf16[56,768]{1,0:T(8,128)(2,1)S(1)}, u32[]{:S(2)}, u32[]{:S(2)}) collective-permute-start(bf16[56,768]{1,0:T(8,128)(2,1)S(1)} %get-tuple-element.233), channel_id=1, source_target_pairs={{0,1},{1,2},{2,3},{3,0},{4,5},{5,6},{6,7},{7,4},{8,9},{9,10},{10,1... | collective-permute-start | bytes 258056 | tf_op jit(solution)/shard_map/cond/branch_1_fun/ppermute | solution.py:508
  290.9 4.4 %collective-permute-start.13 = (bf16[56,768]{1,0:T(8,128)(2,1)S(1)}, bf16[56,768]{1,0:T(8,128)(2,1)S(1)}, u32[]{:S(2)}, u32[]{:S(2)}) collective-permute-start(bf16[56,768]{1,0:T(8,128)(2,1)S(1)} %get-tuple-element.235), channel_id=1, source_target_pairs={{0,2},{1,3},{2,0},{3,1},{4,6},{5,7},{6,4},{7,5},{8,10},{9,11},{10,... | collective-permute-start | bytes 258056 | tf_op jit(solution)/shard_map/cond/branch_1_fun/ppermute | solution.py:508
  307.4 5.7 %collective-permute-done.17 = bf16[56,768]{1,0:T(8,128)(2,1)S(1)} collective-permute-done((bf16[56,768]{1,0:T(8,128)(2,1)S(1)}, bf16[56,768]{1,0:T(8,128)(2,1)S(1)}, u32[]{:S(2)}, u32[]{:S(2)}) %collective-permute-start.17) | collective-permute-done | bytes 86048 | tf_op jit(solution)/shard_map/cond/branch_1_fun/ppermute | solution.py:508
  314.7 7.7 %collective-permute-done.19 = bf16[576,768]{1,0:T(8,128)(2,1)S(1)} collective-permute-done((bf16[576,768]{1,0:T(8,128)(2,1)S(1)}, bf16[576,768]{1,0:T(8,128)(2,1)S(1)}, u32[]{:S(2)}, u32[]{:S(2)}) %collective-permute-start.19) | collective-permute-done | bytes 884768 | tf_op jit(solution)/shard_map/cond/branch_1_fun/ppermute | solution.py:499
  324.2 6.8 %collective-permute-done.20 = bf16[224,768]{1,0:T(8,128)(2,1)S(1)} collective-permute-done((bf16[224,768]{1,0:T(8,128)(2,1)S(1)}, bf16[224,768]{1,0:T(8,128)(2,1)S(1)}, u32[]{:S(2)}, u32[]{:S(2)}) %collective-permute-start.20) | collective-permute-done | bytes 344096 | tf_op jit(solution)/shard_map/cond/branch_1_fun/ppermute | solution.py:499
  331.3 4.7 %settle_pairs.2 = (f32[768,768]{1,0:T(8,128)}, f32[768,768]{1,0:T(8,128)}, f32[768,768]{1,0:T(8,128)}, f32[768,768]{1,0:T(8,128)}, f32[768,768]{1,0:T(8,128)}) custom-call(s32[32]{0:T(128)S(1)} %fusion.17.place_ref, bf16[2304,768]{1,0:T(8,128)(2,1)S(1)} %pad_maximum_fusion.in_ref), custom_call_target="tpu_custom_call" | custom-call | tf_op jit(solution)/shard_map/cond/branch_1_fun/settle_pairs/pallas_call | solution.py:603
  338.9 8.1 %collective-permute-done.22 = bf16[448,768]{1,0:T(8,128)(2,1)S(1)} collective-permute-done((bf16[448,768]{1,0:T(8,128)(2,1)S(1)}, bf16[448,768]{1,0:T(8,128)(2,1)S(1)}, u32[]{:S(2)}, u32[]{:S(2)}) %collective-permute-start.22) | collective-permute-done | bytes 688160 | tf_op jit(solution)/shard_map/cond/branch_1_fun/ppermute | solution.py:499
  353.2 4.0 %settle_pairs.3 = (f32[768,768]{1,0:T(8,128)}, f32[768,768]{1,0:T(8,128)}, f32[768,768]{1,0:T(8,128)}, f32[768,768]{1,0:T(8,128)}, f32[24,768]{1,0:T(8,128)S(1)}) custom-call(s32[32]{0:T(128)S(1)} %fusion.17.place_ref, bf16[1792,768]{1,0:T(8,128)(2,1)S(1)} %pad_maximum_fusion.1.in_ref, ...), custom_call_target="tpu_custom_call", output_to_operand_aliasing={{0}: (2, {}), {1}: (3, {}), {2}: (4, {}), {3}: (5, {})} | custom-call | tf_op jit(solution)/shard_map/cond/branch_1_fun/settle_pairs/pallas_call | solution.py:603
  357.7 10.1 %widen.1 = (f32[3072,768]{1,0:T(8,128)}, f32[768,3072]{1,0:T(8,128)}) custom-call(bf16[768,3072]{1,0:T(8,128)(2,1)} %get-tuple-element.226.outer_ref, bf16[768,3072]{1,0:T(8,128)(2,1)} %get-tuple-element.227.inner_ref), custom_call_target="tpu_custom_call" | custom-call | tf_op jit(solution)/shard_map/widen/pallas_call | solution.py:652
  (196 shorter events, 76.8 us)
Async XLA Ops:
  7.2 22.5 %all-to-all-start = ((bf16[4,96,768]{2,1,0:T(8,128)(2,1)}), bf16[4,96,768]{2,1,0:T(8,128)(2,1)}, u32[]{:S(2)}, u32[]{:S(2)}) async-start(bf16[4,96,768]{2,1,0:T(8,128)(2,1)} %param.29), calls=%async_computation | async-start | bytes 1179648 | tf_op jit(solution)/shard_map/all_to_all | solution.py:682
  13.7 344.0 %all-reduce.4.cloned.1.call-start = ((), (), s32[]{:S(2)}) async-start(), calls=%async_computation.1 | async-start | bytes 18874368 | tf_op jit(solution)/shard_map/psum | solution.py:715
  197.6 38.1 %collective-permute-start.1 = (bf16[576,768]{1,0:T(8,128)(2,1)S(1)}, bf16[576,768]{1,0:T(8,128)(2,1)S(1)}, u32[]{:S(2)}, u32[]{:S(2)}) collective-permute-start(bf16[576,768]{1,0:T(8,128)(2,1)S(1)} %constant_dynamic-slice_fusion.10), channel_id=1, source_target_pairs={{0,8},{4,20},{8,0},{12,28},{16,24},{20,4},{24,16},{28,12},{1,9},{5... | collective-permute-start | bytes 2654216 | tf_op jit(solution)/shard_map/cond/branch_1_fun/ppermute | solution.py:499
  238.7 8.6 %collective-permute-start.2 = (bf16[896,768]{1,0:T(8,128)(2,1)S(1)}, bf16[896,768]{1,0:T(8,128)(2,1)}, u32[]{:S(2)}, u32[]{:S(2)}) collective-permute-start(bf16[896,768]{1,0:T(8,128)(2,1)S(1)} %constant_dynamic-slice_fusion.9), channel_id=1, source_target_pairs={{0,4},{4,0},{8,12},{12,8},{16,20},{20,16},{24,28},{28,24},{1,5},{5... | collective-permute-start | bytes 4128776 | tf_op jit(solution)/shard_map/cond/branch_1_fun/ppermute | solution.py:499
  238.9 8.4 %collective-permute-start.3 = (bf16[288,768]{1,0:T(8,128)(2,1)S(1)}, bf16[288,768]{1,0:T(8,128)(2,1)S(1)}, u32[]{:S(2)}, u32[]{:S(2)}) collective-permute-start(bf16[288,768]{1,0:T(8,128)(2,1)S(1)} %constant_dynamic-slice_fusion.8), channel_id=1, source_target_pairs={{0,16},{4,12},{8,24},{12,4},{16,0},{20,28},{24,8},{28,20},{1,17},{... | collective-permute-start | bytes 1327112 | tf_op jit(solution)/shard_map/cond/branch_1_fun/ppermute | solution.py:499
  249.6 17.4 %collective-permute-start.4 = (bf16[448,768]{1,0:T(8,128)(2,1)S(1)}, bf16[448,768]{1,0:T(8,128)(2,1)}, u32[]{:S(2)}, u32[]{:S(2)}) collective-permute-start(bf16[448,768]{1,0:T(8,128)(2,1)S(1)} %constant_dynamic-slice_fusion.7), channel_id=1, source_target_pairs={{0,8},{4,20},{8,0},{12,28},{16,24},{20,4},{24,16},{28,12},{1,9},{5... | collective-permute-start | bytes 2064392 | tf_op jit(solution)/shard_map/cond/branch_1_fun/ppermute | solution.py:499
  251.0 9.0 %collective-permute-start.5 = (bf16[72,768]{1,0:T(8,128)(2,1)S(1)}, bf16[72,768]{1,0:T(8,128)(2,1)S(1)}, u32[]{:S(2)}, u32[]{:S(2)}) collective-permute-start(bf16[72,768]{1,0:T(8,128)(2,1)S(1)} %get-tuple-element.230), channel_id=1, source_target_pairs={{0,1},{1,2},{2,3},{3,0},{4,5},{5,6},{6,7},{7,4},{8,9},{9,10},{10,1... | collective-permute-start | bytes 331784 | tf_op jit(solution)/shard_map/cond/branch_1_fun/ppermute | solution.py:508
  251.0 10.5 %collective-permute-start.7 = (bf16[72,768]{1,0:T(8,128)(2,1)S(1)}, bf16[72,768]{1,0:T(8,128)(2,1)S(1)}, u32[]{:S(2)}, u32[]{:S(2)}) collective-permute-start(bf16[72,768]{1,0:T(8,128)(2,1)S(1)} %get-tuple-element.231), channel_id=1, source_target_pairs={{0,3},{1,0},{2,1},{3,2},{4,7},{5,4},{6,5},{7,6},{8,11},{9,8},{10,9... | collective-permute-start | bytes 331784 | tf_op jit(solution)/shard_map/cond/branch_1_fun/ppermute | solution.py:508
  254.8 12.1 %collective-permute-start.6 = (bf16[72,768]{1,0:T(8,128)(2,1)S(1)}, bf16[72,768]{1,0:T(8,128)(2,1)S(1)}, u32[]{:S(2)}, u32[]{:S(2)}) collective-permute-start(bf16[72,768]{1,0:T(8,128)(2,1)S(1)} %get-tuple-element.232), channel_id=1, source_target_pairs={{0,2},{1,3},{2,0},{3,1},{4,6},{5,7},{6,4},{7,5},{8,10},{9,11},{10,... | collective-permute-start | bytes 331784 | tf_op jit(solution)/shard_map/cond/branch_1_fun/ppermute | solution.py:508
  268.4 17.1 %collective-permute-start.8 = (bf16[224,768]{1,0:T(8,128)(2,1)S(1)}, bf16[224,768]{1,0:T(8,128)(2,1)S(1)}, u32[]{:S(2)}, u32[]{:S(2)}) collective-permute-start(bf16[224,768]{1,0:T(8,128)(2,1)S(1)} %constant_dynamic-slice_fusion.3), channel_id=1, source_target_pairs={{0,16},{4,12},{8,24},{12,4},{16,0},{20,28},{24,8},{28,20},{1,17},{... | collective-permute-start | bytes 1032200 | tf_op jit(solution)/shard_map/cond/branch_1_fun/ppermute | solution.py:499
  269.4 8.2 %collective-permute-start.11 = (bf16[72,768]{1,0:T(8,128)(2,1)S(1)}, bf16[72,768]{1,0:T(8,128)(2,1)S(1)}, u32[]{:S(2)}, u32[]{:S(2)}) collective-permute-start(bf16[72,768]{1,0:T(8,128)(2,1)S(1)} %add_convert_fusion.6), channel_id=1, source_target_pairs={{0,3},{1,0},{2,1},{3,2},{4,7},{5,4},{6,5},{7,6},{8,11},{9,8},{10,9... | collective-permute-start | bytes 331784 | tf_op jit(solution)/shard_map/cond/branch_1_fun/ppermute | solution.py:508
  270.5 14.9 %collective-permute-start.10 = (bf16[72,768]{1,0:T(8,128)(2,1)S(1)}, bf16[72,768]{1,0:T(8,128)(2,1)S(1)}, u32[]{:S(2)}, u32[]{:S(2)}) collective-permute-start(bf16[72,768]{1,0:T(8,128)(2,1)S(1)} %add_convert_fusion.6), channel_id=1, source_target_pairs={{0,2},{1,3},{2,0},{3,1},{4,6},{5,7},{6,4},{7,5},{8,10},{9,11},{10,... | collective-permute-start | bytes 331784 | tf_op jit(solution)/shard_map/cond/branch_1_fun/ppermute | solution.py:508
  270.5 14.9 %collective-permute-start.9 = (bf16[72,768]{1,0:T(8,128)(2,1)S(1)}, bf16[72,768]{1,0:T(8,128)(2,1)S(1)}, u32[]{:S(2)}, u32[]{:S(2)}) collective-permute-start(bf16[72,768]{1,0:T(8,128)(2,1)S(1)} %add_convert_fusion.6), channel_id=1, source_target_pairs={{0,1},{1,2},{2,3},{3,0},{4,5},{5,6},{6,7},{7,4},{8,9},{9,10},{10,1... | collective-permute-start | bytes 331784 | tf_op jit(solution)/shard_map/cond/branch_1_fun/ppermute | solution.py:508
  285.6 14.2 %collective-permute-start.15 = (bf16[288,768]{1,0:T(8,128)(2,1)S(1)}, bf16[288,768]{1,0:T(8,128)(2,1)S(1)}, u32[]{:S(2)}, u32[]{:S(2)}) collective-permute-start(bf16[288,768]{1,0:T(8,128)(2,1)S(1)} %pad_maximum_fusion.6), channel_id=1, source_target_pairs={{0,16},{4,12},{8,24},{12,4},{16,0},{20,28},{24,8},{28,20},{1,17},{... | collective-permute-start | bytes 1327112 | tf_op jit(solution)/shard_map/cond/branch_1_fun/ppermute | solution.py:499
  286.6 8.7 %collective-permute-start.12 = (bf16[56,768]{1,0:T(8,128)(2,1)S(1)}, bf16[56,768]{1,0:T(8,128)(2,1)S(1)}, u32[]{:S(2)}, u32[]{:S(2)}) collective-permute-start(bf16[56,768]{1,0:T(8,128)(2,1)S(1)} %get-tuple-element.233), channel_id=1, source_target_pairs={{0,1},{1,2},{2,3},{3,0},{4,5},{5,6},{6,7},{7,4},{8,9},{9,10},{10,1... | collective-permute-start | bytes 258056 | tf_op jit(solution)/shard_map/cond/branch_1_fun/ppermute | solution.py:508
  290.7 6.0 %collective-permute-start.14 = (bf16[56,768]{1,0:T(8,128)(2,1)S(1)}, bf16[56,768]{1,0:T(8,128)(2,1)S(1)}, u32[]{:S(2)}, u32[]{:S(2)}) collective-permute-start(bf16[56,768]{1,0:T(8,128)(2,1)S(1)} %get-tuple-element.234), channel_id=1, source_target_pairs={{0,3},{1,0},{2,1},{3,2},{4,7},{5,4},{6,5},{7,6},{8,11},{9,8},{10,9... | collective-permute-start | bytes 258056 | tf_op jit(solution)/shard_map/cond/branch_1_fun/ppermute | solution.py:508
  290.9 8.8 %collective-permute-start.13 = (bf16[56,768]{1,0:T(8,128)(2,1)S(1)}, bf16[56,768]{1,0:T(8,128)(2,1)S(1)}, u32[]{:S(2)}, u32[]{:S(2)}) collective-permute-start(bf16[56,768]{1,0:T(8,128)(2,1)S(1)} %get-tuple-element.235), channel_id=1, source_target_pairs={{0,2},{1,3},{2,0},{3,1},{4,6},{5,7},{6,4},{7,5},{8,10},{9,11},{10,... | collective-permute-start | bytes 258056 | tf_op jit(solution)/shard_map/cond/branch_1_fun/ppermute | solution.py:508
  299.8 22.6 %collective-permute-start.19 = (bf16[576,768]{1,0:T(8,128)(2,1)S(1)}, bf16[576,768]{1,0:T(8,128)(2,1)S(1)}, u32[]{:S(2)}, u32[]{:S(2)}) collective-permute-start(bf16[576,768]{1,0:T(8,128)(2,1)S(1)} %pad_maximum_fusion.4), channel_id=1, source_target_pairs={{0,8},{4,20},{8,0},{12,28},{16,24},{20,4},{24,16},{28,12},{1,9},{5... | collective-permute-start | bytes 2654216 | tf_op jit(solution)/shard_map/cond/branch_1_fun/ppermute | solution.py:499
  300.4 6.9 %collective-permute-start.18 = (bf16[56,768]{1,0:T(8,128)(2,1)S(1)}, bf16[56,768]{1,0:T(8,128)(2,1)S(1)}, u32[]{:S(2)}, u32[]{:S(2)}) collective-permute-start(bf16[56,768]{1,0:T(8,128)(2,1)S(1)} %add_convert_fusion.7), channel_id=1, source_target_pairs={{0,3},{1,0},{2,1},{3,2},{4,7},{5,4},{6,5},{7,6},{8,11},{9,8},{10,9... | collective-permute-start | bytes 258056 | tf_op jit(solution)/shard_map/cond/branch_1_fun/ppermute | solution.py:508
  301.2 11.8 %collective-permute-start.17 = (bf16[56,768]{1,0:T(8,128)(2,1)S(1)}, bf16[56,768]{1,0:T(8,128)(2,1)S(1)}, u32[]{:S(2)}, u32[]{:S(2)}) collective-permute-start(bf16[56,768]{1,0:T(8,128)(2,1)S(1)} %add_convert_fusion.7), channel_id=1, source_target_pairs={{0,2},{1,3},{2,0},{3,1},{4,6},{5,7},{6,4},{7,5},{8,10},{9,11},{10,... | collective-permute-start | bytes 258056 | tf_op jit(solution)/shard_map/cond/branch_1_fun/ppermute | solution.py:508
  302.0 12.7 %collective-permute-start.16 = (bf16[56,768]{1,0:T(8,128)(2,1)S(1)}, bf16[56,768]{1,0:T(8,128)(2,1)S(1)}, u32[]{:S(2)}, u32[]{:S(2)}) collective-permute-start(bf16[56,768]{1,0:T(8,128)(2,1)S(1)} %add_convert_fusion.7), channel_id=1, source_target_pairs={{0,1},{1,2},{2,3},{3,0},{4,5},{5,6},{6,7},{7,4},{8,9},{9,10},{10,1... | collective-permute-start | bytes 258056 | tf_op jit(solution)/shard_map/cond/branch_1_fun/ppermute | solution.py:508
  322.6 8.5 %collective-permute-start.21 = (bf16[1152,768]{1,0:T(8,128)(2,1)S(1)}, bf16[1152,768]{1,0:T(8,128)(2,1)S(1)}, u32[]{:S(2)}, u32[]{:S(2)}) collective-permute-start(bf16[1152,768]{1,0:T(8,128)(2,1)S(1)} %pad_maximum_fusion.2), channel_id=1, source_target_pairs={{0,4},{4,0},{8,12},{12,8},{16,20},{20,16},{24,28},{28,24},{1,5},{5... | collective-permute-start | bytes 5308424 | tf_op jit(solution)/shard_map/cond/branch_1_fun/ppermute | solution.py:499
  322.7 8.3 %collective-permute-start.20 = (bf16[224,768]{1,0:T(8,128)(2,1)S(1)}, bf16[224,768]{1,0:T(8,128)(2,1)S(1)}, u32[]{:S(2)}, u32[]{:S(2)}) collective-permute-start(bf16[224,768]{1,0:T(8,128)(2,1)S(1)} %pad_maximum_fusion.7), channel_id=1, source_target_pairs={{0,16},{4,12},{8,24},{12,4},{16,0},{20,28},{24,8},{28,20},{1,17},{... | collective-permute-start | bytes 1032200 | tf_op jit(solution)/shard_map/cond/branch_1_fun/ppermute | solution.py:499
  336.0 11.0 %collective-permute-start.22 = (bf16[448,768]{1,0:T(8,128)(2,1)S(1)}, bf16[448,768]{1,0:T(8,128)(2,1)S(1)}, u32[]{:S(2)}, u32[]{:S(2)}) collective-permute-start(bf16[448,768]{1,0:T(8,128)(2,1)S(1)} %pad_maximum_fusion.5), channel_id=1, source_target_pairs={{0,8},{4,20},{8,0},{12,28},{16,24},{20,4},{24,16},{28,12},{1,9},{5... | collective-permute-start | bytes 2064392 | tf_op jit(solution)/shard_map/cond/branch_1_fun/ppermute | solution.py:499
  (46 other events, 294.8 us)
Sparse Core Ops, SparseCore 0:
  144.5 206.2 all-reduce.3
